TPU v7x, 32 devices: a whole 2x2x4 slice. The times are simulated.
32 devices in a mesh: rep: 4 (over z), fsdp: 8 (over y, x, core).
Axes of the slice: x: 2, y: 2, z: 4, core: 2. Of those that a mesh axis runs over, the one named last changes fastest.
Arguments:
- byte_feats: bfloat16 [8, 4096, 768], P('rep', 'fsdp'), may hold values from -6 to 6
- latent_init: bfloat16 [256, 1280], P('fsdp'), may hold values from -6 to 6
- prefix: int32 [8], P('rep'), may hold values from 409 to 2048, as said below
- byte_gain: float32 [768], replicated, may hold values from 0.25 to 1.75
- query_gain: float32 [1280], replicated, may hold values from 0.25 to 1.75
- mixer_gain: float32 [1280], replicated, may hold values from 0.25 to 1.75
- query_weight: bfloat16 [1280, 256], P('fsdp'), may hold values from -0.25 to 0.25
- key_weight: bfloat16 [768, 256], P('fsdp'), may hold values from -0.3125 to 0.3125
- value_weight: bfloat16 [768, 1280], P('fsdp'), may hold values from -0.21875 to 0.21875
- out_weight: bfloat16 [1280, 1280], P('fsdp'), may hold values from -0.625 to 0.625
- up_weight: bfloat16 [1280, 1280], P('fsdp'), may hold values from -0.15625 to 0.15625
- down_weight: bfloat16 [1280, 1280], P('fsdp'), may hold values from -0.15625 to 0.15625
- cotangent: bfloat16 [8, 256, 1280], P('rep', 'fsdp'), may hold values from -6 to 6
Outputs:
- latents: bfloat16 [8, 256, 1280], P('rep', 'fsdp')
- byte_grads: float32 [8, 4096, 768], P('rep', 'fsdp')
- init_grads: float32 [256, 1280], P('fsdp')
- byte_norm: float32 [768], replicated
- query_norm: float32 [1280], replicated
- mixer_norm: float32 [1280], replicated
- query_grads: float32 [1280, 256], P('fsdp')
- key_grads: float32 [768, 256], P('fsdp')
- value_grads: float32 [768, 1280], P('fsdp')
- out_grads: float32 [1280, 1280], P('fsdp')
- up_grads: float32 [1280, 1280], P('fsdp')
- down_grads: float32 [1280, 1280], P('fsdp')
Inputs may be any that keep to these rules, and one draw needn't show every extreme that they name: Bytes below a sequence's prefix length are seen by every latent; in every draw one sequence has the least prefix and another the most.
All inputs are finite; a program needn't handle non-finite values.
Results may differ from a plain program's by a relative error of at most 0.023.
Values may be sent and summed in bfloat16 or wider, within the bound.
No kernel may reach another device: no remote copies, remote signals or barrier semaphores. Data moves between devices by JAX's collectives and lax.ppermute only.
A program may use at most 128 MiB of HBM per device.

v0:
```python
import jax
import jax.numpy as jnp
from jax import lax
from jax.sharding import PartitionSpec as P

DL = 1280
H = 8
QK = 256
VD = 1280
STRIDE = 16


EPSILON = 1e-05


def norm_parts(values, gain):
    centered = values - jnp.mean(values, axis=-1, keepdims=True)
    variance = jnp.mean(centered * centered, axis=-1, keepdims=True)
    inverse = lax.rsqrt(variance + EPSILON)
    normal = centered * inverse
    return (normal * gain, normal, inverse)


def norm_back(grad_out, normal, inverse, gain):
    scaled = grad_out * gain
    mean_one = jnp.mean(scaled, axis=-1, keepdims=True)
    mean_two = jnp.mean(scaled * normal, axis=-1, keepdims=True)
    return inverse * (scaled - mean_one - normal * mean_two)


def per_device(
    byte_feats,
    latent_init,
    prefix,
    byte_gain,
    query_gain,
    mixer_gain,
    query_weight,
    key_weight,
    value_weight,
    out_weight,
    up_weight,
    down_weight,
    cotangent,
):
    shard_count = lax.axis_size("fsdp")
    shard_index = lax.axis_index("fsdp")
    seq_count, seq_rows, byte_width = byte_feats.shape
    own_latents = latent_init.shape[0]
    latent_count = own_latents * shard_count
    head_qk = QK // H
    head_value = VD // H
    scale = head_qk ** (-0.5)
    row_count = seq_count * own_latents
    latent_all, query_full, key_full, value_full = (
        lax.all_gather(latent_init, "fsdp", axis=0, tiled=True),
        lax.all_gather(query_weight, "fsdp", axis=0, tiled=True),
        lax.all_gather(key_weight, "fsdp", axis=0, tiled=True),
        lax.all_gather(value_weight, "fsdp", axis=0, tiled=True),
    )
    out_full, up_full, down_full = (
        lax.all_gather(out_weight, "fsdp", axis=0, tiled=True),
        lax.all_gather(up_weight, "fsdp", axis=0, tiled=True),
        lax.all_gather(down_weight, "fsdp", axis=0, tiled=True),
    )
    byte_flat = byte_feats.astype(jnp.float32).reshape(seq_count * seq_rows, byte_width)
    byte_normed, byte_hat, byte_inv = norm_parts(byte_flat, byte_gain)
    byte_low = byte_normed.astype(jnp.bfloat16)
    keys_low = (
        jnp.dot(byte_low, key_full, preferred_element_type=jnp.float32)
        .astype(jnp.bfloat16)
        .reshape(seq_count, seq_rows, H, head_qk)
    )
    values_low = (
        jnp.dot(byte_low, value_full, preferred_element_type=jnp.float32)
        .astype(jnp.bfloat16)
        .reshape(seq_count, seq_rows, H, head_value)
    )
    latent_normed, latent_hat, latent_inv = norm_parts(latent_all.astype(jnp.float32), query_gain)
    latent_low = latent_normed.astype(jnp.bfloat16)
    query_low = (
        jnp.dot(latent_low, query_full, preferred_element_type=jnp.float32)
        .astype(jnp.bfloat16)
        .reshape(latent_count, H, head_qk)
    )
    byte_pos = shard_index * seq_rows + jnp.arange(seq_rows, dtype=jnp.int32)
    latent_pos = jnp.arange(latent_count, dtype=jnp.int32)

    def exp_scores(keys_seq, limit):
        scores = scale * jnp.einsum(
            "jhd,ihd->hji", query_low, keys_seq, preferred_element_type=jnp.float32
        )
        visible = (byte_pos[None, :] < limit) | (
            byte_pos[None, :] < STRIDE * (latent_pos[:, None] + 1)
        )
        return jnp.where(visible[None], jnp.exp(scores), 0.0)

    def forward_step(carry, inputs):
        keys_seq, values_seq, limit = inputs
        weights = exp_scores(keys_seq, limit)
        totals = jnp.transpose(jnp.sum(weights, axis=-1))
        summed = jnp.einsum(
            "hji,ihv->jhv",
            weights.astype(jnp.bfloat16),
            values_seq,
            preferred_element_type=jnp.float32,
        ).reshape(latent_count, VD)
        own_sum, own_total = (
            lax.psum_scatter(summed, "fsdp", scatter_dimension=0, tiled=True),
            lax.psum_scatter(totals, "fsdp", scatter_dimension=0, tiled=True),
        )
        return (carry, (own_sum, own_total))

    _, (sums_own, totals_own) = lax.scan(
        forward_step, jnp.zeros((), jnp.float32), (keys_low, values_low, prefix)
    )
    attended = sums_own.reshape(seq_count, own_latents, H, head_value) / totals_own[..., None]
    attn_low = attended.reshape(row_count, VD).astype(jnp.bfloat16)
    mixed = jnp.dot(attn_low, out_full, preferred_element_type=jnp.float32).reshape(
        seq_count, own_latents, DL
    )
    hidden = (mixed + latent_init.astype(jnp.float32)[None]).reshape(row_count, DL)
    mixer_normed, mixer_hat, mixer_inv = norm_parts(hidden, mixer_gain)
    mixer_low = mixer_normed.astype(jnp.bfloat16)
    pre_act = jnp.dot(mixer_low, up_full, preferred_element_type=jnp.float32)
    activated, gelu_back = jax.vjp(lambda value: jax.nn.gelu(value, approximate=False), pre_act)
    act_low = activated.astype(jnp.bfloat16)
    output = hidden + jnp.dot(act_low, down_full, preferred_element_type=jnp.float32)
    latents = output.reshape(seq_count, own_latents, DL).astype(jnp.bfloat16)
    cot_low = cotangent.reshape(row_count, DL)
    down_local = jnp.einsum("rf,rd->fd", act_low, cot_low, preferred_element_type=jnp.float32)
    act_grad = jnp.einsum("rd,fd->rf", cot_low, down_full, preferred_element_type=jnp.float32)
    pre_grad = gelu_back(act_grad)[0].astype(jnp.bfloat16)
    up_local = jnp.einsum("rd,rf->df", mixer_low, pre_grad, preferred_element_type=jnp.float32)
    mixer_grad = jnp.einsum("rf,df->rd", pre_grad, up_full, preferred_element_type=jnp.float32)
    mixer_part = jnp.sum(mixer_grad * mixer_hat, axis=0)
    hidden_grad = cot_low.astype(jnp.float32) + norm_back(
        mixer_grad, mixer_hat, mixer_inv, mixer_gain
    )
    hidden_low = hidden_grad.astype(jnp.bfloat16)
    out_local = jnp.einsum("rv,rd->vd", attn_low, hidden_low, preferred_element_type=jnp.float32)
    attn_grad = jnp.einsum(
        "rd,vd->rv", hidden_low, out_full, preferred_element_type=jnp.float32
    ).astype(jnp.bfloat16)
    attn_heads = attn_grad.astype(jnp.float32).reshape(seq_count, own_latents, H, head_value)
    sum_grad = (
        (attn_heads / totals_own[..., None])
        .astype(jnp.bfloat16)
        .reshape(seq_count, own_latents, VD)
    )
    total_grad = (-jnp.sum(attn_heads * attended, axis=-1) / totals_own).astype(jnp.bfloat16)
    init_rows = jnp.sum(hidden_grad.reshape(seq_count, own_latents, DL), axis=0)

    def backward_step(carry, inputs):
        keys_seq, values_seq, limit, sum_own, total_own = inputs
        sum_all, total_all = (
            lax.all_gather(sum_own, "fsdp", axis=0, tiled=True),
            lax.all_gather(total_own, "fsdp", axis=0, tiled=True),
        )
        weights = exp_scores(keys_seq, limit)
        sum_heads = sum_all.reshape(latent_count, H, head_value)
        values_grad = jnp.einsum(
            "hji,jhv->ihv",
            weights.astype(jnp.bfloat16),
            sum_heads,
            preferred_element_type=jnp.float32,
        ).astype(jnp.bfloat16)
        weights_grad = (
            jnp.einsum("jhv,ihv->hji", sum_heads, values_seq, preferred_element_type=jnp.float32)
            + jnp.transpose(total_all.astype(jnp.float32))[:, :, None]
        )
        score_grad = (weights * weights_grad).astype(jnp.bfloat16)
        query_part = scale * jnp.einsum(
            "hji,ihd->jhd", score_grad, keys_seq, preferred_element_type=jnp.float32
        )
        keys_grad = (
            scale
            * jnp.einsum("hji,jhd->ihd", score_grad, query_low, preferred_element_type=jnp.float32)
        ).astype(jnp.bfloat16)
        query_own = lax.psum_scatter(
            query_part.reshape(latent_count, QK), "fsdp", scatter_dimension=0, tiled=True
        )
        return (carry, (keys_grad, values_grad, query_own))

    _, (keys_grad, values_grad, query_own) = lax.scan(
        backward_step,
        jnp.zeros((), jnp.float32),
        (keys_low, values_low, prefix, sum_grad, total_grad),
    )
    keys_flat = keys_grad.reshape(seq_count * seq_rows, QK)
    values_flat = values_grad.reshape(seq_count * seq_rows, VD)
    key_local = jnp.einsum("rb,rq->bq", byte_low, keys_flat, preferred_element_type=jnp.float32)
    value_local = jnp.einsum("rb,rv->bv", byte_low, values_flat, preferred_element_type=jnp.float32)
    normed_grad = jnp.einsum(
        "rq,bq->rb", keys_flat, key_full, preferred_element_type=jnp.float32
    ) + jnp.einsum("rv,bv->rb", values_flat, value_full, preferred_element_type=jnp.float32)
    byte_part = jnp.sum(normed_grad * byte_hat, axis=0)
    byte_grads = norm_back(normed_grad, byte_hat, byte_inv, byte_gain).reshape(
        seq_count, seq_rows, byte_width
    )
    query_grad_low = query_own.astype(jnp.bfloat16)
    own_low = lax.dynamic_slice_in_dim(latent_low, shard_index * own_latents, own_latents, 0)
    own_hat = lax.dynamic_slice_in_dim(latent_hat, shard_index * own_latents, own_latents, 0)
    own_inv = lax.dynamic_slice_in_dim(latent_inv, shard_index * own_latents, own_latents, 0)
    query_local = jnp.einsum(
        "ld,slq->dq", own_low, query_grad_low, preferred_element_type=jnp.float32
    )
    latent_grad = jnp.einsum(
        "slq,dq->ld", query_grad_low, query_full, preferred_element_type=jnp.float32
    )
    query_part_gain = jnp.sum(latent_grad * own_hat, axis=0)
    init_local = init_rows + norm_back(latent_grad, own_hat, own_inv, query_gain)
    byte_norm, query_norm, mixer_norm = lax.psum(
        (byte_part, query_part_gain, mixer_part), ("rep", "fsdp")
    )
    group_parts = (
        lax.psum_scatter(query_local, "fsdp", scatter_dimension=0, tiled=True),
        lax.psum_scatter(key_local, "fsdp", scatter_dimension=0, tiled=True),
        lax.psum_scatter(value_local, "fsdp", scatter_dimension=0, tiled=True),
        lax.psum_scatter(out_local, "fsdp", scatter_dimension=0, tiled=True),
        lax.psum_scatter(up_local, "fsdp", scatter_dimension=0, tiled=True),
        lax.psum_scatter(down_local, "fsdp", scatter_dimension=0, tiled=True),
    )
    query_grads, key_grads, value_grads, out_grads, up_grads, down_grads, init_grads = lax.psum(
        (
            group_parts[0],
            group_parts[1],
            group_parts[2],
            group_parts[3],
            group_parts[4],
            group_parts[5],
            init_local,
        ),
        "rep",
    )
    return (
        latents,
        byte_grads,
        init_grads,
        byte_norm,
        query_norm,
        mixer_norm,
        query_grads,
        key_grads,
        value_grads,
        out_grads,
        up_grads,
        down_grads,
    )


def solution(mesh):
    placed = (
        P("rep", "fsdp", None),
        P("fsdp", None),
        P("rep"),
        P(),
        P(),
        P(),
        P("fsdp", None),
        P("fsdp", None),
        P("fsdp", None),
        P("fsdp", None),
        P("fsdp", None),
        P("fsdp", None),
        P("rep", "fsdp", None),
    )
    return jax.shard_map(
        per_device,
        mesh=mesh,
        in_specs=placed,
        out_specs=(
            P("rep", "fsdp", None),
            P("rep", "fsdp", None),
            P("fsdp", None),
            P(),
            P(),
            P(),
            P("fsdp", None),
            P("fsdp", None),
            P("fsdp", None),
            P("fsdp", None),
            P("fsdp", None),
            P("fsdp", None),
        ),
        check_vma=False,
    )
```

profile of v0, /device:TPU:0, one launch (start us, length us, event | category | flops | bytes accessed | tf_op | source)
XLA Modules:
  0.0 963.5 jit_solution(4429042801356380215)
XLA Ops:
  12.3 11.1 %all_gather.28 = bf16[768,256]{1,0:T(8,128)(2,1)S(1)} all-gather(bf16[96,256]{1,0:T(8,128)(2,1)S(1)} %copy-done.55), channel_id=1, replica_groups=mesh['rep'=4,'fsdp'=8] {'fsdp'}, dimensions={0}, use_global_device_ids=true | all-gather | bytes 442368 | tf_op jit(solution)/shard_map/all_gather | solution.py:58
  26.6 14.1 %all_gather.29 = bf16[256,1280]{1,0:T(8,128)(2,1)S(1)} all-gather(bf16[32,1280]{1,0:T(8,128)(2,1)S(1)} %copy-done.42), channel_id=1, replica_groups=mesh['rep'=4,'fsdp'=8] {'fsdp'}, dimensions={0}, use_global_device_ids=true | all-gather | bytes 737280 | tf_op jit(solution)/shard_map/all_gather | solution.py:56
  40.6 9.5 all_gather.30
  53.3 5.7 convolution_convert_fusion
  59.0 8.2 reshape.370
  67.3 7.5 copy.67
  74.8 164.6 %while.28 = (s32[]{:T(128)}, f32[2,32,1280]{1,2,0:T(8,128)}, f32[2,32,8]{1,2,0:T(8,128)}, bf16[2,512,8,160]{1,3,2,0:T(8,128)(2,1)}, s32[2]{0:T(128)}, /*index=5*...) while((s32[]{:T(128)}, f32[2,32,1280]{1,2,0:T(8,128)}, ...), condition=%wide.region_8.9_spmd.clone, body=%wide.region_4.8_spmd.clone.sunk | while | flops 409206784 | bytes 20717816 | solution.py:114
  85.8 29.1 %reduce-scatter.36.cloned.1.call-done = f32[32,8]{1,0:T(8,128)} async-done(((f32[256,8]{1,0:T(8,128)}), f32[32,8]{1,0:T(8,128)}) %reduce-scatter.36.cloned.1.call-update) | async-done | bytes 1040 | tf_op jit(solution)/shard_map/while
  116.3 39.1 %reduce-scatter.34.cloned.1.call-done = f32[32,1280]{1,0:T(8,128)} async-done(((f32[256,1280]{1,0:T(8,128)}), f32[32,1280]{1,0:T(8,128)}) %reduce-scatter.34.cloned.1.call-update) | async-done | bytes 163856 | tf_op jit(solution)/shard_map/while
  168.4 28.7 %reduce-scatter.36.cloned.1.call-done = f32[32,8]{1,0:T(8,128)} async-done(((f32[256,8]{1,0:T(8,128)}), f32[32,8]{1,0:T(8,128)}) %reduce-scatter.36.cloned.1.call-update) | async-done | bytes 1040 | tf_op jit(solution)/shard_map/while
  198.5 38.9 %reduce-scatter.34.cloned.1.call-done = f32[32,1280]{1,0:T(8,128)} async-done(((f32[256,1280]{1,0:T(8,128)}), f32[32,1280]{1,0:T(8,128)}) %reduce-scatter.34.cloned.1.call-update) | async-done | bytes 163856 | tf_op jit(solution)/shard_map/while
  248.4 26.2 %all-gather.15.cloned.1.call-done = bf16[1280,1280]{1,0:T(8,128)(2,1)} async-done(((bf16[160,1280]{1,0:T(8,128)(2,1)}), bf16[1280,1280]{1,0:T(8,128)(2,1)}) %all-gather.15.cloned.1.call-update) | async-done | bytes 3276816 | tf_op jit(solution)/shard_map/all_gather | solution.py:62
  277.8 31.4 %all-gather.17.cloned.1.call-done = bf16[1280,1280]{1,0:T(8,128)(2,1)} async-done(((bf16[160,1280]{1,0:T(8,128)(2,1)}), bf16[1280,1280]{1,0:T(8,128)(2,1)}) %all-gather.17.cloned.1.call-update) | async-done | bytes 3276816 | tf_op jit(solution)/shard_map/all_gather | solution.py:63
  311.9 32.0 %all-gather.19.cloned.1.call-done = bf16[1280,1280]{1,0:T(8,128)(2,1)} async-done(((bf16[160,1280]{1,0:T(8,128)(2,1)}), bf16[1280,1280]{1,0:T(8,128)(2,1)}) %all-gather.19.cloned.1.call-update) | async-done | bytes 3276816 | tf_op jit(solution)/shard_map/all_gather | solution.py:64
  353.2 127.2 %while.29 = (s32[]{:T(128)}, bf16[2,512,8,32]{1,3,2,0:T(8,128)(2,1)}, bf16[2,512,8,160]{1,3,2,0:T(8,128)(2,1)}, bf16[2,32,256]{1,2,0:T(8,128)(2,1)}, s32[2]{0:T(...) while((s32[]{:T(128)}, ...), condition=%wide.region_16.17_spmd.clone, body=%wide.region_14.16_spmd.clone.sunk | while | flops 882053120 | bytes 49334148 | solution.py:185
  353.9 10.1 %all-gather.6 = bf16[1,256,1280]{2,1,0:T(8,128)(2,1)S(1)} all-gather(bf16[1,32,1280]{2,1,0:T(8,128)(2,1)S(1)} %constant_dynamic-slice_fusion.4), channel_id=2, replica_groups=mesh['rep'=4,'fsdp'=8] {'fsdp'}, dimensions={1}, use_global_device_ids=true | all-gather | bytes 737280 | tf_op jit(solution)/shard_map/while/body/eval_jaxpr/all_gather | solution.py:157
  365.0 8.3 all-gather.7
  382.9 4.4 fusion.168
  387.3 28.0 %reduce-scatter.38.cloned.1.call-done = f32[32,256]{1,0:T(8,128)} async-done(((f32[256,256]{1,0:T(8,128)}), f32[32,256]{1,0:T(8,128)}) %reduce-scatter.38.cloned.1.call-update) | async-done | bytes 32784 | tf_op jit(solution)/shard_map/while
  417.5 10.0 %all-gather.6 = bf16[1,256,1280]{2,1,0:T(8,128)(2,1)S(1)} all-gather(bf16[1,32,1280]{2,1,0:T(8,128)(2,1)S(1)} %constant_dynamic-slice_fusion.4), channel_id=2, replica_groups=mesh['rep'=4,'fsdp'=8] {'fsdp'}, dimensions={1}, use_global_device_ids=true | all-gather | bytes 737280 | tf_op jit(solution)/shard_map/while/body/eval_jaxpr/all_gather | solution.py:157
  428.6 8.3 all-gather.7
  446.5 4.5 fusion.168
  451.0 27.9 %reduce-scatter.38.cloned.1.call-done = f32[32,256]{1,0:T(8,128)} async-done(((f32[256,256]{1,0:T(8,128)}), f32[32,256]{1,0:T(8,128)}) %reduce-scatter.38.cloned.1.call-update) | async-done | bytes 32784 | tf_op jit(solution)/shard_map/while
  487.7 4.4 copy.77
  520.3 40.3 %reduce-scatter.22.cloned.1.call-done = f32[160,256]{1,0:T(8,128)} async-done(((f32[1280,256]{1,0:T(8,128)}), f32[160,256]{1,0:T(8,128)}) %reduce-scatter.22.cloned.1.call-update) | async-done | bytes 163856 | tf_op jit(solution)/shard_map/reduce_scatter | solution.py:217
  560.7 53.4 %reduce-scatter.26.cloned.1.call-done = f32[96,1280]{1,0:T(8,128)} async-done(((f32[768,1280]{1,0:T(8,128)}), f32[96,1280]{1,0:T(8,128)}) %reduce-scatter.26.cloned.1.call-update) | async-done | bytes 491536 | tf_op jit(solution)/shard_map/reduce_scatter | solution.py:219
  614.1 66.4 %reduce-scatter.28.cloned.1.call-done = f32[160,1280]{1,0:T(8,128)} async-done(((f32[1280,1280]{1,0:T(8,128)}), f32[160,1280]{1,0:T(8,128)}) %reduce-scatter.28.cloned.1.call-update) | async-done | bytes 819216 | tf_op jit(solution)/shard_map/reduce_scatter | solution.py:220
  680.4 66.3 %reduce-scatter.30.cloned.1.call-done = f32[160,1280]{1,0:T(8,128)} async-done(((f32[1280,1280]{1,0:T(8,128)}), f32[160,1280]{1,0:T(8,128)}) %reduce-scatter.30.cloned.1.call-update) | async-done | bytes 819216 | tf_op jit(solution)/shard_map/reduce_scatter | solution.py:221
  746.8 66.4 %reduce-scatter.32.cloned.1.call-done = f32[160,1280]{1,0:T(8,128)} async-done(((f32[1280,1280]{1,0:T(8,128)}), f32[160,1280]{1,0:T(8,128)}) %reduce-scatter.32.cloned.1.call-update) | async-done | bytes 819216 | tf_op jit(solution)/shard_map/reduce_scatter | solution.py:222
  813.2 4.7 fusion.86
  821.1 43.6 %all-reduce = (f32[768]{0:T(1024)}, f32[1280]{0:T(1024)}, f32[1280]{0:T(1024)}) all-reduce(f32[768]{0:T(1024)S(1)} %get-tuple-element.232, f32[1280]{0:T(1024)S(1)} %get-tuple-element.235, f32[1280]{0:T(1024)S(1)} %copy-done.56), channel_id=1, replica_groups=mesh['rep'=4,'fsdp'=8] {'rep','fsdp'}, use_global_device_ids=true, to_apply=%region_25.26 | all-reduce | flops 3328 | bytes 26624 | tf_op jit(solution)/shard_map/psum | solution.py:213
  870.3 75.8 %all-reduce.4.cloned.1.call-done = (f32[32,1280]{1,0:T(8,128)}, f32[160,256]{1,0:T(8,128)}, f32[96,256]{1,0:T(8,128)}, f32[96,1280]{1,0:T(8,128)}, f32[160,1280]...) async-done(((f32[32,1280]{1,0:T(8,128)}, f32[160,256]{1,0:T(8,128)}, f32[96,256]{1,0:T(8,128)}, f32[96,1280]{1,0:T(8,128)}, f32[160,1280]{1,0:T(8,128)}, ...) | async-done | bytes 3375120 | tf_op jit(solution)/shard_map/psum | solution.py:224
  (307 shorter events, 144.0 us)
Async XLA Ops:
  7.2 16.2 %copy-start.1 = (bf16[2,512,768]{2,1,0:T(8,128)(2,1)S(1)}, bf16[2,512,768]{2,1,0:T(8,128)(2,1)}, u32[]{:S(2)}) copy-start(bf16[2,512,768]{2,1,0:T(8,128)(2,1)} %param.17) | copy-start | bytes 4718596
  7.2 46.1 %all-gather.13.cloned.1.call-start = ((), (), s32[]{:S(2)}) async-start(), calls=%async_computation.9 | async-start | bytes 2211840 | tf_op jit(solution)/shard_map/all_gather | solution.py:59
  25.9 24.7 %copy-start.48 = (f32[1280]{0:T(1024)S(1)}, f32[1280]{0:T(1024)}, u32[]{:S(2)}) copy-start(f32[1280]{0:T(1024)} %param.21) | copy-start | bytes 15364
  74.8 40.1 %reduce-scatter.36.cloned.1.call-start = ((), (), s32[]{:S(2)}) async-start(), calls=%async_computation.21 | async-start | bytes 147456 | tf_op jit(solution)/shard_map/while
  80.8 74.6 %reduce-scatter.34.cloned.1.call-start = ((), (), s32[]{:S(2)}) async-start(), calls=%async_computation.20 | async-start | bytes 1474560 | tf_op jit(solution)/shard_map/while
  157.4 39.7 %reduce-scatter.36.cloned.1.call-start = ((), (), s32[]{:S(2)}) async-start(), calls=%async_computation.21 | async-start | bytes 147456 | tf_op jit(solution)/shard_map/while
  163.4 74.1 %reduce-scatter.34.cloned.1.call-start = ((), (), s32[]{:S(2)}) async-start(), calls=%async_computation.20 | async-start | bytes 1474560 | tf_op jit(solution)/shard_map/while
  239.5 35.1 %all-gather.15.cloned.1.call-start = ((), (), s32[]{:S(2)}) async-start(), calls=%async_computation.10 | async-start | bytes 3686400 | tf_op jit(solution)/shard_map/all_gather | solution.py:62
  240.0 69.2 %all-gather.17.cloned.1.call-start = ((), (), s32[]{:S(2)}) async-start(), calls=%async_computation.11 | async-start | bytes 3686400 | tf_op jit(solution)/shard_map/all_gather | solution.py:63
  240.8 103.1 %all-gather.19.cloned.1.call-start = ((), (), s32[]{:S(2)}) async-start(), calls=%async_computation.12 | async-start | bytes 3686400 | tf_op jit(solution)/shard_map/all_gather | solution.py:64
  245.5 29.1 %copy-start.34 = (f32[32,1280]{1,0:T(8,128)S(1)}, f32[32,1280]{1,0:T(8,128)}, u32[]{:S(2)}) copy-start(f32[32,1280]{1,0:T(8,128)} %convert_element_type.107) | copy-start | bytes 491524
  245.8 31.5 %copy-start.18 = (f32[2,32,1280]{2,1,0:T(8,128)}, f32[2,32,1280]{2,1,0:T(8,128)S(1)}, u32[]{:S(2)}) copy-start(f32[2,32,1280]{2,1,0:T(8,128)S(1)} %copy.70) | copy-start | bytes 983044
  246.6 30.7 %copy-start.39 = (f32[2,32,8]{2,1,0:T(8,128)}, f32[2,32,8]{2,1,0:T(8,128)S(1)}, u32[]{:S(2)}) copy-start(f32[2,32,8]{2,1,0:T(8,128)S(1)} %copy.69) | copy-start | bytes 6148
  248.4 29.3 %copy-start.47 = (f32[1280]{0:T(1024)S(1)}, f32[1280]{0:T(1024)}, u32[]{:S(2)}) copy-start(f32[1280]{0:T(1024)} %param.22) | copy-start | bytes 15364
  277.3 72.6 %copy-start.8 = (f32[2,32,1280]{2,1,0:T(8,128)}, f32[2,32,1280]{2,1,0:T(8,128)S(1)}, u32[]{:S(2)}) copy-start(f32[2,32,1280]{2,1,0:T(8,128)S(1)} %get-tuple-element.300) | copy-start | bytes 983044
  277.3 66.6 %copy-start.37 = (bf16[2,32,1280]{2,1,0:T(8,128)(2,1)S(1)}, bf16[2,32,1280]{2,1,0:T(8,128)(2,1)}, u32[]{:S(2)}) copy-start(bf16[2,32,1280]{2,1,0:T(8,128)(2,1)} %param.29) | copy-start | bytes 491524
  277.8 70.3 %copy-start.22 = (bf16[64,1280]{1,0:T(8,128)(2,1)}, bf16[64,1280]{1,0:T(8,128)(2,1)S(1)}, u32[]{:S(2)}) copy-start(bf16[64,1280]{1,0:T(8,128)(2,1)S(1)} %multiply_convert_fusion.5) | copy-start | bytes 491524
  311.9 36.3 %copy-start.30 = (f32[64,1280]{1,0:T(8,128)}, f32[64,1280]{1,0:T(8,128)S(1)}, u32[]{:S(2)}) copy-start(f32[64,1280]{1,0:T(8,128)S(1)} %fusion.85) | copy-start | bytes 983044
  353.2 62.0 %reduce-scatter.38.cloned.1.call-start = ((), (), s32[]{:S(2)}) async-start(), calls=%async_computation.22 | async-start | bytes 294912 | tf_op jit(solution)/shard_map/while
  382.9 33.3 %copy-start.43 = (bf16[2,32,256]{1,2,0:T(8,128)(2,1)S(1)}, bf16[2,32,256]{1,2,0:T(8,128)(2,1)}, u32[]{:S(2)}) copy-start(bf16[2,32,256]{1,2,0:T(8,128)(2,1)} %get-tuple-element.468) | copy-start | bytes 98308 | tf_op jit(solution)/shard_map/while
  382.9 34.0 %copy-start.26 = (bf16[2,32,1280]{2,1,0:T(8,128)(2,1)S(1)}, bf16[2,32,1280]{2,1,0:T(8,128)(2,1)}, u32[]{:S(2)}) copy-start(bf16[2,32,1280]{2,1,0:T(8,128)(2,1)} %copy-done.25) | copy-start | bytes 491524 | tf_op jit(solution)/shard_map/while
  416.8 62.0 %reduce-scatter.38.cloned.1.call-start = ((), (), s32[]{:S(2)}) async-start(), calls=%async_computation.22 | async-start | bytes 294912 | tf_op jit(solution)/shard_map/while
  446.5 33.3 %copy-start.43 = (bf16[2,32,256]{1,2,0:T(8,128)(2,1)S(1)}, bf16[2,32,256]{1,2,0:T(8,128)(2,1)}, u32[]{:S(2)}) copy-start(bf16[2,32,256]{1,2,0:T(8,128)(2,1)} %get-tuple-element.468) | copy-start | bytes 98308 | tf_op jit(solution)/shard_map/while
  446.5 33.9 %copy-start.26 = (bf16[2,32,1280]{2,1,0:T(8,128)(2,1)S(1)}, bf16[2,32,1280]{2,1,0:T(8,128)(2,1)}, u32[]{:S(2)}) copy-start(bf16[2,32,1280]{2,1,0:T(8,128)(2,1)} %copy-done.25) | copy-start | bytes 491524 | tf_op jit(solution)/shard_map/while
  480.4 39.9 %reduce-scatter.24.cloned.1.call-start = ((), (), s32[]{:S(2)}) async-start(), calls=%async_computation.14 | async-start | bytes 884736 | tf_op jit(solution)/shard_map/reduce_scatter | solution.py:218
  485.2 75.5 %reduce-scatter.22.cloned.1.call-start = ((), (), s32[]{:S(2)}) async-start(), calls=%async_computation.13 | async-start | bytes 1474560 | tf_op jit(solution)/shard_map/reduce_scatter | solution.py:217
  487.7 126.4 %reduce-scatter.26.cloned.1.call-start = ((), (), s32[]{:S(2)}) async-start(), calls=%async_computation.15 | async-start | bytes 4423680 | tf_op jit(solution)/shard_map/reduce_scatter | solution.py:219
  498.6 181.8 %reduce-scatter.28.cloned.1.call-start = ((), (), s32[]{:S(2)}) async-start(), calls=%async_computation.16 | async-start | bytes 7372800 | tf_op jit(solution)/shard_map/reduce_scatter | solution.py:220
  503.7 243.0 %reduce-scatter.30.cloned.1.call-start = ((), (), s32[]{:S(2)}) async-start(), calls=%async_computation.17 | async-start | bytes 7372800 | tf_op jit(solution)/shard_map/reduce_scatter | solution.py:221
  508.5 304.6 %reduce-scatter.32.cloned.1.call-start = ((), (), s32[]{:S(2)}) async-start(), calls=%async_computation.18 | async-start | bytes 7372800 | tf_op jit(solution)/shard_map/reduce_scatter | solution.py:222
  513.4 432.8 %all-reduce.4.cloned.1.call-start = ((), (), s32[]{:S(2)}) async-start(), calls=%async_computation.19 | async-start | bytes 6750208 | tf_op jit(solution)/shard_map/psum | solution.py:224
  818.0 46.7 %copy-start.9 = (f32[2,32,1280]{2,1,0:T(8,128)S(1)}, f32[2,32,1280]{2,1,0:T(8,128)}, u32[]{:S(2)}) copy-start(f32[2,32,1280]{2,1,0:T(8,128)} %copy-done.8) | copy-start | bytes 983044
  (51 other events, 205.1 us)
Sparse Core Ops, SparseCore 0:
  9.9 31.6 all-gather.12
  80.9 33.9 reduce-scatter.35
  118.2 37.1 reduce-scatter.33
  163.5 33.5 reduce-scatter.35
  200.2 37.1 reduce-scatter.33
  241.8 32.7 all-gather.14
  276.5 32.7 all-gather.16
  311.1 32.7 all-gather.18
  381.6 33.6 reduce-scatter.37
  445.1 33.6 reduce-scatter.37
  485.3 34.9 reduce-scatter.23
  523.4 37.1 reduce-scatter.21
  564.2 49.8 reduce-scatter.25
  617.4 63.0 reduce-scatter.27
  683.7 63.0 reduce-scatter.29
  750.1 63.0 reduce-scatter.31
  816.5 129.5 all-reduce.3
where the time goes:
time: 969 us; the launch traced here: 963 us
  waiting for transfers between devices  656 us (68%)
  blocking collectives  115 us (12%)
  matrix products  86.9 us (9%)
  local copies, waits for them, and re-layouts  70.2 us (7%)
  other arithmetic  19.9 us (2%)
  between operations  14.8 us (2%)
    while x12, waiting for transfers between devices  192 us
    psum x1, waiting for transfers between devices, per_device(): lax.psum((group_parts[0], group_parts[1], group_parts[2], group_parts[3],...  75.8 us
    reduce_scatter x1, waiting for transfers between devices, per_device(): lax.psum_scatter(down_local, 'fsdp', scatter_dimension=0, tiled=True)  66.4 us
    reduce_scatter x1, waiting for transfers between devices, per_device(): lax.psum_scatter(out_local, 'fsdp', scatter_dimension=0, tiled=True)  66.4 us
    reduce_scatter x1, waiting for transfers between devices, per_device(): lax.psum_scatter(up_local, 'fsdp', scatter_dimension=0, tiled=True)  66.3 us
    reduce_scatter x1, waiting for transfers between devices, per_device(): lax.psum_scatter(value_local, 'fsdp', scatter_dimension=0, tiled=True)  53.4 us
    psum x1, blocking collectives, per_device(): lax.psum((byte_part, query_part_gain, mixer_part), ('rep', 'fsdp'))  43.6 us
    reduce_scatter x1, waiting for transfers between devices, per_device(): lax.psum_scatter(query_local, 'fsdp', scatter_dimension=0, tiled=True)  40.3 us
  transfers between devices with their start and end apart: 17, of which 16 were waited for; matrix products, arithmetic and copies ran while one was open for 9% of the time, Pallas kernels for 0%

commit v1 on v0

--- a/solution.py
+++ b/solution.py
@@ -1,6 +1,8 @@
 import jax
 import jax.numpy as jnp
 from jax import lax
+from jax.experimental import pallas as pl
+from jax.experimental.pallas import tpu as pltpu
 from jax.sharding import PartitionSpec as P
 
 DL = 1280
@@ -28,7 +30,7 @@
     return inverse * (scaled - mean_one - normal * mean_two)
 
 
-def per_device(
+def per_device_plain(
     byte_feats,
     latent_init,
     prefix,
@@ -249,7 +251,544 @@
     )
 
 
+BF = jnp.bfloat16
+F32 = jnp.float32
+N = 8
+NZ = 4
+LOG2E = 1.4426950408889634
+ANY = pl.BlockSpec(memory_space=pl.ANY)
+VMEM = pl.BlockSpec(memory_space=pltpu.VMEM)
+SMEM = pl.BlockSpec(memory_space=pltpu.SMEM)
+
+
+def dot(a, b, ca, cb):
+    return lax.dot_general(a, b, (((ca,), (cb,)), ((), ())), preferred_element_type=F32)
+
+
+def send(x, k):
+    return lax.ppermute(x, "fsdp", [(i, i ^ k) for i in range(N)])
+
+
+def send_split(x, even, odd):
+    return lax.ppermute(x, "fsdp", [(i, i ^ (odd if i & 1 else even)) for i in range(N)])
+
+
+def send_z(x, k):
+    return lax.ppermute(x, "rep", [(i, i ^ k) for i in range(NZ)])
+
+
+def gather_wide(x):
+    near = send(x, 1)
+    ra = send_split(x, 2, 4)
+    rb = send_split(x, 4, 2)
+    rd = send_split(ra, 4, 2)
+    na, nb, nd = send(ra, 1), send(rb, 1), send(rd, 1)
+    return [x, near, ra, rb, rd, na, nb, nd], [
+        (0, 0), (1, 1), (2, 4), (4, 2), (6, 6), (5, 3), (3, 5), (7, 7),
+    ]
+
+
+def gather_direct(x):
+    r2, r4, r6 = send(x, 2), send(x, 4), send(x, 6)
+    return [x, send(x, 1), r2, send(r2, 1), r4, send(r4, 1), r6, send(r6, 1)], [
+        (k, k) for k in range(N)
+    ]
+
+
+def owner(meta, rel):
+    me = meta[0]
+    even, odd = rel
+    if even == odd:
+        return me ^ even
+    return me ^ jnp.where((me & 1) == 0, even, odd)
+
+
+def call(body, out, ins, specs, scratch=(), name=None, cost=None):
+    return pl.pallas_call(
+        body,
+        out_shape=out,
+        in_specs=specs,
+        out_specs=jax.tree.map(lambda _: VMEM, out),
+        scratch_shapes=list(scratch),
+        name=name,
+        cost_estimate=pl.CostEstimate(flops=cost[0], bytes_accessed=cost[1], transcendentals=0) if cost else None,
+    )(*ins)
+
+
+def sds(shape, dtype):
+    return jax.ShapeDtypeStruct(shape, dtype)
+
+
+def ln_parts(v):
+    centered = v - jnp.mean(v, axis=-1, keepdims=True)
+    inverse = lax.rsqrt(jnp.mean(centered * centered, axis=-1, keepdims=True) + EPSILON)
+    return centered * inverse, inverse
+
+
+def ln_back(grad, hat, inverse, gain):
+    scaled = grad * gain
+    return inverse * (
+        scaled
+        - jnp.mean(scaled, axis=-1, keepdims=True)
+        - hat * jnp.mean(scaled * hat, axis=-1, keepdims=True)
+    )
+
+
+def pack_kernel(wk, wv, wq, lat, out):
+    rows = wk.shape[0]
+    out[0:rows, :] = wk[...]
+    for c in range(5):
+        out[rows * (c + 1) : rows * (c + 2), :] = wv[:, 256 * c : 256 * (c + 1)]
+    at = rows * 6
+    out[at : at + wq.shape[0], :] = wq[...]
+    at += wq.shape[0]
+    for c in range(5):
+        out[at : at + lat.shape[0], :] = lat[:, 256 * c : 256 * (c + 1)]
+        at += lat.shape[0]
+
+
+def forward_kernel(rels, meta, x, bg, qg, *rest):
+    pieces, rest = rest[:N], rest[N:]
+    xn_o, k_o, vt_o, wkv_o, wq_o, q_o, zn_o, mine_o, theirs_o = rest[:9]
+    lat, aat, lls, acc, sem = rest[9:]
+    copies = []
+    for piece, rel in zip(pieces, rels):
+        j = owner(meta, rel)
+        r96 = pl.ds(pl.multiple_of(j * 96, 32), 96)
+        r160 = pl.ds(pl.multiple_of(j * 160, 32), 160)
+        r32 = pl.ds(pl.multiple_of(j * 32, 32), 32)
+        for c in range(6):
+            copies.append((piece.at[pl.ds(96 * c, 96), :], wkv_o.at[r96, pl.ds(256 * c, 256)]))
+        copies.append((piece.at[pl.ds(576, 160), :], wq_o.at[r160, :]))
+        for c in range(5):
+            copies.append((piece.at[pl.ds(736 + 32 * c, 32), :], lat.at[r32, pl.ds(256 * c, 256)]))
+    handles = [pltpu.make_async_copy(a, b, sem.at[n]) for n, (a, b) in enumerate(copies)]
+    for h in handles:
+        h.start()
+    hat, _ = ln_parts(x[...].astype(F32))
+    xn_o[...] = (hat * bg[...]).astype(BF)
+    for h in handles:
+        h.wait()
+    zhat, _ = ln_parts(lat[...].astype(F32))
+    zn_o[...] = (zhat * qg[...]).astype(BF)
+    q_o[...] = dot(zn_o[...], wq_o[...], 1, 0).astype(BF)
+    k_o[...] = dot(xn_o[...], wkv_o[:, 0:256], 1, 0).astype(BF)
+    for c in range(5):
+        vt_o[256 * c : 256 * (c + 1), :] = dot(
+            wkv_o[:, 256 * (c + 1) : 256 * (c + 2)], xn_o[...], 0, 1
+        ).astype(BF)
+    lanes = lax.broadcasted_iota(jnp.int32, (256, 256), 1) // 32
+    pos = lax.broadcasted_iota(jnp.int32, (256, 512), 1) + meta[0] * 512
+    own = STRIDE * (lax.broadcasted_iota(jnp.int32, (256, 1), 0) + 1)
+    lls[...] = jnp.zeros_like(lls)
+    lane = lax.broadcasted_iota(jnp.int32, (256, 128), 1)
+    for s in range(2):
+        seen = jnp.maximum(own, meta[2 + s])
+
+        def head(h, carry, s=s, seen=seen):
+            qh = jnp.where(lanes == h, q_o[...], jnp.zeros((), BF))
+            scores = dot(qh, k_o[512 * s : 512 * (s + 1), :], 1, 1)
+            e = jnp.where(pos < seen, jnp.exp2(scores * (LOG2E * 32 ** (-0.5))), 0.0)
+            lls[s] = lls[s] + jnp.where(lane == h, jnp.sum(e, axis=-1, keepdims=True), 0.0)
+            rows = pl.ds(pl.multiple_of(h * 160, 32), 160)
+            aat[s, rows, :] = dot(vt_o[rows, 512 * s : 512 * (s + 1)], e.astype(BF), 1, 1).astype(BF)
+            return carry
+
+        lax.fori_loop(0, H, head, 0, unroll=2)
+        acc[:, 0:1280] = aat[s].T
+        acc[:, 1280:1408] = lls[s].astype(BF)
+        for kk in range(4):
+            for odd, ref in ((0, mine_o), (1, theirs_o)):
+                j = meta[0] ^ (2 * kk + odd)
+                ref[kk, 32 * s : 32 * (s + 1), :] = acc[pl.ds(pl.multiple_of(j * 32, 32), 32), :]
+
+
+def add4_kernel(a, b, *outs):
+    for kk in range(4):
+        outs[kk][...] = (a[kk].astype(F32) + b[kk].astype(F32)).astype(BF)
+
+
+def latent_kernel(rels, meta, m0, r1, r2, r3, lat, mg, cot, *rest):
+    wout_p, wup_p, wdown_p, rest = rest[:N], rest[N : 2 * N], rest[2 * N : 3 * N], rest[3 * N :]
+    latents_o, agb_o, mine_o, theirs_o, dab_o, init_o = rest[:6]
+    wout, wup, wdown, sem = rest[6:]
+    groups = []
+    for g, (ps, w) in enumerate(((wout_p, wout), (wup_p, wup), (wdown_p, wdown))):
+        hs = []
+        for n, (p, rel) in enumerate(zip(ps, rels)):
+            rows = pl.ds(pl.multiple_of(owner(meta, rel) * 160, 32), 160)
+            hs.append(pltpu.make_async_copy(p, w.at[rows, :], sem.at[g, n]))
+        for h in hs:
+            h.start()
+        groups.append(hs)
+    total = (m0[...].astype(F32) + r1[...].astype(F32)) + (r2[...].astype(F32) + r3[...].astype(F32))
+    aa = total[:, 0:1280]
+    ll = total[:, 1280:1408]
+    head = lax.broadcasted_iota(jnp.int32, (64, 1280), 1) // 160
+    inv = jnp.zeros((64, 1280), F32)
+    for h in range(H):
+        inv = jnp.where(head == h, 1.0 / ll[:, h : h + 1], inv)
+    oo = aa * inv
+    ob = oo.astype(BF)
+    for h in groups[0]:
+        h.wait()
+    start = lat[...].astype(F32)
+    hh = jnp.concatenate([start, start], axis=0) + dot(ob, wout[...], 1, 0)
+    hat, inverse = ln_parts(hh)
+    hn = (hat * mg[...]).astype(BF)
+    for h in groups[1]:
+        h.wait()
+    uu = dot(hn, wup[...], 1, 0)
+    cdf = 0.5 * (1.0 + lax.erf(uu * (0.5**0.5)))
+    gg = (uu * cdf).astype(BF)
+    slope = cdf + uu * (jnp.exp(-0.5 * uu * uu) * 0.3989422804014327)
+    for h in groups[2]:
+        h.wait()
+    latents_o[...] = (hh + dot(gg, wdown[...], 1, 0)).astype(BF)
+    du = (dot(cot[...], wdown[...], 1, 1) * slope).astype(BF)
+    dhn = dot(du, wup[...], 1, 1)
+    dhh = cot[...].astype(F32) + ln_back(dhn, hat, inverse, mg[...])
+    init_o[...] = dhh[0:32] + dhh[32:64]
+    dhb = dhh.astype(BF)
+    dob = dot(dhb, wout[...], 1, 1).astype(BF).astype(F32)
+    dab_o[:, 0:1280] = (dob * inv).astype(BF)
+    prod = dob * oo
+    lane = lax.broadcasted_iota(jnp.int32, (64, 128), 1)
+    dlb = jnp.zeros((64, 128), F32)
+    for h in range(H):
+        part = jnp.sum(jnp.where(head == h, prod, 0.0), axis=-1, keepdims=True)
+        dlb = jnp.where(lane == h, -part / ll[:, h : h + 1], dlb)
+    dab_o[:, 1280:1408] = dlb.astype(BF)
+    agb_o[0] = dhb
+    agb_o[1] = du
+    agb_o[2] = cot[...]
+    me = meta[0]
+    for j in range(N):
+        kk = (me >> 1) ^ (j >> 1)
+        cols = slice(160 * j, 160 * (j + 1))
+
+        @pl.when((me & 1) == (j & 1))
+        def _():
+            for n, v in enumerate((ob, hn, gg)):
+                mine_o[kk, n] = v[:, cols]
+
+        @pl.when((me & 1) != (j & 1))
+        def _():
+            for n, v in enumerate((ob, hn, gg)):
+                theirs_o[kk, n] = v[:, cols]
+
+
+def backward_kernel(rels, meta, k, vt, xn, q, zn, *rest):
+    pieces, rest = rest[:N], rest[N:]
+    dkvt_o, mine_o, theirs_o = rest[:3]
+    dabx, dabt, qt, xnt, dqs, dw, dqg, sem = rest[3:]
+    handles = []
+    for n, (p, rel) in enumerate(zip(pieces, rels)):
+        rows = pl.ds(pl.multiple_of(owner(meta, rel) * 32, 32), 32)
+        for s in range(2):
+            handles.append(
+                pltpu.make_async_copy(p.at[pl.ds(32 * s, 32), :], dabx.at[s, rows, :], sem.at[2 * n + s])
+            )
+    for h in handles:
+        h.start()
+    qt[...] = q[...].T
+    xnt[...] = xn[...].T
+    dqs[...] = jnp.zeros_like(dqs)
+    for h in handles:
+        h.wait()
+    lanes = lax.broadcasted_iota(jnp.int32, (256, 256), 1) // 32
+    pos = lax.broadcasted_iota(jnp.int32, (256, 512), 1) + meta[0] * 512
+    own = STRIDE * (lax.broadcasted_iota(jnp.int32, (256, 1), 0) + 1)
+    lane = lax.broadcasted_iota(jnp.int32, (256, 128), 1)
+    scale = 32 ** (-0.5)
+    for s in range(2):
+        seen = jnp.maximum(own, meta[2 + s])
+        dabt[...] = dabx[s, :, 0:1280].T
+        cols = slice(512 * s, 512 * (s + 1))
+
+        def head(h, carry, s=s, seen=seen, cols=cols):
+            qh = jnp.where(lanes == h, q[...], jnp.zeros((), BF))
+            scores = dot(qh, k[cols, :], 1, 1)
+            e = jnp.where(pos < seen, jnp.exp2(scores * (LOG2E * scale)), 0.0)
+            rows = pl.ds(pl.multiple_of(h * 160, 32), 160)
+            dkvt_o[pl.ds(pl.multiple_of(256 + h * 160, 32), 160), cols] = dot(
+                dabt[rows, :], e.astype(BF), 1, 0
+            ).astype(BF)
+            dlb = jnp.sum(
+                jnp.where(lane == h, dabx[s, :, 1280:1408].astype(F32), 0.0), axis=-1, keepdims=True
+            )
+            dee = dot(dabt[rows, :], vt[rows, cols], 0, 0) + dlb
+            dss = (e * dee).astype(BF)
+            krows = pl.ds(pl.multiple_of(h * 32, 32), 32)
+            dkvt_o[krows, cols] = (dot(qt[krows, :], dss, 1, 0) * scale).astype(BF)
+            dqs[...] += jnp.where(lanes == h, dot(dss, k[cols, :], 1, 0), 0.0)
+            return carry
+
+        lax.fori_loop(0, H, head, 0, unroll=2)
+    dq = (dqs[...] * scale).astype(BF)
+    for c in range(6):
+        dw[:, 256 * c : 256 * (c + 1)] = dot(
+            xnt[...], dkvt_o[256 * c : 256 * (c + 1), :], 1, 1
+        ).astype(BF)
+    dqg[...] = dot(zn[...], dq, 0, 0).astype(BF)
+    dqs[...] = dqs[...] * scale
+    for kk in range(4):
+        for odd, ref in ((0, mine_o), (1, theirs_o)):
+            j = meta[0] ^ (2 * kk + odd)
+            r96 = pl.ds(pl.multiple_of(j * 96, 32), 96)
+            for c in range(6):
+                ref[kk, 96 * c : 96 * (c + 1), :] = dw[r96, 256 * c : 256 * (c + 1)]
+            ref[kk, 576:736, :] = dqg[pl.ds(pl.multiple_of(j * 160, 32), 160), :]
+            ref[kk, 736:768, :] = dqs[pl.ds(pl.multiple_of(j * 32, 32), 32), :].astype(BF)
+
+
+def bytes_kernel(x, bg, wkv, dkvt, out):
+    hat, inverse = ln_parts(x[...].astype(F32))
+    dxn = dot(dkvt[...], wkv[...], 0, 1)
+    out[...] = ln_back(dxn, hat, inverse, bg[...])
+
+
+def latent_grads_kernel(meta, init, *rest):
+    rows, cols, outs, (xs, ys, acc) = rest[:N], rest[N : 2 * N], rest[2 * N : 2 * N + 4], rest[2 * N + 4 :]
+    for k in range(N):
+        for n in range(3):
+            ys[n, 64 * k : 64 * (k + 1), :] = rows[k][n]
+            xs[n, 64 * k : 64 * (k + 1), :] = cols[k][n]
+    for n in range(3):
+        acc[160 * n : 160 * (n + 1), :] = dot(xs[n], ys[n], 0, 0).astype(BF)
+    acc[480:512, :] = init[...].astype(BF)
+    for r in range(NZ):
+        z = meta[1] ^ r
+        outs[r][...] = acc[pl.ds(pl.multiple_of(z * 128, 128), 128), :]
+
+
+def row_sums(a, b):
+    ones = jnp.ones((8, a.shape[1]), F32)
+    return lax.dot_general(
+        ones, a * b, (((1,), (1,)), ((), ())), precision=lax.Precision.HIGHEST, preferred_element_type=F32
+    )
+
+
+def finish_latent_kernel(meta, wup, mgs, *rest):
+    pieces, (out_o, up_o, down_o, init_o, norm_o, acc) = rest[:NZ], rest[NZ:]
+    for r in range(NZ):
+        z = meta[1] ^ r
+        acc[pl.ds(pl.multiple_of(z * 128, 128), 128), :] = pieces[r][...]
+    out_o[...] = acc[0:160, :].astype(F32)
+    up_o[...] = acc[160:320, :].astype(F32)
+    down_o[...] = acc[320:480, :].astype(F32)
+    init_o[...] = acc[480:512, :].astype(F32)
+    norm_o[...] = row_sums(up_o[...], wup[...].astype(F32)) / mgs[...]
+
+
+def finish_kernel(meta, wk, wv, wq, wq_full, lat, qg, bgs, qgs, init, mix, *rest):
+    pieces, (key_o, value_o, query_o, init_o, norm_o, acc) = rest[:NZ], rest[NZ:]
+    for r in range(NZ):
+        z = meta[1] ^ r
+        acc[pl.ds(pl.multiple_of(z * 192, 64), 192), :] = pieces[r][...]
+    key_o[...] = acc[0:96, :].astype(F32)
+    sums = row_sums(key_o[...], wk[...].astype(F32))
+    for c in range(5):
+        cols = slice(256 * c, 256 * (c + 1))
+        part = acc[96 * (c + 1) : 96 * (c + 2), :].astype(F32)
+        value_o[:, cols] = part
+        sums = sums + row_sums(part, wv[:, cols].astype(F32))
+    query_o[...] = acc[576:736, :].astype(F32)
+    dzn = dot(acc[736:768, :], wq_full[...], 1, 1)
+    hat, inverse = ln_parts(lat[...].astype(F32))
+    init_o[...] = init[...] + ln_back(dzn, hat, inverse, qg[...])
+    norm_o[...] = jnp.zeros_like(norm_o)
+    norm_o[0:8, 0:96] = sums / bgs[...]
+    norm_o[8:16, 0:160] = mix[...]
+    norm_o[16:24, 0:160] = row_sums(query_o[...], wq[...].astype(F32)) / qgs[...]
+
+
+def norms_kernel(meta, *rest):
+    pieces, (byte_o, mixer_o, query_o) = rest[:N], rest[N:]
+    for k in range(N):
+        j = meta[0] ^ k
+        byte_o[pl.ds(j, 1), :] = pieces[k][0:1, 0:96]
+        mixer_o[pl.ds(j, 1), :] = pieces[k][8:9, 0:160]
+        query_o[pl.ds(j, 1), :] = pieces[k][16:17, 0:160]
+
+
+def part(f, *args):
+    def body(*refs):
+        return f(*args, *refs)
+
+    return body
+
+
+def per_device_fast(
+    byte_feats,
+    latent_init,
+    prefix,
+    byte_gain,
+    query_gain,
+    mixer_gain,
+    query_weight,
+    key_weight,
+    value_weight,
+    out_weight,
+    up_weight,
+    down_weight,
+    cotangent,
+):
+    me = lax.axis_index("fsdp")
+    zi = lax.axis_index("rep")
+    meta = jnp.concatenate([jnp.stack([me, zi]).astype(jnp.int32), prefix])
+    seqs, rows, width = byte_feats.shape
+    own = latent_init.shape[0]
+    x = byte_feats.reshape(seqs * rows, width)
+    cot = cotangent.reshape(seqs * own, DL)
+    bg = byte_gain.reshape(1, -1)
+    qg = query_gain.reshape(1, -1)
+    mg = mixer_gain.reshape(1, -1)
+    packed = call(pack_kernel, sds((896, 256), BF), (key_weight, value_weight, query_weight, latent_init), [VMEM] * 4, name="pack")
+    pieces, rels = gather_wide(packed)
+    wout_p, _ = gather_wide(out_weight)
+    wup_p, _ = gather_wide(up_weight)
+    wdown_p, _ = gather_wide(down_weight)
+    xn, k, vt, wkv, wq_full, q, zn, mine, theirs = call(
+        part(forward_kernel, rels),
+        (
+            sds((1024, 768), BF), sds((1024, 256), BF), sds((1280, 1024), BF), sds((768, 1536), BF),
+            sds((1280, 256), BF), sds((256, 256), BF), sds((256, 1280), BF),
+            sds((4, 64, 1408), BF), sds((4, 64, 1408), BF),
+        ),
+        (meta, x, bg, qg, *pieces),
+        [SMEM, VMEM, VMEM, VMEM] + [ANY] * N,
+        [
+            pltpu.VMEM((256, 1280), BF), pltpu.VMEM((2, 1280, 256), BF), pltpu.VMEM((2, 256, 128), F32),
+            pltpu.VMEM((256, 1408), BF), pltpu.SemaphoreType.DMA((12 * N,)),
+        ],
+        name="forward",
+        cost=(8_000_000_000, 12_000_000),
+    )
+    got = send(theirs, 1)
+    m = call(add4_kernel, (sds((64, 1408), BF),) * 4, (mine, got), [VMEM] * 2, name="add4")
+    r1, r2, r3 = send(m[1], 2), send(m[2], 4), send(m[3], 6)
+    latents, agb, amine, atheirs, dabx, init = call(
+        part(latent_kernel, rels),
+        (
+            sds((64, 1280), BF), sds((3, 64, 1280), BF), sds((4, 3, 64, 160), BF), sds((4, 3, 64, 160), BF),
+            sds((64, 1408), BF), sds((32, 1280), F32),
+        ),
+        (meta, m[0], r1, r2, r3, latent_init, mg, cot, *wout_p, *wup_p, *wdown_p),
+        [SMEM] + [VMEM] * 7 + [ANY] * (3 * N),
+        [pltpu.VMEM((1280, 1280), BF)] * 3 + [pltpu.SemaphoreType.DMA((3, N))],
+        name="latent",
+        cost=(5_000_000_000, 12_000_000),
+    )
+    dab_p, drels = gather_direct(dabx)
+    dkvt, gmine, gtheirs = call(
+        part(backward_kernel, drels),
+        (sds((1536, 1024), BF), sds((4, 768, 256), BF), sds((4, 768, 256), BF)),
+        (meta, k, vt, xn, q, zn, *dab_p),
+        [SMEM] + [VMEM] * 5 + [ANY] * N,
+        [
+            pltpu.VMEM((2, 256, 1408), BF), pltpu.VMEM((1280, 256), BF), pltpu.VMEM((256, 256), BF),
+            pltpu.VMEM((768, 1024), BF), pltpu.VMEM((256, 256), F32), pltpu.VMEM((768, 1536), BF),
+            pltpu.VMEM((1280, 256), BF), pltpu.SemaphoreType.DMA((2 * N,)),
+        ],
+        name="backward",
+        cost=(10_000_000_000, 12_000_000),
+    )
+    rows_p, _ = gather_wide(agb)
+    at = send(atheirs, 1)
+    cols_p = [amine[0], at[0]]
+    for kk in range(1, 4):
+        both = send(jnp.stack([amine[kk], at[kk]]), 2 * kk)
+        cols_p += [both[0], both[1]]
+    even = [0, 1, 2, 6, 3, 5, 4, 7]
+    odd = [0, 1, 3, 5, 2, 6, 4, 7]
+    is_odd = (me & 1) == 1
+    rows_r = [
+        rows_p[a] if a == b else jnp.where(is_odd, rows_p[b], rows_p[a]) for a, b in zip(even, odd)
+    ]
+    oud = call(
+        latent_grads_kernel,
+        (sds((128, 1280), BF),) * NZ,
+        (meta, init, *rows_r, *cols_p),
+        [SMEM] + [VMEM] * (1 + 2 * N),
+        [pltpu.VMEM((3, 512, 160), BF), pltpu.VMEM((3, 512, 1280), BF), pltpu.VMEM((512, 1280), BF)],
+        name="latent_grads",
+        cost=(1_000_000_000, 6_000_000),
+    )
+    zsum = (
+        oud[0].astype(F32) + send_z(oud[1], 1).astype(F32) + send_z(oud[2], 2).astype(F32) + send_z(oud[3], 3).astype(F32)
+    ).astype(BF)
+    zall = [zsum, send_z(zsum, 1), send_z(zsum, 2), send_z(zsum, 3)]
+    mgs = lax.dynamic_slice_in_dim(mixer_gain, me * 160, 160, 0).reshape(1, 160)
+    qgs = lax.dynamic_slice_in_dim(query_gain, me * 160, 160, 0).reshape(1, 160)
+    bgs = lax.dynamic_slice_in_dim(byte_gain, me * 96, 96, 0).reshape(1, 96)
+    out_g, up_g, down_g, init_sum, mix = call(
+        finish_latent_kernel,
+        (sds((160, 1280), F32),) * 3 + (sds((32, 1280), F32), sds((8, 160), F32)),
+        (meta, up_weight, mgs, *zall),
+        [SMEM] + [VMEM] * (2 + NZ),
+        [pltpu.VMEM((512, 1280), BF)],
+        name="finish_latent",
+    )
+    gg = send(gtheirs, 1)
+    gm = call(add4_kernel, (sds((768, 256), BF),) * 4, (gmine, gg), [VMEM] * 2, name="add4g")
+    g1, g2, g3 = send(gm[1], 2), send(gm[2], 4), send(gm[3], 6)
+    gsum = (gm[0].astype(F32) + g1.astype(F32) + g2.astype(F32) + g3.astype(F32)).astype(BF)
+    byte_grads = pl.pallas_call(
+        bytes_kernel,
+        grid=(4,),
+        out_shape=sds((1024, 768), F32),
+        in_specs=[
+            pl.BlockSpec((256, 768), lambda b: (b, 0)),
+            pl.BlockSpec((1, 768), lambda b: (0, 0)),
+            pl.BlockSpec((768, 1536), lambda b: (0, 0)),
+            pl.BlockSpec((1536, 256), lambda b: (0, b)),
+        ],
+        out_specs=pl.BlockSpec((256, 768), lambda b: (b, 0)),
+        name="bytes",
+        cost_estimate=pl.CostEstimate(flops=2_400_000_000, bytes_accessed=10_000_000, transcendentals=0),
+    )(x, bg, wkv, dkvt)
+    zrel = (jnp.arange(NZ) ^ zi).astype(jnp.int32)
+    gquart = [lax.dynamic_slice_in_dim(gsum, zrel[r] * 192, 192, 0) for r in range(NZ)]
+    gz = (
+        gquart[0].astype(F32) + send_z(gquart[1], 1).astype(F32) + send_z(gquart[2], 2).astype(F32) + send_z(gquart[3], 3).astype(F32)
+    ).astype(BF)
+    gall = [gz, send_z(gz, 1), send_z(gz, 2), send_z(gz, 3)]
+    key_g, value_g, query_g, init_g, norm = call(
+        finish_kernel,
+        (sds((96, 256), F32), sds((96, 1280), F32), sds((160, 256), F32), sds((32, 1280), F32), sds((24, 256), F32)),
+        (meta, key_weight, value_weight, query_weight, wq_full, latent_init, qg, bgs, qgs, init_sum, mix, *gall),
+        [SMEM] + [VMEM] * (10 + NZ),
+        [pltpu.VMEM((768, 256), BF)],
+        name="finish",
+    )
+    norm_p, _ = gather_direct(norm)
+    byte_n, mixer_n, query_n = call(
+        norms_kernel,
+        (sds((8, 96), F32), sds((8, 160), F32), sds((8, 160), F32)),
+        (meta, *norm_p),
+        [SMEM] + [VMEM] * N,
+        name="norms",
+    )
+    return (
+        latents.reshape(seqs, own, DL),
+        byte_grads.reshape(seqs, rows, width),
+        init_g,
+        byte_n.reshape(-1),
+        query_n.reshape(-1),
+        mixer_n.reshape(-1),
+        query_g,
+        key_g,
+        value_g,
+        out_g,
+        up_g,
+        down_g,
+    )
+
+
 def solution(mesh):
+    fast = mesh.shape["fsdp"] == 8 and mesh.shape["rep"] == 4
+    device_fn = per_device_fast if fast else per_device_plain
     placed = (
         P("rep", "fsdp", None),
         P("fsdp", None),
@@ -266,7 +805,7 @@
         P("rep", "fsdp", None),
     )
     return jax.shard_map(
-        per_device,
+        device_fn,
         mesh=mesh,
         in_specs=placed,
         out_specs=(

time: 969 us -> 296 us (0.31)
  waiting for transfers between devices: 656 us -> 106 us
  blocking collectives: 115 us -> 0 us
  matrix products: 86.9 us -> 0 us
  starting transfers between devices: 1.11 us -> 79.8 us
  Pallas kernels: 0 us -> 73.6 us
  local copies, waits for them, and re-layouts: 70.2 us -> 23.1 us
  other arithmetic: 19.9 us -> 7.86 us
  between operations: 14.8 us -> 3.76 us
    reduce_scatter x6 -> x0, waiting for transfers between devices: 296 us -> none  [the longest x1 66.4 us: per_device(): lax.psum_scatter(down_local, 'fsdp', scatter_dimension=0, tiled=True)]
    while x12 -> x0, waiting for transfers between devices: 192 us -> none
    ppermute x0 -> x73, waiting for transfers between devices: none -> 106 us  [the longest x46 38.1 us: send(): return lax.ppermute(x, 'fsdp', [(i, i ^ k) for i in range(N)])]
    all_gather x4 -> x0, waiting for transfers between devices: 89.7 us -> none  [the longest x1 32 us: per_device(): lax.all_gather(down_weight, 'fsdp', axis=0, tiled=True)]
    dot_general x32 -> x0, matrix products: 86.9 us -> none  [the longest x2 8.92 us: backward_step(): jnp.einsum('hji,jhv->ihv', weights.astype(jnp.bfloat16), sum_heads, prefe...]
    ppermute x0 -> x73, starting transfers between devices: none -> 79.8 us  [the longest x12 31.5 us: send_z(): return lax.ppermute(x, 'rep', [(i, i ^ k) for i in range(NZ)])]
    psum x1 -> x0, waiting for transfers between devices: 75.8 us -> none  [per_device(): lax.psum((group_parts[0], group_parts[1], group_parts[2], group_parts[3],...]
    pallas_call x0 -> x11, Pallas kernels: none -> 73.6 us  [the longest x10 65.8 us: call(): pl.pallas_call(body, out_shape=out, in_specs=specs, out_specs=jax.tree.ma...]
  transfers between devices with their start and end apart: 17 -> 73, of which waited for: 16 -> 27; matrix products, arithmetic and copies ran while one was open for 9% -> 7% of each run, Pallas kernels for 0% -> 19%
where the time goes in v1:
time: 296 us; the launch traced here: 294 us
  waiting for transfers between devices  106 us (36%)
  starting transfers between devices  79.8 us (27%)
  Pallas kernels  73.6 us (25%)
  local copies, waits for them, and re-layouts  23.1 us (8%)
  other arithmetic  7.86 us (3%)
  between operations  3.76 us (1%)
    pallas_call x10, Pallas kernels, call(): pl.pallas_call(body, out_shape=out, in_specs=specs, out_specs=jax.tree.ma...  65.8 us
    ppermute x46, waiting for transfers between devices, send(): return lax.ppermute(x, 'fsdp', [(i, i ^ k) for i in range(N)])  38.1 us
    ppermute x15, waiting for transfers between devices, send_split(): lax.ppermute(x, 'fsdp', [(i, i ^ (odd if i & 1 else even)) for i in range...  35.5 us
    ppermute x12, waiting for transfers between devices, send_z(): return lax.ppermute(x, 'rep', [(i, i ^ k) for i in range(NZ)])  32 us
    ppermute x12, starting transfers between devices, send_z(): return lax.ppermute(x, 'rep', [(i, i ^ k) for i in range(NZ)])  31.5 us
    ppermute x46, starting transfers between devices, send(): return lax.ppermute(x, 'fsdp', [(i, i ^ k) for i in range(N)])  24.5 us
    ppermute x15, starting transfers between devices, send_split(): lax.ppermute(x, 'fsdp', [(i, i ^ (odd if i & 1 else even)) for i in range...  23.9 us
    pallas_call x1, Pallas kernels, per_device_fast(): pl.pallas_call(bytes_kernel, grid=(4,), out_shape=sds((1024, 768), F32),...  7.74 us
  transfers between devices with their start and end apart: 73, of which 27 were waited for; matrix products, arithmetic and copies ran while one was open for 7% of the time, Pallas kernels for 19%

profile of v1, /device:TPU:0, one launch (start us, length us, event | category | flops | bytes accessed | tf_op | source)
XLA Modules:
  0.0 293.7 jit_solution(14854365437382812798)
XLA Ops:
  2.5 3.0 %collective-permute-start.1 = (bf16[896,256]{1,0:T(8,128)(2,1)}, bf16[896,256]{1,0:T(8,128)(2,1)S(1)}, u32[]{:S(2)}, u32[]{:S(2)}) collective-permute-start(bf16[896,256]{1,0:T(8,128)(2,1)} %pack.1.refs_4_), channel_id=1, source_target_pairs={{0,2},{1,5},{2,0},{3,7},{4,6},{5,1},{6,4},{7,3},{8,10},{9,13},{10,... | collective-permute-start | bytes 1376264 | tf_op jit(solution)/shard_map/ppermute | solution.py:273
  9.6 5.4 %collective-permute-done.1.refs_6_ = bf16[896,256]{1,0:T(8,128)(2,1)S(1)} collective-permute-done((bf16[896,256]{1,0:T(8,128)(2,1)}, bf16[896,256]{1,0:T(8,128)(2,1)S(1)}, u32[]{:S(2)}, u32[]{:S(2)}) %collective-permute-start.1) | collective-permute-done | bytes 458784 | tf_op jit(solution)/shard_map/ppermute | solution.py:273
  14.9 2.4 collective-permute-start.3
  17.3 6.4 %collective-permute-done.12.refs_10_ = bf16[160,1280]{1,0:T(8,128)(2,1)S(1)} collective-permute-done((bf16[160,1280]{1,0:T(8,128)(2,1)}, bf16[160,1280]{1,0:T(8,128)(2,1)S(1)}, u32[]{:S(2)}, u32[]{:S(2)}) %collective-permute-start.12) | collective-permute-done | bytes 409632 | tf_op jit(solution)/shard_map/ppermute | solution.py:273
  26.1 6.4 %collective-permute-done.19.refs_18_ = bf16[160,1280]{1,0:T(8,128)(2,1)S(1)} collective-permute-done((bf16[160,1280]{1,0:T(8,128)(2,1)}, bf16[160,1280]{1,0:T(8,128)(2,1)S(1)}, u32[]{:S(2)}, u32[]{:S(2)}) %collective-permute-start.19) | collective-permute-done | bytes 409632 | tf_op jit(solution)/shard_map/ppermute | solution.py:273
  34.9 6.4 %collective-permute-done.26.refs_26_ = bf16[160,1280]{1,0:T(8,128)(2,1)S(1)} collective-permute-done((bf16[160,1280]{1,0:T(8,128)(2,1)}, bf16[160,1280]{1,0:T(8,128)(2,1)S(1)}, u32[]{:S(2)}, u32[]{:S(2)}) %collective-permute-start.26) | collective-permute-done | bytes 409632 | tf_op jit(solution)/shard_map/ppermute | solution.py:273
  41.3 2.4 collective-permute-start.27
  44.8 5.0 %collective-permute-done.27.refs_27_ = bf16[160,1280]{1,0:T(8,128)(2,1)S(1)} collective-permute-done((bf16[160,1280]{1,0:T(8,128)(2,1)}, bf16[160,1280]{1,0:T(8,128)(2,1)S(1)}, u32[]{:S(2)}, u32[]{:S(2)}) %collective-permute-start.27) | collective-permute-done | bytes 409632 | tf_op jit(solution)/shard_map/ppermute | solution.py:273
  59.0 16.2 %forward.1 = (bf16[1024,768]{1,0:T(8,128)(2,1)}, bf16[1024,256]{1,0:T(8,128)(2,1)}, bf16[1280,1024]{1,0:T(8,128)(2,1)}, bf16[768,1536]{1,0:T(8,128)(2,1)}, bf16[...) custom-call(s32[4]{0:T(128)} %pad_add_fusion.refs_0_.meta, ...), custom_call_target="tpu_custom_call" | custom-call | flops 8000000000 | bytes 12000000 | tf_op jit(solution)/shard_map/forward/pallas_call | solution.py:307
  87.4 4.5 %collective-permute-done.10.refs_4_ = bf16[64,1408]{1,0:T(8,128)(2,1)S(1)} collective-permute-done((bf16[64,1408]{1,0:T(8,128)(2,1)}, bf16[64,1408]{1,0:T(8,128)(2,1)S(1)}, u32[]{:S(2)}, u32[]{:S(2)}) %collective-permute-start.10) | collective-permute-done | bytes 180256 | tf_op jit(solution)/shard_map/ppermute | solution.py:269
  91.9 2.5 collective-permute-done.8.refs_2_
  95.7 11.3 %latent.1 = (bf16[64,1280]{1,0:T(8,128)(2,1)}, bf16[3,64,1280]{2,1,0:T(8,128)(2,1)}, bf16[4,3,64,160]{3,2,1,0:T(8,128)(2,1)}, bf16[4,3,64,160]{3,2,1,0:T(8,128)(...) custom-call(s32[4]{0:T(128)} %pad_add_fusion.refs_0_.meta, bf16[64,1408]{1,0:T(8,128)(2,1)} %get-tuple-element.57.refs_1_, ...), custom_call_target="tpu_custom_call" | custom-call | flops 5000000000 | bytes 12000000 | tf_op jit(solution)/shard_map/latent/pallas_call | solution.py:307
  118.9 3.9 %collective-permute-done.35.refs_10_ = bf16[64,1408]{1,0:T(8,128)(2,1)S(1)} collective-permute-done((bf16[64,1408]{1,0:T(8,128)(2,1)}, bf16[64,1408]{1,0:T(8,128)(2,1)S(1)}, u32[]{:S(2)}, u32[]{:S(2)}) %collective-permute-start.35) | collective-permute-done | bytes 180256 | tf_op jit(solution)/shard_map/ppermute | solution.py:269
  125.5 18.9 %backward.1 = (bf16[1536,1024]{1,0:T(8,128)(2,1)}, bf16[4,768,256]{2,1,0:T(8,128)(2,1)}, bf16[4,768,256]{2,1,0:T(8,128)(2,1)}) custom-call(s32[4]{0:T(128)} %pad_add_fusion.refs_0_.meta, bf16[1024,256]{1,0:T(8,128)(2,1)} %get-tuple-element.63.refs_1_, bf16[1280,1024]{1,0:T(8,128)(2,1)} %get-tuple-element.64.refs_2_, ...), custom_call_target="tpu_custom_call" | custom-call | flops 10000000000 | bytes 12000000 | tf_op jit(solution)/shard_map/backward/pallas_call | solution.py:307
  149.0 4.8 %collective-permute-done.49 = bf16[2,3,64,160]{3,2,1,0:T(8,128)(2,1)S(1)} collective-permute-done((bf16[2,3,64,160]{3,2,1,0:T(8,128)(2,1)S(1)}, bf16[2,3,64,160]{3,2,1,0:T(8,128)(2,1)S(1)}, u32[]{:S(2)}, u32[]{:S(2)}) %collective-permute-start.49) | collective-permute-done | bytes 122912 | tf_op jit(solution)/shard_map/ppermute | solution.py:269
  156.0 3.9 %collective-permute-done.48 = bf16[2,3,64,160]{3,2,1,0:T(8,128)(2,1)S(1)} collective-permute-done((bf16[2,3,64,160]{3,2,1,0:T(8,128)(2,1)S(1)}, bf16[2,3,64,160]{3,2,1,0:T(8,128)(2,1)S(1)}, u32[]{:S(2)}, u32[]{:S(2)}) %collective-permute-start.48) | collective-permute-done | bytes 122912 | tf_op jit(solution)/shard_map/ppermute | solution.py:269
  162.5 3.1 %collective-permute-done.47 = bf16[2,3,64,160]{3,2,1,0:T(8,128)(2,1)S(1)} collective-permute-done((bf16[2,3,64,160]{3,2,1,0:T(8,128)(2,1)S(1)}, bf16[2,3,64,160]{3,2,1,0:T(8,128)(2,1)S(1)}, u32[]{:S(2)}, u32[]{:S(2)}) %collective-permute-start.47) | collective-permute-done | bytes 122912 | tf_op jit(solution)/shard_map/ppermute | solution.py:269
  169.4 5.9 %collective-permute-done.44.rest_6_ = bf16[3,64,1280]{2,1,0:T(8,128)(2,1)} collective-permute-done((bf16[3,64,1280]{2,1,0:T(8,128)(2,1)S(1)}, bf16[3,64,1280]{2,1,0:T(8,128)(2,1)}, u32[]{:S(2)}, u32[]{:S(2)}) %collective-permute-start.44) | collective-permute-done | bytes 491552 | tf_op jit(solution)/shard_map/ppermute | solution.py:273
  176.5 3.2 %add4g.1 = (bf16[768,256]{1,0:T(8,128)(2,1)}, bf16[768,256]{1,0:T(8,128)(2,1)}, bf16[768,256]{1,0:T(8,128)(2,1)}, bf16[768,256]{1,0:T(8,128)(2,1)}) custom-call(bf16[4,768,256]{2,1,0:T(8,128)(2,1)} %get-tuple-element.81.a, bf16[4,768,256]{2,1,0:T(8,128)(2,1)} %copy-done), custom_call_target="tpu_custom_call" | custom-call | tf_op jit(solution)/shard_map/add4g/pallas_call | solution.py:307
  186.2 4.4 %latent_grads.1 = (bf16[128,1280]{1,0:T(8,128)(2,1)}, bf16[128,1280]{1,0:T(8,128)(2,1)}, bf16[128,1280]{1,0:T(8,128)(2,1)}, bf16[128,1280]{1,0:T(8,128)(2,1)}) custom-call(s32[4]{0:T(128)} %pad_add_fusion.refs_0_.meta, f32[32,1280]{1,0:T(8,128)} %get-tuple-element.71.init, bf16[3,64,1280]{2,1,0:T(8,128)(2,1)} %get-tuple-element.72.rest_0_, ...), custom_call_target="tpu_custom_call" | custom-call | flops 1000000000 | bytes 6000000 | tf_op jit(solution)/shard_map/latent_grads/pallas_call | solution.py:307
  192.2 2.6 collective-permute-start.51
  195.4 5.9 %collective-permute-done.58 = bf16[768,256]{1,0:T(8,128)(2,1)S(1)} collective-permute-done((bf16[768,256]{1,0:T(8,128)(2,1)}, bf16[768,256]{1,0:T(8,128)(2,1)S(1)}, u32[]{:S(2)}, u32[]{:S(2)}) %collective-permute-start.58) | collective-permute-done | bytes 393248 | tf_op jit(solution)/shard_map/ppermute | solution.py:269
  203.3 2.6 collective-permute-start.61
  207.6 4.0 %collective-permute-start.62 = (bf16[192,256]{1,0:T(8,128)(2,1)S(1)}, bf16[192,256]{1,0:T(8,128)(2,1)S(1)}, u32[]{:S(2)}, u32[]{:S(2)}) collective-permute-start(bf16[192,256]{1,0:T(8,128)(2,1)S(1)} %get-tuple-element.103), channel_id=1, source_target_pairs={{0,24},{8,16},{16,8},{24,0},{1,25},{9,17},{17,9},{25,1},{2,26},{10... | collective-permute-start | bytes 294920 | tf_op jit(solution)/shard_map/ppermute | solution.py:277
  211.7 6.8 %collective-permute-done.51 = bf16[128,1280]{1,0:T(8,128)(2,1)S(1)} collective-permute-done((bf16[128,1280]{1,0:T(8,128)(2,1)}, bf16[128,1280]{1,0:T(8,128)(2,1)S(1)}, u32[]{:S(2)}, u32[]{:S(2)}) %collective-permute-start.51) | collective-permute-done | bytes 327712 | tf_op jit(solution)/shard_map/ppermute | solution.py:277
  218.6 11.3 %collective-permute-start.53 = (bf16[128,1280]{1,0:T(8,128)(2,1)S(1)}, bf16[128,1280]{1,0:T(8,128)(2,1)S(1)}, u32[]{:S(2)}, u32[]{:S(2)}) collective-permute-start(bf16[128,1280]{1,0:T(8,128)(2,1)S(1)} %add_convert_fusion.1.rest_0_), channel_id=1, source_target_pairs={{0,8},{8,0},{16,24},{24,16},{1,9},{9,1},{17,25},{25,17},{2,10},{10... | collective-permute-start | bytes 983048 | tf_op jit(solution)/shard_map/ppermute | solution.py:277
  238.2 4.4 %collective-permute-done.53.rest_1_ = bf16[128,1280]{1,0:T(8,128)(2,1)S(1)} collective-permute-done((bf16[128,1280]{1,0:T(8,128)(2,1)S(1)}, bf16[128,1280]{1,0:T(8,128)(2,1)S(1)}, u32[]{:S(2)}, u32[]{:S(2)}) %collective-permute-start.53) | collective-permute-done | bytes 327712 | tf_op jit(solution)/shard_map/ppermute | solution.py:277
  245.3 15.4 %collective-permute-done.54.rest_2_ = bf16[128,1280]{1,0:T(8,128)(2,1)S(1)} collective-permute-done((bf16[128,1280]{1,0:T(8,128)(2,1)S(1)}, bf16[128,1280]{1,0:T(8,128)(2,1)S(1)}, u32[]{:S(2)}, u32[]{:S(2)}) %collective-permute-start.54) | collective-permute-done | bytes 327712 | tf_op jit(solution)/shard_map/ppermute | solution.py:277
  261.7 3.4 %finish_latent.1 = (f32[160,1280]{1,0:T(8,128)}, f32[160,1280]{1,0:T(8,128)}, f32[160,1280]{1,0:T(8,128)}, f32[32,1280]{1,0:T(8,128)}, f32[8,160]{1,0:T(8,128)}) custom-call(s32[4]{0:T(128)} %pad_add_fusion.refs_0_.meta, bf16[160,1280]{1,0:T(8,128)(2,1)} %wup.1, f32[1,160]{1,0:T(1,128)} %bitcast.34, bf16[128,1280]{1,0:T(8,128)(2,1)} %copy-done.1, ...), custom_call_target="tpu_custom_call" | custom-call | tf_op jit(solution)/shard_map/finish_latent/pallas_call | solution.py:307
  265.1 3.6 %collective-permute-done.64.rest_2_ = bf16[192,256]{1,0:T(8,128)(2,1)S(1)} collective-permute-done((bf16[192,256]{1,0:T(8,128)(2,1)S(1)}, bf16[192,256]{1,0:T(8,128)(2,1)S(1)}, u32[]{:S(2)}, u32[]{:S(2)}) %collective-permute-start.64) | collective-permute-done | bytes 98336 | tf_op jit(solution)/shard_map/ppermute | solution.py:277
  269.4 3.0 %finish.1 = (f32[96,256]{1,0:T(8,128)}, f32[96,1280]{1,0:T(8,128)}, f32[160,256]{1,0:T(8,128)}, f32[32,1280]{1,0:T(8,128)}, f32[24,256]{1,0:T(8,128)}) custom-call(s32[4]{0:T(128)} %pad_add_fusion.refs_0_.meta, bf16[96,256]{1,0:T(8,128)(2,1)} %wk.3, bf16[96,1280]{1,0:T(8,128)(2,1)} %wv.3, bf16[160,256]{1,0:T(8,128)(2,1)} %wq.3, ...), custom_call_target="tpu_custom_call" | custom-call | tf_op jit(solution)/shard_map/finish/pallas_call | solution.py:307
  279.1 7.7 %bytes.1 = f32[1024,768]{1,0:T(8,128)} custom-call(bf16[1024,768]{1,0:T(8,128)(2,1)} %bitcast.32, f32[1,768]{1,0:T(1,128)} %reshape.72.refs_2_.bg, bf16[768,1536]{1,0:T(8,128)(2,1)} %get-tuple-element.62.wkv, bf16[1536,1024]{1,0:T(8,128)(2,1)} %get-tuple-element.69.dkvt), custom_call_target="tpu_custom_call" | custom-call | flops 2400000000 | bytes 10000000 | tf_op jit(solution)/shard_map/bytes/pallas_call | solution.py:737
  (253 shorter events, 99.5 us)
Async XLA Ops:
  5.5 18.2 %collective-permute-start.12 = (bf16[160,1280]{1,0:T(8,128)(2,1)}, bf16[160,1280]{1,0:T(8,128)(2,1)S(1)}, u32[]{:S(2)}, u32[]{:S(2)}) collective-permute-start(bf16[160,1280]{1,0:T(8,128)(2,1)} %refs_8_.1), channel_id=1, source_target_pairs={{0,2},{1,5},{2,0},{3,7},{4,6},{5,1},{6,4},{7,3},{8,10},{9,13},{10,... | collective-permute-start | bytes 1228808 | tf_op jit(solution)/shard_map/ppermute | solution.py:273
  5.5 27.0 %collective-permute-start.19 = (bf16[160,1280]{1,0:T(8,128)(2,1)}, bf16[160,1280]{1,0:T(8,128)(2,1)S(1)}, u32[]{:S(2)}, u32[]{:S(2)}) collective-permute-start(bf16[160,1280]{1,0:T(8,128)(2,1)} %wup.1), channel_id=1, source_target_pairs={{0,2},{1,5},{2,0},{3,7},{4,6},{5,1},{6,4},{7,3},{8,10},{9,13},{10,... | collective-permute-start | bytes 1228808 | tf_op jit(solution)/shard_map/ppermute | solution.py:273
  7.5 33.8 %collective-permute-start.26 = (bf16[160,1280]{1,0:T(8,128)(2,1)}, bf16[160,1280]{1,0:T(8,128)(2,1)S(1)}, u32[]{:S(2)}, u32[]{:S(2)}) collective-permute-start(bf16[160,1280]{1,0:T(8,128)(2,1)} %refs_24_.1), channel_id=1, source_target_pairs={{0,2},{1,5},{2,0},{3,7},{4,6},{5,1},{6,4},{7,3},{8,10},{9,13},{10,... | collective-permute-start | bytes 1228808 | tf_op jit(solution)/shard_map/ppermute | solution.py:273
  7.5 36.6 %collective-permute-start.2 = (bf16[896,256]{1,0:T(8,128)(2,1)}, bf16[896,256]{1,0:T(8,128)(2,1)S(1)}, u32[]{:S(2)}, u32[]{:S(2)}) collective-permute-start(bf16[896,256]{1,0:T(8,128)(2,1)} %pack.1.refs_4_), channel_id=1, source_target_pairs={{0,4},{1,3},{2,6},{3,1},{4,0},{5,7},{6,2},{7,5},{8,12},{9,11},{10,... | collective-permute-start | bytes 1376264 | tf_op jit(solution)/shard_map/ppermute | solution.py:273
  14.9 29.3 %collective-permute-start.3 = (bf16[896,256]{1,0:T(8,128)(2,1)S(1)}, bf16[896,256]{1,0:T(8,128)(2,1)S(1)}, u32[]{:S(2)}, u32[]{:S(2)}) collective-permute-start(bf16[896,256]{1,0:T(8,128)(2,1)S(1)} %collective-permute-done.1.refs_6_), channel_id=1, source_target_pairs={{0,4},{1,3},{2,6},{3,1},{4,0},{5,7},{6,2},{7,5},{8,12},{9,11},{10,... | collective-permute-start | bytes 1376264 | tf_op jit(solution)/shard_map/ppermute | solution.py:273
  23.7 19.9 %collective-permute-start.13 = (bf16[160,1280]{1,0:T(8,128)(2,1)}, bf16[160,1280]{1,0:T(8,128)(2,1)S(1)}, u32[]{:S(2)}, u32[]{:S(2)}) collective-permute-start(bf16[160,1280]{1,0:T(8,128)(2,1)} %refs_8_.1), channel_id=1, source_target_pairs={{0,4},{1,3},{2,6},{3,1},{4,0},{5,7},{6,2},{7,5},{8,12},{9,11},{10,... | collective-permute-start | bytes 1228808 | tf_op jit(solution)/shard_map/ppermute | solution.py:273
  54.4 20.8 %collective-permute-start.18 = (bf16[160,1280]{1,0:T(8,128)(2,1)}, bf16[160,1280]{1,0:T(8,128)(2,1)}, u32[]{:S(2)}, u32[]{:S(2)}) collective-permute-start(bf16[160,1280]{1,0:T(8,128)(2,1)} %wup.1), channel_id=1, source_target_pairs={{0,1},{1,0},{2,3},{3,2},{4,5},{5,4},{6,7},{7,6},{8,9},{9,8},{10,11... | collective-permute-start | bytes 1228808 | tf_op jit(solution)/shard_map/ppermute | solution.py:269
  54.4 20.9 %collective-permute-start.25 = (bf16[160,1280]{1,0:T(8,128)(2,1)}, bf16[160,1280]{1,0:T(8,128)(2,1)}, u32[]{:S(2)}, u32[]{:S(2)}) collective-permute-start(bf16[160,1280]{1,0:T(8,128)(2,1)} %refs_24_.1), channel_id=1, source_target_pairs={{0,1},{1,0},{2,3},{3,2},{4,5},{5,4},{6,7},{7,6},{8,9},{9,8},{10,11... | collective-permute-start | bytes 1228808 | tf_op jit(solution)/shard_map/ppermute | solution.py:269
  54.9 20.9 %collective-permute-start.14 = (bf16[160,1280]{1,0:T(8,128)(2,1)}, bf16[160,1280]{1,0:T(8,128)(2,1)}, u32[]{:S(2)}, u32[]{:S(2)}) collective-permute-start(bf16[160,1280]{1,0:T(8,128)(2,1)} %copy-done.29), channel_id=1, source_target_pairs={{0,4},{1,3},{2,6},{3,1},{4,0},{5,7},{6,2},{7,5},{8,12},{9,11},{10,... | collective-permute-start | bytes 1228808 | tf_op jit(solution)/shard_map/ppermute | solution.py:273
  56.9 18.9 %collective-permute-start.21 = (bf16[160,1280]{1,0:T(8,128)(2,1)}, bf16[160,1280]{1,0:T(8,128)(2,1)}, u32[]{:S(2)}, u32[]{:S(2)}) collective-permute-start(bf16[160,1280]{1,0:T(8,128)(2,1)} %copy-done.30), channel_id=1, source_target_pairs={{0,4},{1,3},{2,6},{3,1},{4,0},{5,7},{6,2},{7,5},{8,12},{9,11},{10,... | collective-permute-start | bytes 1228808 | tf_op jit(solution)/shard_map/ppermute | solution.py:273
  57.0 19.3 %collective-permute-start.28 = (bf16[160,1280]{1,0:T(8,128)(2,1)}, bf16[160,1280]{1,0:T(8,128)(2,1)}, u32[]{:S(2)}, u32[]{:S(2)}) collective-permute-start(bf16[160,1280]{1,0:T(8,128)(2,1)} %copy-done.31), channel_id=1, source_target_pairs={{0,4},{1,3},{2,6},{3,1},{4,0},{5,7},{6,2},{7,5},{8,12},{9,11},{10,... | collective-permute-start | bytes 1228808 | tf_op jit(solution)/shard_map/ppermute | solution.py:273
  107.0 16.2 %collective-permute-start.46 = (bf16[4,3,64,160]{3,2,1,0:T(8,128)(2,1)}, bf16[4,3,64,160]{3,2,1,0:T(8,128)(2,1)S(1)}, u32[]{:S(2)}, u32[]{:S(2)}) collective-permute-start(bf16[4,3,64,160]{3,2,1,0:T(8,128)(2,1)} %get-tuple-element.74), channel_id=1, source_target_pairs={{0,1},{1,0},{2,3},{3,2},{4,5},{5,4},{6,7},{7,6},{8,9},{9,8},{10,11... | collective-permute-start | bytes 737288 | tf_op jit(solution)/shard_map/ppermute | solution.py:269
  117.4 48.9 %collective-permute-start.41 = (bf16[3,64,1280]{2,1,0:T(8,128)(2,1)}, bf16[3,64,1280]{2,1,0:T(8,128)(2,1)S(1)}, u32[]{:S(2)}, u32[]{:S(2)}) collective-permute-start(bf16[3,64,1280]{2,1,0:T(8,128)(2,1)} %get-tuple-element.72.rest_0_), channel_id=1, source_target_pairs={{0,2},{1,5},{2,0},{3,7},{4,6},{5,1},{6,4},{7,3},{8,10},{9,13},{10,... | collective-permute-start | bytes 1474568 | tf_op jit(solution)/shard_map/ppermute | solution.py:273
  124.1 43.6 %collective-permute-start.40 = (bf16[3,64,1280]{2,1,0:T(8,128)(2,1)S(1)}, bf16[3,64,1280]{2,1,0:T(8,128)(2,1)S(1)}, u32[]{:S(2)}, u32[]{:S(2)}) collective-permute-start(bf16[3,64,1280]{2,1,0:T(8,128)(2,1)S(1)} %copy-done.3), channel_id=1, source_target_pairs={{0,4},{1,3},{2,6},{3,1},{4,0},{5,7},{6,2},{7,5},{8,12},{9,11},{10,... | collective-permute-start | bytes 1474568 | tf_op jit(solution)/shard_map/ppermute | solution.py:273
  124.6 60.8 %collective-permute-start.39 = (bf16[3,64,1280]{2,1,0:T(8,128)(2,1)S(1)}, bf16[3,64,1280]{2,1,0:T(8,128)(2,1)S(1)}, u32[]{:S(2)}, u32[]{:S(2)}) collective-permute-start(bf16[3,64,1280]{2,1,0:T(8,128)(2,1)S(1)} %copy-done.3), channel_id=1, source_target_pairs={{0,1},{1,0},{2,3},{3,2},{4,5},{5,4},{6,7},{7,6},{8,9},{9,8},{10,11... | collective-permute-start | bytes 1474568 | tf_op jit(solution)/shard_map/ppermute | solution.py:269
  144.4 30.9 %collective-permute-start.56 = (bf16[4,768,256]{2,1,0:T(8,128)(2,1)}, bf16[4,768,256]{2,1,0:T(8,128)(2,1)S(1)}, u32[]{:S(2)}, u32[]{:S(2)}) collective-permute-start(bf16[4,768,256]{2,1,0:T(8,128)(2,1)} %get-tuple-element.82), channel_id=1, source_target_pairs={{0,1},{1,0},{2,3},{3,2},{4,5},{5,4},{6,7},{7,6},{8,9},{9,8},{10,11... | collective-permute-start | bytes 4718600 | tf_op jit(solution)/shard_map/ppermute | solution.py:269
  166.3 15.1 %collective-permute-start.42 = (bf16[3,64,1280]{2,1,0:T(8,128)(2,1)S(1)}, bf16[3,64,1280]{2,1,0:T(8,128)(2,1)}, u32[]{:S(2)}, u32[]{:S(2)}) collective-permute-start(bf16[3,64,1280]{2,1,0:T(8,128)(2,1)S(1)} %collective-permute-done.41), channel_id=1, source_target_pairs={{0,1},{1,0},{2,3},{3,2},{4,5},{5,4},{6,7},{7,6},{8,9},{9,8},{10,11... | collective-permute-start | bytes 1474568 | tf_op jit(solution)/shard_map/ppermute | solution.py:269
  179.6 15.1 %collective-permute-start.57 = (bf16[768,256]{1,0:T(8,128)(2,1)}, bf16[768,256]{1,0:T(8,128)(2,1)S(1)}, u32[]{:S(2)}, u32[]{:S(2)}) collective-permute-start(bf16[768,256]{1,0:T(8,128)(2,1)} %get-tuple-element.84), channel_id=1, source_target_pairs={{0,2},{1,3},{2,0},{3,1},{4,6},{5,7},{6,4},{7,5},{8,10},{9,11},{10,... | collective-permute-start | bytes 1179656 | tf_op jit(solution)/shard_map/ppermute | solution.py:269
  181.5 19.9 %collective-permute-start.58 = (bf16[768,256]{1,0:T(8,128)(2,1)}, bf16[768,256]{1,0:T(8,128)(2,1)S(1)}, u32[]{:S(2)}, u32[]{:S(2)}) collective-permute-start(bf16[768,256]{1,0:T(8,128)(2,1)} %get-tuple-element.85), channel_id=1, source_target_pairs={{0,4},{1,5},{2,6},{3,7},{4,0},{5,1},{6,2},{7,3},{8,12},{9,13},{10,... | collective-permute-start | bytes 1179656 | tf_op jit(solution)/shard_map/ppermute | solution.py:269
  181.8 19.5 %collective-permute-start.59 = (bf16[768,256]{1,0:T(8,128)(2,1)}, bf16[768,256]{1,0:T(8,128)(2,1)S(1)}, u32[]{:S(2)}, u32[]{:S(2)}) collective-permute-start(bf16[768,256]{1,0:T(8,128)(2,1)} %get-tuple-element.86), channel_id=1, source_target_pairs={{0,6},{1,7},{2,4},{3,5},{4,2},{5,3},{6,0},{7,1},{8,14},{9,15},{10,... | collective-permute-start | bytes 1179656 | tf_op jit(solution)/shard_map/ppermute | solution.py:269
  190.5 17.1 %collective-permute-start.50 = (bf16[128,1280]{1,0:T(8,128)(2,1)}, bf16[128,1280]{1,0:T(8,128)(2,1)S(1)}, u32[]{:S(2)}, u32[]{:S(2)}) collective-permute-start(bf16[128,1280]{1,0:T(8,128)(2,1)} %get-tuple-element.76), channel_id=1, source_target_pairs={{0,8},{8,0},{16,24},{24,16},{1,9},{9,1},{17,25},{25,17},{2,10},{10... | collective-permute-start | bytes 983048 | tf_op jit(solution)/shard_map/ppermute | solution.py:277
  192.2 26.3 %collective-permute-start.51 = (bf16[128,1280]{1,0:T(8,128)(2,1)}, bf16[128,1280]{1,0:T(8,128)(2,1)S(1)}, u32[]{:S(2)}, u32[]{:S(2)}) collective-permute-start(bf16[128,1280]{1,0:T(8,128)(2,1)} %get-tuple-element.77), channel_id=1, source_target_pairs={{0,16},{8,24},{16,0},{24,8},{1,17},{9,25},{17,1},{25,9},{2,18},{10... | collective-permute-start | bytes 983048 | tf_op jit(solution)/shard_map/ppermute | solution.py:277
  194.8 23.7 %collective-permute-start.52 = (bf16[128,1280]{1,0:T(8,128)(2,1)}, bf16[128,1280]{1,0:T(8,128)(2,1)S(1)}, u32[]{:S(2)}, u32[]{:S(2)}) collective-permute-start(bf16[128,1280]{1,0:T(8,128)(2,1)} %get-tuple-element.78), channel_id=1, source_target_pairs={{0,24},{8,16},{16,8},{24,0},{1,25},{9,17},{17,9},{25,1},{2,26},{10... | collective-permute-start | bytes 983048 | tf_op jit(solution)/shard_map/ppermute | solution.py:277
  201.6 32.1 %collective-permute-start.60 = (bf16[192,256]{1,0:T(8,128)(2,1)S(1)}, bf16[192,256]{1,0:T(8,128)(2,1)S(1)}, u32[]{:S(2)}, u32[]{:S(2)}) collective-permute-start(bf16[192,256]{1,0:T(8,128)(2,1)S(1)} %get-tuple-element.102), channel_id=1, source_target_pairs={{0,8},{8,0},{16,24},{24,16},{1,9},{9,1},{17,25},{25,17},{2,10},{10... | collective-permute-start | bytes 294920 | tf_op jit(solution)/shard_map/ppermute | solution.py:277
  203.3 31.9 %collective-permute-start.61 = (bf16[192,256]{1,0:T(8,128)(2,1)S(1)}, bf16[192,256]{1,0:T(8,128)(2,1)S(1)}, u32[]{:S(2)}, u32[]{:S(2)}) collective-permute-start(bf16[192,256]{1,0:T(8,128)(2,1)S(1)} %get-tuple-element.104), channel_id=1, source_target_pairs={{0,16},{8,24},{16,0},{24,8},{1,17},{9,25},{17,1},{25,9},{2,18},{10... | collective-permute-start | bytes 294920 | tf_op jit(solution)/shard_map/ppermute | solution.py:277
  207.6 27.5 %collective-permute-start.62 = (bf16[192,256]{1,0:T(8,128)(2,1)S(1)}, bf16[192,256]{1,0:T(8,128)(2,1)S(1)}, u32[]{:S(2)}, u32[]{:S(2)}) collective-permute-start(bf16[192,256]{1,0:T(8,128)(2,1)S(1)} %get-tuple-element.103), channel_id=1, source_target_pairs={{0,24},{8,16},{16,8},{24,0},{1,25},{9,17},{17,9},{25,1},{2,26},{10... | collective-permute-start | bytes 294920 | tf_op jit(solution)/shard_map/ppermute | solution.py:277
  218.6 23.9 %collective-permute-start.53 = (bf16[128,1280]{1,0:T(8,128)(2,1)S(1)}, bf16[128,1280]{1,0:T(8,128)(2,1)S(1)}, u32[]{:S(2)}, u32[]{:S(2)}) collective-permute-start(bf16[128,1280]{1,0:T(8,128)(2,1)S(1)} %add_convert_fusion.1.rest_0_), channel_id=1, source_target_pairs={{0,8},{8,0},{16,24},{24,16},{1,9},{9,1},{17,25},{25,17},{2,10},{10... | collective-permute-start | bytes 983048 | tf_op jit(solution)/shard_map/ppermute | solution.py:277
  232.6 28.1 %collective-permute-start.54 = (bf16[128,1280]{1,0:T(8,128)(2,1)S(1)}, bf16[128,1280]{1,0:T(8,128)(2,1)S(1)}, u32[]{:S(2)}, u32[]{:S(2)}) collective-permute-start(bf16[128,1280]{1,0:T(8,128)(2,1)S(1)} %add_convert_fusion.1.rest_0_), channel_id=1, source_target_pairs={{0,16},{8,24},{16,0},{24,8},{1,17},{9,25},{17,1},{25,9},{2,18},{10... | collective-permute-start | bytes 983048 | tf_op jit(solution)/shard_map/ppermute | solution.py:277
  233.7 27.1 %collective-permute-start.55 = (bf16[128,1280]{1,0:T(8,128)(2,1)S(1)}, bf16[128,1280]{1,0:T(8,128)(2,1)S(1)}, u32[]{:S(2)}, u32[]{:S(2)}) collective-permute-start(bf16[128,1280]{1,0:T(8,128)(2,1)S(1)} %add_convert_fusion.1.rest_0_), channel_id=1, source_target_pairs={{0,24},{8,16},{16,8},{24,0},{1,25},{9,17},{17,9},{25,1},{2,26},{10... | collective-permute-start | bytes 983048 | tf_op jit(solution)/shard_map/ppermute | solution.py:277
  235.2 29.9 %collective-permute-start.63 = (bf16[192,256]{1,0:T(8,128)(2,1)S(1)}, bf16[192,256]{1,0:T(8,128)(2,1)S(1)}, u32[]{:S(2)}, u32[]{:S(2)}) collective-permute-start(bf16[192,256]{1,0:T(8,128)(2,1)S(1)} %add_convert_fusion.2.rest_0_), channel_id=1, source_target_pairs={{0,8},{8,0},{16,24},{24,16},{1,9},{9,1},{17,25},{25,17},{2,10},{10... | collective-permute-start | bytes 294920 | tf_op jit(solution)/shard_map/ppermute | solution.py:277
  236.2 32.5 %collective-permute-start.64 = (bf16[192,256]{1,0:T(8,128)(2,1)S(1)}, bf16[192,256]{1,0:T(8,128)(2,1)S(1)}, u32[]{:S(2)}, u32[]{:S(2)}) collective-permute-start(bf16[192,256]{1,0:T(8,128)(2,1)S(1)} %add_convert_fusion.2.rest_0_), channel_id=1, source_target_pairs={{0,16},{8,24},{16,0},{24,8},{1,17},{9,25},{17,1},{25,9},{2,18},{10... | collective-permute-start | bytes 294920 | tf_op jit(solution)/shard_map/ppermute | solution.py:277
  242.6 26.1 %collective-permute-start.65 = (bf16[192,256]{1,0:T(8,128)(2,1)S(1)}, bf16[192,256]{1,0:T(8,128)(2,1)S(1)}, u32[]{:S(2)}, u32[]{:S(2)}) collective-permute-start(bf16[192,256]{1,0:T(8,128)(2,1)S(1)} %add_convert_fusion.2.rest_0_), channel_id=1, source_target_pairs={{0,24},{8,16},{16,8},{24,0},{1,25},{9,17},{17,9},{25,1},{2,26},{10... | collective-permute-start | bytes 294920 | tf_op jit(solution)/shard_map/ppermute | solution.py:277
  (92 other events, 778.6 us)

commit v2 on v0

--- a/solution.py
+++ b/solution.py
@@ -1,6 +1,8 @@
 import jax
 import jax.numpy as jnp
 from jax import lax
+from jax.experimental import pallas as pl
+from jax.experimental.pallas import tpu as pltpu
 from jax.sharding import PartitionSpec as P
 
 DL = 1280
@@ -28,7 +30,7 @@
     return inverse * (scaled - mean_one - normal * mean_two)
 
 
-def per_device(
+def per_device_plain(
     byte_feats,
     latent_init,
     prefix,
@@ -249,7 +251,713 @@
     )
 
 
+BF = jnp.bfloat16
+F32 = jnp.float32
+N = 8
+NZ = 4
+COST = pl.CostEstimate(flops=100_000_000_000, bytes_accessed=1024, transcendentals=0)
+LOG2E = 1.4426950408889634
+ANY = pl.BlockSpec(memory_space=pl.ANY)
+VMEM = pl.BlockSpec(memory_space=pltpu.VMEM)
+SMEM = pl.BlockSpec(memory_space=pltpu.SMEM)
+
+
+def dot(a, b, ca, cb):
+    return lax.dot_general(a, b, (((ca,), (cb,)), ((), ())), preferred_element_type=F32)
+
+
+def send(x, k):
+    return lax.ppermute(x, "fsdp", [(i, i ^ k) for i in range(N)])
+
+
+def send_split(x, even, odd):
+    return lax.ppermute(x, "fsdp", [(i, i ^ (odd if i & 1 else even)) for i in range(N)])
+
+
+def send_z(x, k):
+    return lax.ppermute(x, "rep", [(i, i ^ k) for i in range(NZ)])
+
+
+def after(x, *deps):
+    return lax.optimization_barrier((x, *deps))[0]
+
+
+def me_z():
+    return lax.axis_index("fsdp"), lax.axis_index("rep")
+
+
+def owner(me, rel):
+    even, odd = rel
+    if even == odd:
+        return me ^ even
+    return me ^ jnp.where((me & 1) == 0, even, odd)
+
+
+def call(body, out, ins, specs, scratch=(), name=None, grid=(), deps=(), out_specs=None, aliases=None):
+    n, skip = len(ins), len(deps)
+
+    def run(*refs):
+        return body(*refs[:n], *refs[n + skip :])
+
+    return pl.pallas_call(
+        run,
+        grid=grid,
+        out_shape=out,
+        in_specs=list(specs) + [ANY] * skip,
+        out_specs=jax.tree.map(lambda _: VMEM, out) if out_specs is None else out_specs,
+        scratch_shapes=list(scratch),
+        input_output_aliases=aliases or {},
+        name=name,
+        cost_estimate=COST,
+    )(*ins, *deps)
+
+
+def sds(shape, dtype):
+    return jax.ShapeDtypeStruct(shape, dtype)
+
+
+def ln_parts(v):
+    centered = v - jnp.mean(v, axis=-1, keepdims=True)
+    inverse = lax.rsqrt(jnp.mean(centered * centered, axis=-1, keepdims=True) + EPSILON)
+    return centered * inverse, inverse
+
+
+def ln_back(grad, hat, inverse, gain):
+    scaled = grad * gain
+    return inverse * (
+        scaled
+        - jnp.mean(scaled, axis=-1, keepdims=True)
+        - hat * jnp.mean(scaled * hat, axis=-1, keepdims=True)
+    )
+
+
+WIDE = ((0, 0), (1, 1), (2, 4), (4, 2), (6, 6), (5, 3), (3, 5), (7, 7))
+DIRECT = tuple((k, k) for k in range(N))
+
+
+def pack_kernel(wk, wq, lat, wv, out):
+    rows = wk.shape[0]
+    out[0:rows, :] = wk[...]
+    at = rows
+    out[at : at + wq.shape[0], :] = wq[...]
+    at += wq.shape[0]
+    for c in range(5):
+        out[at : at + lat.shape[0], :] = lat[:, 256 * c : 256 * (c + 1)]
+        at += lat.shape[0]
+    for c in range(5):
+        out[at : at + wv.shape[0], :] = wv[:, 256 * c : 256 * (c + 1)]
+        at += wv.shape[0]
+
+
+def pack_rows_kernel(a, b, c, out):
+    rows = a.shape[0]
+    for n, ref in enumerate((a, b, c)):
+        out[rows * n : rows * (n + 1), :] = ref[...]
+
+
+def rows_of(j, size):
+    return pl.ds(pl.multiple_of(j * size, size & -size), size)
+
+
+def run_copies(copies, sem):
+    handles = [pltpu.make_async_copy(a, b, sem.at[n]) for n, (a, b) in enumerate(copies)]
+    for h in handles:
+        h.start()
+    return handles
+
+
+def wait_all(handles):
+    for h in handles:
+        h.wait()
+
+
+def norm_kernel(x, bg, xn_o):
+    hat, _ = ln_parts(x[...].astype(F32))
+    xn_o[...] = (hat * bg[...][None, :]).astype(BF)
+
+
+def query_kernel(xn, qg, *rest):
+    pieces, (k_o, wk_o, wq_o, q_o, zn_o, lat, sem) = rest[:N], rest[N:]
+    me, _ = me_z()
+    copies = []
+    for piece, rel in zip(pieces, WIDE):
+        j = owner(me, rel)
+        copies.append((piece.at[pl.ds(0, 96), :], wk_o.at[rows_of(j, 96), :]))
+        copies.append((piece.at[pl.ds(96, 160), :], wq_o.at[rows_of(j, 160), :]))
+        for c in range(5):
+            copies.append((piece.at[pl.ds(256 + 32 * c, 32), :], lat.at[rows_of(j, 32), pl.ds(256 * c, 256)]))
+    wait_all(run_copies(copies, sem))
+    zhat, _ = ln_parts(lat[...].astype(F32))
+    zn_o[...] = (zhat * qg[...][None, :]).astype(BF)
+    q_o[...] = dot(zn_o[...], wq_o[...], 1, 0).astype(BF)
+    k_o[...] = dot(xn[...], wk_o[...], 1, 0).astype(BF)
+
+
+def scores_kernel(prefix, k, q, e_o, ll_o):
+    me, _ = me_z()
+    lanes = lax.broadcasted_iota(jnp.int32, (256, 256), 1) // 32
+    pos = lax.broadcasted_iota(jnp.int32, (256, 512), 1) + me * 512
+    own = STRIDE * (lax.broadcasted_iota(jnp.int32, (256, 1), 0) + 1)
+    lane = lax.broadcasted_iota(jnp.int32, (256, 128), 1)
+    ll_o[...] = jnp.zeros_like(ll_o)
+    for s in range(2):
+        seen = jnp.maximum(own, prefix[s])
+
+        def head(h, carry, s=s, seen=seen):
+            qh = jnp.where(lanes == h, q[...], jnp.zeros((), BF))
+            scores = dot(qh, k[512 * s : 512 * (s + 1), :], 1, 1)
+            e = jnp.where(pos < seen, jnp.exp2(scores * (LOG2E * 32 ** (-0.5))), 0.0)
+            ll_o[s] += jnp.where(lane == h, jnp.sum(e, axis=-1, keepdims=True), 0.0)
+            e_o[s, h] = e.astype(BF)
+            return carry
+
+        lax.fori_loop(0, H, head, 0, unroll=2)
+
+
+def values_kernel(xn, *rest):
+    pieces, (vt_o, wv_o, sem) = rest[:N], rest[N:]
+    me, _ = me_z()
+    wait_all(
+        run_copies(
+            [
+                (p.at[pl.ds(416 + 96 * c, 96), :], wv_o.at[rows_of(owner(me, rel), 96), pl.ds(256 * c, 256)])
+                for p, rel in zip(pieces, WIDE)
+                for c in range(5)
+            ],
+            sem,
+        )
+    )
+    for c in range(5):
+        cols = slice(256 * c, 256 * (c + 1))
+        vt_o[cols, :] = dot(wv_o[:, cols], xn[...], 0, 1).astype(BF)
+
+
+def sums_kernel(vt, e, ll, *rest):
+    mine_o, theirs_o, aat, acc = rest[-4:]
+    me, _ = me_z()
+
+    def head(h, carry):
+        rows = rows_of(h, 160)
+        aat[rows, :] = dot(vt[rows, :], e[h], 1, 1).astype(BF)
+        return carry
+
+    lax.fori_loop(0, H, head, 0, unroll=2)
+    acc[:, 0:1280] = aat[...].T
+    acc[:, 1280:1408] = ll[...].astype(BF)
+    for kk in range(4):
+        for odd, ref in ((0, mine_o), (1, theirs_o)):
+            ref[kk] = acc[rows_of(me ^ (2 * kk + odd), 32), :]
+
+
+def add4_kernel(a, b, *outs):
+    for kk in range(4):
+        outs[kk][...] = (a[kk].astype(F32) + b[kk].astype(F32)).astype(BF)
+
+
+def latent_kernel(m0, r1, r2, r3, lat, mg1, cot, *rest):
+    pieces, rest = rest[:N], rest[N:]
+    latents_o, agb_o, mine_o, theirs_o, dab_o, init_o = rest[:6]
+    wout, wup, wdown, sem = rest[6:]
+    me, zi = me_z()
+    groups = []
+    for g, w in enumerate((wout, wup, wdown)):
+        copies = [
+            (p.at[pl.ds(160 * g, 160), :], w.at[rows_of(owner(me, rel), 160), :]) for p, rel in zip(pieces, WIDE)
+        ]
+        groups.append(run_copies(copies, sem.at[g]))
+    mg = mg1[...][None, :]
+    total = (m0[...].astype(F32) + r1[...].astype(F32)) + (r2[...].astype(F32) + r3[...].astype(F32))
+    aa = total[:, 0:1280]
+    ll = total[:, 1280:1408]
+    head = lax.broadcasted_iota(jnp.int32, (64, 1280), 1) // 160
+    inv = jnp.zeros((64, 1280), F32)
+    for h in range(H):
+        inv = jnp.where(head == h, 1.0 / ll[:, h : h + 1], inv)
+    oo = aa * inv
+    ob = oo.astype(BF)
+    for h in groups[0]:
+        h.wait()
+    start = lat[...].astype(F32)
+    hh = jnp.concatenate([start, start], axis=0) + dot(ob, wout[...], 1, 0)
+    hat, inverse = ln_parts(hh)
+    hn = (hat * mg).astype(BF)
+    for h in groups[1]:
+        h.wait()
+    uu = dot(hn, wup[...], 1, 0)
+    cdf = 0.5 * (1.0 + lax.erf(uu * (0.5**0.5)))
+    gg = (uu * cdf).astype(BF)
+    slope = cdf + uu * (jnp.exp(-0.5 * uu * uu) * 0.3989422804014327)
+    for h in groups[2]:
+        h.wait()
+    latents_o[...] = (hh + dot(gg, wdown[...], 1, 0)).astype(BF)
+    du = (dot(cot[...], wdown[...], 1, 1) * slope).astype(BF)
+    dhn = dot(du, wup[...], 1, 1)
+    dhh = cot[...].astype(F32) + ln_back(dhn, hat, inverse, mg)
+    init_o[...] = dhh[0:32] + dhh[32:64]
+    dhb = dhh.astype(BF)
+    dob = dot(dhb, wout[...], 1, 1).astype(BF).astype(F32)
+    dab_o[:, 0:1280] = (dob * inv).astype(BF)
+    prod = dob * oo
+    lane = lax.broadcasted_iota(jnp.int32, (64, 128), 1)
+    dlb = jnp.zeros((64, 128), F32)
+    for h in range(H):
+        part = jnp.sum(jnp.where(head == h, prod, 0.0), axis=-1, keepdims=True)
+        dlb = jnp.where(lane == h, -part / ll[:, h : h + 1], dlb)
+    dab_o[:, 1280:1408] = dlb.astype(BF)
+    agb_o[0] = dhb
+    agb_o[1] = du
+    agb_o[2] = cot[...]
+    for j in range(N):
+        kk = (me >> 1) ^ (j >> 1)
+        cols = slice(160 * j, 160 * (j + 1))
+
+        @pl.when((me & 1) == (j & 1))
+        def _():
+            for n, v in enumerate((ob, hn, gg)):
+                mine_o[kk, n] = v[:, cols]
+
+        @pl.when((me & 1) != (j & 1))
+        def _():
+            for n, v in enumerate((ob, hn, gg)):
+                theirs_o[kk, n] = v[:, cols]
+
+
+def stack_kernel(mine, other, *outs):
+    for kk in range(1, 4):
+        outs[kk - 1][0] = mine[kk]
+        outs[kk - 1][1] = other[kk]
+
+
+def backward_kernel(s, k, vt, q, e, *rest):
+    pieces, rest = rest[:N], rest[N + s :]
+    dkvt_o, dq_o = rest[:2]
+    dabx, dabt, qt, sem = rest[2:]
+    me, _ = me_z()
+    handles = run_copies(
+        [(p.at[pl.ds(32 * s, 32), :], dabx.at[rows_of(owner(me, rel), 32), :]) for p, rel in zip(pieces, DIRECT)], sem
+    )
+    qt[...] = q[...].T
+    dq_o[...] = jnp.zeros_like(dq_o)
+    wait_all(handles)
+    lanes = lax.broadcasted_iota(jnp.int32, (256, 256), 1) // 32
+    lane = lax.broadcasted_iota(jnp.int32, (256, 128), 1)
+    scale = 32 ** (-0.5)
+    dabt[...] = dabx[:, 0:1280].T
+
+    def head(h, carry):
+        rows = rows_of(h, 160)
+        dkvt_o[pl.ds(pl.multiple_of(256 + h * 160, 32), 160), :] = dot(dabt[rows, :], e[h], 1, 0).astype(BF)
+        dlb = jnp.sum(jnp.where(lane == h, dabx[:, 1280:1408].astype(F32), 0.0), axis=-1, keepdims=True)
+        dee = dot(dabt[rows, :], vt[rows, :], 0, 0) + dlb
+        dss = (e[h].astype(F32) * dee).astype(BF)
+        krows = rows_of(h, 32)
+        dkvt_o[krows, :] = (dot(qt[krows, :], dss, 1, 0) * scale).astype(BF)
+        dq_o[...] += jnp.where(lanes == h, dot(dss, k[...], 1, 0), 0.0)
+        return carry
+
+    lax.fori_loop(0, H, head, 0, unroll=2)
+    dq_o[...] = dq_o[...] * scale
+
+
+def weights_kernel(xn, zn, dkvt, dq0, dq1, mine_o, theirs_o, xnt, dw, dqg, dqs):
+    me, _ = me_z()
+    xnt[...] = xn[...].T
+    dqs[...] = dq0[...] + dq1[...]
+    for c in range(6):
+        cols = slice(256 * c, 256 * (c + 1))
+        dw[:, cols] = dot(xnt[...], dkvt[cols, :], 1, 1).astype(BF)
+    dqg[...] = dot(zn[...], dqs[...].astype(BF), 0, 0).astype(BF)
+    for kk in range(4):
+        for odd, ref in ((0, mine_o), (1, theirs_o)):
+            j = me ^ (2 * kk + odd)
+            for c in range(6):
+                ref[kk, 96 * c : 96 * (c + 1), :] = dw[rows_of(j, 96), 256 * c : 256 * (c + 1)]
+            ref[kk, 576:736, :] = dqg[rows_of(j, 160), :]
+            ref[kk, 736:768, :] = dqs[rows_of(j, 32), :].astype(BF)
+
+
+def own_part(gain, me, size):
+    out = gain[0:size][None, :]
+    for j in range(1, N):
+        out = jnp.where(me == j, gain[size * j : size * (j + 1)][None, :], out)
+    return out
+
+
+def sum_slots_kernel(a, b, c, d, wk, wv, wq, bg, qg, mix, *rest):
+    outs, norm_o, acc = rest[:NZ], rest[NZ], rest[NZ + 1]
+    me, zi = me_z()
+    total = (a[...].astype(F32) + b[...].astype(F32)) + (c[...].astype(F32) + d[...].astype(F32))
+    acc[...] = total.astype(BF)
+    for r in range(NZ):
+        outs[r][...] = acc[rows_of(zi ^ r, 192), :]
+    prod = total[0:96] * wk[...].astype(F32)
+    for n in range(5):
+        prod += total[96 * (n + 1) : 96 * (n + 2)] * wv[:, 256 * n : 256 * (n + 1)].astype(F32)
+    parts = (
+        (row_sums(prod) / own_part(bg[...], me, 96), 96),
+        (mix[...], 160),
+        (row_sums(total[576:736] * wq[...].astype(F32)) / own_part(qg[...], me, 160), 160),
+    )
+    row = lax.broadcasted_iota(jnp.int32, (8, 1280), 0)
+    placed = jnp.zeros((8, 1280), F32)
+    for n, (v, size) in enumerate(parts):
+        at = lax.broadcasted_iota(jnp.int32, (size, 1280), 1)
+        pick = (at == lax.broadcasted_iota(jnp.int32, (size, 1280), 0) + size * me).astype(F32)
+        wide = lax.dot_general(
+            v, pick, (((1,), (0,)), ((), ())), precision=lax.Precision.HIGHEST, preferred_element_type=F32
+        )
+        placed = jnp.where(row == n, wide, placed)
+    norm_o[...] = placed
+
+
+def bytes_kernel(x, bg, wk, wv, dkvt, *rest):
+    out = rest[-1]
+    hat, inverse = ln_parts(x[...].astype(F32))
+    dxn = dot(dkvt[0:256, :], wk[...], 0, 1) + dot(dkvt[256:1536, :], wv[...], 0, 1)
+    out[...] = ln_back(dxn, hat, inverse, bg[...][None, :])
+
+
+def latent_grads_kernel(init, wup, mg, amine, at, b1, b2, b3, *rest):
+    rows, outs, mix_o, (xs, ys, acc, sem) = rest[:N], rest[N : N + 4], rest[N + 4], rest[N + 5 :]
+    me, zi = me_z()
+    copies = []
+    cols = (amine.at[0], at.at[0], b1.at[0], b1.at[1], b2.at[0], b2.at[1], b3.at[0], b3.at[1])
+    for k in range(N):
+        copies.append((cols[k], xs.at[:, rows_of(me ^ k, 64), :]))
+        copies.append((rows[k], ys.at[:, rows_of(owner(me, WIDE[k]), 64), :]))
+    wait_all(run_copies(copies, sem))
+    for n in range(3):
+        grad = dot(xs[n], ys[n], 0, 0)
+        acc[160 * n : 160 * (n + 1), :] = grad.astype(BF)
+        if n == 1:
+            mix_o[...] = row_sums(grad * wup[...].astype(F32)) / own_part(mg[...], me, 160)
+    acc[480:512, :] = init[...].astype(BF)
+    for r in range(NZ):
+        outs[r][...] = acc[rows_of(zi ^ r, 128), :]
+
+
+def row_sums(v):
+    ones = jnp.ones((8, v.shape[1]), F32)
+    return lax.dot_general(
+        ones, v, (((1,), (1,)), ((), ())), precision=lax.Precision.HIGHEST, preferred_element_type=F32
+    )
+
+
+def finish_latent_kernel(*rest):
+    pieces, (out_o, up_o, down_o, init_o, acc) = rest[:NZ], rest[NZ:]
+    _, zi = me_z()
+    for r in range(NZ):
+        acc[rows_of(zi ^ r, 128), :] = pieces[r][...]
+    out_o[...] = acc[0:160, :].astype(F32)
+    up_o[...] = acc[160:320, :].astype(F32)
+    down_o[...] = acc[320:480, :].astype(F32)
+    init_o[...] = acc[480:512, :].astype(F32)
+
+
+def finish_kernel(wq_full, lat, qg, init, *rest):
+    pieces, (key_o, value_o, query_o, init_o, acc) = rest[:NZ], rest[NZ:]
+    _, zi = me_z()
+    for r in range(NZ):
+        acc[rows_of(zi ^ r, 192), :] = pieces[r][...]
+    key_o[...] = acc[0:96, :].astype(F32)
+    for c in range(5):
+        value_o[:, 256 * c : 256 * (c + 1)] = acc[96 * (c + 1) : 96 * (c + 2), :].astype(F32)
+    query_o[...] = acc[576:736, :].astype(F32)
+    dzn = dot(acc[736:768, :], wq_full[...], 1, 1)
+    hat, inverse = ln_parts(lat[...].astype(F32))
+    init_o[...] = init[...] + ln_back(dzn, hat, inverse, qg[...][None, :])
+
+
+def norms_kernel(a, b, byte_o, mixer_o, query_o):
+    total = a[...] + b[...]
+    row = lax.broadcasted_iota(jnp.int32, (8, 1280), 0)
+    for n, out in enumerate((byte_o, mixer_o, query_o)):
+        out[...] = jnp.sum(jnp.where(row == n, total, 0.0), axis=0)[: out.shape[0]]
+
+
+def sums_of_pairs_kernel(*refs):
+    n = len(refs) // 3
+    for k in range(n):
+        a, b, out = refs[2 * k], refs[2 * k + 1], refs[2 * n + k]
+        out[...] = (a[...].astype(F32) + b[...].astype(F32)).astype(out.dtype)
+
+
+def sums_of_pairs(pairs, name, deps=()):
+    flat = [x for pair in pairs for x in pair]
+    out = [sds(a.shape, a.dtype) for a, _ in pairs]
+    return call(sums_of_pairs_kernel, out, flat, [VMEM] * len(flat), name=name, deps=deps)
+
+
+def part(f, *args):
+    def body(*refs):
+        return f(*args, *refs)
+
+    return body
+
+
+def tie(*xs):
+    return lax.optimization_barrier(xs)
+
+
+def per_device_fast(
+    byte_feats,
+    latent_init,
+    prefix,
+    byte_gain,
+    query_gain,
+    mixer_gain,
+    query_weight,
+    key_weight,
+    value_weight,
+    out_weight,
+    up_weight,
+    down_weight,
+    cotangent,
+):
+    seqs, rows, width = byte_feats.shape
+    own = latent_init.shape[0]
+    x = byte_feats.reshape(seqs * rows, width)
+    cot = cotangent.reshape(seqs * own, DL)
+
+    def first(w):
+        return send_split(w, 2, 4), send_split(w, 4, 2)
+
+    packed = call(
+        pack_kernel, sds((896, 256), BF), (key_weight, query_weight, latent_init, value_weight), [VMEM] * 4, name="pack"
+    )
+    pa, pb = first(packed)
+    wcat = call(
+        pack_rows_kernel, sds((480, 1280), BF), (out_weight, up_weight, down_weight), [VMEM] * 3, name="pack_rows", deps=(packed,)
+    )
+    xn = call(norm_kernel, sds((1024, 768), BF), (x, byte_gain), [VMEM] * 2, name="norm", deps=(wcat,))
+    pa, pb, xn, near = tie(pa, pb, xn, packed)
+    pd = send_split(pa, 4, 2)
+    pn, pna, pnb = send(near, 1), send(pa, 1), send(pb, 1)
+    pd, wcat = tie(pd, wcat)
+    pnd = send(pd, 1)
+    wa, wb = first(wcat)
+    wn = send(wcat, 1)
+    pieces = (packed, pn, pa, pb, pd, pna, pnb, pnd)
+    k, wk, wq_full, q, zn = call(
+        query_kernel,
+        (sds((1024, 256), BF), sds((768, 256), BF), sds((1280, 256), BF), sds((256, 256), BF), sds((256, 1280), BF)),
+        (xn, query_gain, *pieces),
+        [VMEM] * 2 + [ANY] * N,
+        [pltpu.VMEM((256, 1280), BF), pltpu.SemaphoreType.DMA((7 * N,))],
+        name="query",
+    )
+    e, ll = call(
+        scores_kernel,
+        (sds((2, 8, 256, 512), BF), sds((2, 256, 128), F32)),
+        (prefix, k, q),
+        [SMEM, VMEM, VMEM],
+        name="scores",
+    )
+    vt, wv = call(
+        values_kernel,
+        (sds((1280, 1024), BF), sds((768, 1280), BF)),
+        (xn, *pieces),
+        [VMEM] + [ANY] * N,
+        [pltpu.SemaphoreType.DMA((5 * N,))],
+        name="values",
+        deps=(e, wn),
+    )
+    def sums(s, *prev):
+        return call(
+            sums_kernel,
+            (sds((4, 64, 1408), BF), sds((4, 64, 1408), BF)),
+            (vt, e, ll, *prev),
+            [
+                pl.BlockSpec((1280, 512), lambda g: (0, s)),
+                pl.BlockSpec((None, 8, 256, 512), lambda g: (s, 0, 0, 0)),
+                pl.BlockSpec((None, 256, 128), lambda g: (s, 0, 0)),
+            ]
+            + [ANY] * len(prev),
+            [pltpu.VMEM((1280, 256), BF), pltpu.VMEM((256, 1408), BF)],
+            out_specs=[pl.BlockSpec((4, 32, 1408), lambda g: (0, s, 0))] * 2,
+            aliases={3: 0, 4: 1} if prev else {},
+            name="sums",
+            grid=(1,),
+        )
+
+    mine, theirs = sums(0)
+    mine, wa, wb = tie(mine, wa, wb)
+    wd = send_split(wa, 4, 2)
+    wna, wnb = send(wa, 1), send(wb, 1)
+    mine, theirs = sums(1, mine, theirs)
+    got = send(theirs, 1)
+    m0, m1, m2, m3 = call(
+        add4_kernel, (sds((64, 1408), BF),) * 4, (mine, got), [VMEM] * 2, name="add4", deps=(wna, wnb)
+    )
+    r1, r2, r3 = send(m1, 2), send(m2, 4), send(m3, 6)
+    r1, r2, r3, wd = tie(r1, r2, r3, wd)
+    wnd = send(wd, 1)
+    latents, agb, amine, atheirs, dabx, init = call(
+        latent_kernel,
+        (
+            sds((64, 1280), BF), sds((3, 64, 1280), BF), sds((4, 3, 64, 160), BF), sds((4, 3, 64, 160), BF),
+            sds((64, 1408), BF), sds((32, 1280), F32),
+        ),
+        (m0, r1, r2, r3, latent_init, mixer_gain, cot, wcat, wn, wa, wb, wd, wna, wnb, wnd),
+        [VMEM] * 7 + [ANY] * N,
+        [pltpu.VMEM((1280, 1280), BF)] * 3 + [pltpu.SemaphoreType.DMA((3, N))],
+        name="latent",
+    )
+    d2, d4, d6, d1 = send(dabx, 2), send(dabx, 4), send(dabx, 6), send(dabx, 1)
+    at = send(atheirs, 1)
+    d2, d4, d6, agb = tie(d2, d4, d6, agb)
+    d3, d5, d7 = send(d2, 1), send(d4, 1), send(d6, 1)
+    dab_p = [dabx, d1, d2, d3, d4, d5, d6, d7]
+    ga, gb = first(agb)
+    gn = send(agb, 1)
+
+    def backward(s, *prev):
+        return call(
+            part(backward_kernel, s),
+            (sds((1536, 1024), BF), sds((256, 256), F32)),
+            (k, vt, q, e, *dab_p, *prev),
+            [
+                pl.BlockSpec((512, 256), lambda g: (s, 0)),
+                pl.BlockSpec((1280, 512), lambda g: (0, s)),
+                VMEM,
+                pl.BlockSpec((None, 8, 256, 512), lambda g: (s, 0, 0, 0)),
+            ]
+            + [ANY] * (N + len(prev)),
+            [
+                pltpu.VMEM((256, 1408), BF), pltpu.VMEM((1280, 256), BF), pltpu.VMEM((256, 256), BF),
+                pltpu.SemaphoreType.DMA((N,)),
+            ],
+            out_specs=(pl.BlockSpec((1536, 512), lambda g: (0, s)), VMEM),
+            aliases={4 + N: 0} if prev else {},
+            name="backward",
+            grid=(1,),
+            deps=deps_of[s],
+        )
+
+    deps_of = {0: ()}
+    dkvt, dq0 = backward(0)
+    dq0, ga, gb, gn, at = tie(dq0, ga, gb, gn, at)
+    gd = send_split(ga, 4, 2)
+    gna = send(ga, 1)
+    both = call(stack_kernel, (sds((2, 3, 64, 160), BF),) * 3, (amine, at), [VMEM] * 2, name="stack", deps=(dq0,))
+    both_s = [send(b, 2 * kk + 2) for kk, b in enumerate(both)]
+    deps_of[1] = (both[0], dq0)
+    dkvt, dq1 = backward(1, dkvt)
+    dq1, gd, gna, gb = tie(dq1, gd, gna, gb)
+    gnb, gnd = send(gb, 1), send(gd, 1)
+    gmine, gtheirs = call(
+        weights_kernel,
+        (sds((4, 768, 256), BF), sds((4, 768, 256), BF)),
+        (xn, zn, dkvt, dq0, dq1),
+        [VMEM] * 5,
+        [
+            pltpu.VMEM((768, 1024), BF), pltpu.VMEM((768, 1536), BF), pltpu.VMEM((1280, 256), BF),
+            pltpu.VMEM((256, 256), F32),
+        ],
+        name="weights",
+        deps=(),
+    )
+    gg = send(gtheirs, 1)
+
+    *oud, mix = call(
+        latent_grads_kernel,
+        (sds((128, 1280), BF),) * NZ + (sds((8, 160), F32),),
+        (init, up_weight, mixer_gain, amine, at, *both_s, agb, gn, ga, gb, gd, gna, gnb, gnd),
+        [VMEM] * 3 + [ANY] * (5 + N),
+        [
+            pltpu.VMEM((3, 512, 160), BF), pltpu.VMEM((3, 512, 1280), BF), pltpu.VMEM((512, 1280), BF),
+            pltpu.SemaphoreType.DMA((2 * N,)),
+        ],
+        name="latent_grads",
+        deps=(gtheirs,),
+    )
+    o3, o1 = send_z(oud[3], 1), send_z(oud[1], 1)
+    gm = call(add4_kernel, (sds((768, 256), BF),) * 4, (gmine, gg), [VMEM] * 2, name="add4g", deps=(oud[0],))
+    g1, g2, g3 = send(gm[1], 2), send(gm[2], 4), send(gm[3], 6)
+    byte_grads = call(
+        bytes_kernel,
+        sds((2, 512, 768), F32),
+        (x, byte_gain, wk, wv, dkvt),
+        [
+            pl.BlockSpec((256, 768), lambda b: (b, 0)),
+            pl.BlockSpec((768,), lambda b: (0,)),
+            pl.BlockSpec((768, 256), lambda b: (0, 0)),
+            pl.BlockSpec((768, 1280), lambda b: (0, 0)),
+            pl.BlockSpec((1536, 256), lambda b: (0, b)),
+        ],
+        out_specs=pl.BlockSpec((None, 256, 768), lambda b: (b // 2, b % 2, 0)),
+        name="bytes",
+        grid=(4,),
+        deps=(gm[0],),
+    )
+    o2, o0 = sums_of_pairs(((oud[2], o3), (oud[0], o1)), "osum", deps=(byte_grads,))
+    o22 = send_z(o2, 2)
+    *gq, norm = call(
+        sum_slots_kernel,
+        (sds((192, 256), BF),) * NZ + (sds((8, 1280), F32),),
+        (gm[0], g1, g2, g3, key_weight, value_weight, query_weight, byte_gain, query_gain, mix),
+        [VMEM] * 10,
+        [pltpu.VMEM((768, 256), BF)],
+        name="gsum",
+        deps=(o0,),
+    )
+    q3, q1, n1 = send_z(gq[3], 1), send_z(gq[1], 1), send_z(norm, 1)
+    q2, q0, norm, ototal = sums_of_pairs(((gq[2], q3), (gq[0], q1), (norm, n1), (o0, o22)), "qsum")
+    ofar, onear = send_z(ototal, 2), send_z(ototal, 1)
+    q22, n2 = send_z(q2, 2), send_z(norm, 2)
+    qtotal, norm = sums_of_pairs(((q0, q22), (norm, n2)), "qtotal")
+    qfar, qnear, n3 = send_z(qtotal, 2), send_z(qtotal, 1), send(norm, 1)
+    ofar2 = send_z(ofar, 1)
+    (norm,) = sums_of_pairs(((norm, n3),), "nsum")
+    n4 = send(norm, 2)
+    qfar2 = send_z(qfar, 1)
+    out_g, up_g, down_g, init_sum = call(
+        finish_latent_kernel,
+        (sds((160, 1280), F32),) * 3 + (sds((32, 1280), F32),),
+        (ototal, onear, ofar, ofar2),
+        [VMEM] * NZ,
+        [pltpu.VMEM((512, 1280), BF)],
+        name="finish_latent",
+        deps=(norm,),
+    )
+    (norm,) = sums_of_pairs(((norm, n4),), "nsum", deps=(init_sum,))
+    n5 = send(norm, 4)
+    key_g, value_g, query_g, init_g = call(
+        finish_kernel,
+        (sds((96, 256), F32), sds((96, 1280), F32), sds((160, 256), F32), sds((32, 1280), F32)),
+        (wq_full, latent_init, query_gain, init_sum, qtotal, qnear, qfar, qfar2),
+        [VMEM] * (4 + NZ),
+        [pltpu.VMEM((768, 256), BF)],
+        name="finish",
+        deps=(norm,),
+    )
+    byte_n, mixer_n, query_n = call(
+        norms_kernel,
+        (sds((768,), F32), sds((1280,), F32), sds((1280,), F32)),
+        (norm, n5),
+        [VMEM] * 2,
+        name="norms",
+        deps=(init_g,),
+    )
+    return (
+        latents.reshape(seqs, own, DL),
+        byte_grads,
+        init_g,
+        byte_n,
+        query_n,
+        mixer_n,
+        query_g,
+        key_g,
+        value_g,
+        out_g,
+        up_g,
+        down_g,
+    )
+
+
 def solution(mesh):
+    fast = mesh.shape["fsdp"] == 8 and mesh.shape["rep"] == 4
+    device_fn = per_device_fast if fast else per_device_plain
     placed = (
         P("rep", "fsdp", None),
         P("fsdp", None),
@@ -266,7 +974,7 @@
         P("rep", "fsdp", None),
     )
     return jax.shard_map(
-        per_device,
+        device_fn,
         mesh=mesh,
         in_specs=placed,
         out_specs=(

time: 969 us -> 259 us (0.27)
  waiting for transfers between devices: 656 us -> 79.8 us
  blocking collectives: 115 us -> 0 us
  Pallas kernels: 0 us -> 111 us
  matrix products: 86.9 us -> 0 us
  local copies, waits for them, and re-layouts: 70.2 us -> 11.5 us
  starting transfers between devices: 1.11 us -> 54 us
  other arithmetic: 19.9 us -> 0 us
  between operations: 14.8 us -> 1 us
    reduce_scatter x6 -> x0, waiting for transfers between devices: 296 us -> none  [the longest x1 66.4 us: per_device(): lax.psum_scatter(down_local, 'fsdp', scatter_dimension=0, tiled=True)]
    while x12 -> x0, waiting for transfers between devices: 192 us -> none
    pallas_call x0 -> x26, Pallas kernels: none -> 111 us  [call(): pl.pallas_call(run, grid=grid, out_shape=out, in_specs=list(specs) + [ANY...]
    all_gather x4 -> x0, waiting for transfers between devices: 89.7 us -> none  [the longest x1 32 us: per_device(): lax.all_gather(down_weight, 'fsdp', axis=0, tiled=True)]
    dot_general x32 -> x0, matrix products: 86.9 us -> none  [the longest x2 8.92 us: backward_step(): jnp.einsum('hji,jhv->ihv', weights.astype(jnp.bfloat16), sum_heads, prefe...]
    ppermute x0 -> x57, waiting for transfers between devices: none -> 79.8 us  [the longest x14 34.5 us: send_z(): return lax.ppermute(x, 'rep', [(i, i ^ k) for i in range(NZ)])]
    psum x1 -> x0, waiting for transfers between devices: 75.8 us -> none  [per_device(): lax.psum((group_parts[0], group_parts[1], group_parts[2], group_parts[3],...]
    all_gather x7 -> x0, blocking collectives: 71.2 us -> none  [the longest x2 20.1 us: backward_step(): lax.all_gather(sum_own, 'fsdp', axis=0, tiled=True)]
  transfers between devices with their start and end apart: 17 -> 57, of which waited for: 16 -> 18; matrix products, arithmetic and copies ran while one was open for 9% -> 0% of each run, Pallas kernels for 0% -> 37%
where the time goes in v2:
time: 259 us; the launch traced here: 258 us
  Pallas kernels  111 us (43%)
  waiting for transfers between devices  79.8 us (31%)
  starting transfers between devices  54 us (21%)
  local copies, waits for them, and re-layouts  11.5 us (4%)
    pallas_call x26, Pallas kernels, call(): pl.pallas_call(run, grid=grid, out_shape=out, in_specs=list(specs) + [ANY...  111 us
    ppermute x14, waiting for transfers between devices, send_z(): return lax.ppermute(x, 'rep', [(i, i ^ k) for i in range(NZ)])  34.5 us
    ppermute x9, waiting for transfers between devices, send_split(): lax.ppermute(x, 'fsdp', [(i, i ^ (odd if i & 1 else even)) for i in range...  25.4 us
    ppermute x34, starting transfers between devices, send(): return lax.ppermute(x, 'fsdp', [(i, i ^ k) for i in range(N)])  21.5 us
    ppermute x34, waiting for transfers between devices, send(): return lax.ppermute(x, 'fsdp', [(i, i ^ k) for i in range(N)])  19.9 us
    ppermute x14, starting transfers between devices, send_z(): return lax.ppermute(x, 'rep', [(i, i ^ k) for i in range(NZ)])  18.7 us
    ppermute x9, starting transfers between devices, send_split(): lax.ppermute(x, 'fsdp', [(i, i ^ (odd if i & 1 else even)) for i in range...  13.7 us
    unnamed x80, local copies, waits for them, and re-layouts  11.5 us
  transfers between devices with their start and end apart: 57, of which 18 were waited for; matrix products, arithmetic and copies ran while one was open for 0% of the time, Pallas kernels for 37%

profile of v2, /device:TPU:0, one launch (start us, length us, event | category | flops | bytes accessed | tf_op | source)
XLA Modules:
  0.0 257.8 jit_solution(9464732738200384988)
XLA Ops:
  2.5 3.0 %collective-permute-start = (bf16[896,256]{1,0:T(8,128)(2,1)}, bf16[896,256]{1,0:T(8,128)(2,1)}, u32[]{:S(2)}, u32[]{:S(2)}) collective-permute-start(bf16[896,256]{1,0:T(8,128)(2,1)} %pack.1.refs_3_.refs_2_.refs_1_), channel_id=1, source_target_pairs={{0,2},{1,5},{2,0},{3,7},{4,6},{5,1},{6,4},{7,3},{8,10},{9,13},{10,... | collective-permute-start | bytes 1376264 | tf_op jit(solution)/shard_map/ppermute | solution.py:274
  9.4 3.6 %norm.1.refs_0_ = bf16[1024,768]{1,0:T(8,128)(2,1)} custom-call(bf16[1024,768]{1,0:T(8,128)(2,1)} %bitcast.3, f32[768]{0:T(1024)} %refs_7_.1, bf16[480,1280]{1,0:T(8,128)(2,1)} %pack_rows.1.refs_2_.refs_7_), custom_call_target="tpu_custom_call" | custom-call | flops 99999997952 | bytes 1024 | tf_op jit(solution)/shard_map/norm/pallas_call | solution.py:302
  13.0 3.5 %collective-permute-done.refs_4_.refs_3_ = bf16[896,256]{1,0:T(8,128)(2,1)} collective-permute-done((bf16[896,256]{1,0:T(8,128)(2,1)}, bf16[896,256]{1,0:T(8,128)(2,1)}, u32[]{:S(2)}, u32[]{:S(2)}) %collective-permute-start) | collective-permute-done | bytes 458784 | tf_op jit(solution)/shard_map/ppermute | solution.py:274
  19.4 5.9 %collective-permute-done.3.refs_6_.refs_5_ = bf16[896,256]{1,0:T(8,128)(2,1)S(1)} collective-permute-done((bf16[896,256]{1,0:T(8,128)(2,1)}, bf16[896,256]{1,0:T(8,128)(2,1)S(1)}, u32[]{:S(2)}, u32[]{:S(2)}) %collective-permute-start.3) | collective-permute-done | bytes 458784 | tf_op jit(solution)/shard_map/ppermute | solution.py:274
  30.6 5.2 %query.1 = (bf16[1024,256]{1,0:T(8,128)(2,1)}, bf16[768,256]{1,0:T(8,128)(2,1)}, bf16[1280,256]{1,0:T(8,128)(2,1)}, bf16[256,256]{1,0:T(8,128)(2,1)}, bf16[256,1280]{1,0:T(8,128)(2,1)}) custom-call(bf16[1024,768]{1,0:T(8,128)(2,1)} %norm.1.refs_0_, f32[1280]{0:T(1024)} %refs_2_.7, bf16[896,256]{1,0:T(8,128)(2,1)} %pack.1.refs_3_.refs_2_.refs_1_, ...), custom_call_target="tpu_custom_call" | custom-call | flops 99999997952 | bytes 1024 | tf_op jit(solution)/shard_map/query/pallas_call | solution.py:302
  35.8 6.8 %scores.1 = (bf16[2,8,256,512]{3,2,1,0:T(8,128)(2,1)}, f32[2,256,128]{2,1,0:T(8,128)}) custom-call(s32[2]{0:T(128)} %refs_0_.5, bf16[1024,256]{1,0:T(8,128)(2,1)} %get-tuple-element.108.refs_1_.refs_0_, bf16[256,256]{1,0:T(8,128)(2,1)} %get-tuple-element.109.refs_2_), custom_call_target="tpu_custom_call" | custom-call | flops 99999997952 | bytes 1024 | tf_op jit(solution)/shard_map/scores/pallas_call | solution.py:302
  42.6 7.0 %values.1 = (bf16[1280,1024]{1,0:T(8,128)(2,1)}, bf16[768,1280]{1,0:T(8,128)(2,1)}) custom-call(bf16[1024,768]{1,0:T(8,128)(2,1)} %norm.1.refs_0_, bf16[896,256]{1,0:T(8,128)(2,1)} %pack.1.refs_3_.refs_2_.refs_1_, bf16[896,256]{1,0:T(8,128)(2,1)} %copy-done.14, bf16[896,256]{1,0:T(8,128)(2,1)} %collective-permute-done.refs_4_.refs_3_, ...), custom_call_target="tpu_custom_call" | custom-call | flops 99999997952 | bytes 1024 | tf_op jit(solution)/shard_map/values/pallas_call | solution.py:302
  49.6 4.4 %sums.2 = (bf16[4,64,1408]{2,1,0:T(8,128)(2,1)}, bf16[4,64,1408]{2,1,0:T(8,128)(2,1)}) custom-call(bf16[1280,1024]{1,0:T(8,128)(2,1)} %get-tuple-element.112.refs_0_.refs_1_, bf16[2,8,256,512]{3,2,1,0:T(8,128)(2,1)} %get-tuple-element.110.refs_9_.refs_1_.refs_3_, f32[2,256,128]{2,1,0:T(8,128)} %get-tuple-element.113.refs_2_), custom_call_target="tpu_custom_call" | custom-call | flops 99999997952 | bytes 1024 | tf_op jit(solution)/shard_map/sums/pallas_call | solution.py:302
  56.9 4.4 %sums.3 = (bf16[4,64,1408]{2,1,0:T(8,128)(2,1)}, bf16[4,64,1408]{2,1,0:T(8,128)(2,1)}) custom-call(bf16[1280,1024]{1,0:T(8,128)(2,1)} %get-tuple-element.112.refs_0_.refs_1_, bf16[2,8,256,512]{3,2,1,0:T(8,128)(2,1)} %get-tuple-element.110.refs_9_.refs_1_.refs_3_, ...), custom_call_target="tpu_custom_call", output_to_operand_aliasing={{0}: (3, {}), {1}: (4, {})} | custom-call | flops 99999997952 | bytes 1024 | tf_op jit(solution)/shard_map/sums/pallas_call | solution.py:302
  71.1 11.1 %collective-permute-done.16.refs_11_ = bf16[480,1280]{1,0:T(8,128)(2,1)} collective-permute-done((bf16[480,1280]{1,0:T(8,128)(2,1)}, bf16[480,1280]{1,0:T(8,128)(2,1)}, u32[]{:S(2)}, u32[]{:S(2)}) %collective-permute-start.16) | collective-permute-done | bytes 1228832 | tf_op jit(solution)/shard_map/ppermute | solution.py:274
  85.8 2.8 %collective-permute-done.17.refs_14_ = bf16[480,1280]{1,0:T(8,128)(2,1)S(1)} collective-permute-done((bf16[480,1280]{1,0:T(8,128)(2,1)}, bf16[480,1280]{1,0:T(8,128)(2,1)S(1)}, u32[]{:S(2)}, u32[]{:S(2)}) %collective-permute-start.17) | collective-permute-done | bytes 1228832 | tf_op jit(solution)/shard_map/ppermute | solution.py:270
  89.5 11.4 %latent.1 = (bf16[64,1280]{1,0:T(8,128)(2,1)}, bf16[3,64,1280]{2,1,0:T(8,128)(2,1)}, bf16[4,3,64,160]{3,2,1,0:T(8,128)(2,1)}, bf16[4,3,64,160]{3,2,1,0:T(8,128)(...) custom-call(bf16[64,1408]{1,0:T(8,128)(2,1)} %get-tuple-element.121.refs_0_, bf16[64,1408]{1,0:T(8,128)(2,1)} %copy-done.29, ...), custom_call_target="tpu_custom_call" | custom-call | flops 99999997952 | bytes 1024 | tf_op jit(solution)/shard_map/latent/pallas_call | solution.py:302
  104.6 4.1 %collective-permute-done.19.refs_6_ = bf16[64,1408]{1,0:T(8,128)(2,1)S(1)} collective-permute-done((bf16[64,1408]{1,0:T(8,128)(2,1)}, bf16[64,1408]{1,0:T(8,128)(2,1)S(1)}, u32[]{:S(2)}, u32[]{:S(2)}) %collective-permute-start.19) | collective-permute-done | bytes 180256 | tf_op jit(solution)/shard_map/ppermute | solution.py:270
  108.7 4.7 %collective-permute-done.20.refs_8_ = bf16[64,1408]{1,0:T(8,128)(2,1)S(1)} collective-permute-done((bf16[64,1408]{1,0:T(8,128)(2,1)}, bf16[64,1408]{1,0:T(8,128)(2,1)S(1)}, u32[]{:S(2)}, u32[]{:S(2)}) %collective-permute-start.20) | collective-permute-done | bytes 180256 | tf_op jit(solution)/shard_map/ppermute | solution.py:270
  117.8 8.2 %backward.2 = (bf16[1536,1024]{1,0:T(8,128)(2,1)}, f32[256,256]{1,0:T(8,128)}) custom-call(bf16[1024,256]{1,0:T(8,128)(2,1)} %get-tuple-element.108.refs_1_.refs_0_, bf16[1280,1024]{1,0:T(8,128)(2,1)} %get-tuple-element.112.refs_0_.refs_1_, bf16[256,256]{1,0:T(8,128)(2,1)} %get-tuple-element.109.refs_2_, ...), custom_call_target="tpu_custom_call" | custom-call | flops 99999997952 | bytes 1024 | tf_op jit(solution)/shard_map/backward/pallas_call | solution.py:302
  126.0 2.5 collective-permute-done.25.refs_10_
  135.6 8.3 %backward.3 = (bf16[1536,1024]{1,0:T(8,128)(2,1)}, f32[256,256]{1,0:T(8,128)}) custom-call(bf16[1024,256]{1,0:T(8,128)(2,1)} %get-tuple-element.108.refs_1_.refs_0_, bf16[1280,1024]{1,0:T(8,128)(2,1)} %get-tuple-element.112.refs_0_.refs_1_, bf16[256,256]{1,0:T(8,128)(2,1)} %get-tuple-element.109.refs_2_, ...), custom_call_target="tpu_custom_call", output_to_operand_aliasing={{0}: (12, {})} | custom-call | flops 99999997952 | bytes 1024 | tf_op jit(solution)/shard_map/backward/pallas_call | solution.py:302
  144.4 7.2 %weights.1 = (bf16[4,768,256]{2,1,0:T(8,128)(2,1)}, bf16[4,768,256]{2,1,0:T(8,128)(2,1)}) custom-call(bf16[1024,768]{1,0:T(8,128)(2,1)} %norm.1.refs_0_, bf16[256,1280]{1,0:T(8,128)(2,1)} %get-tuple-element.146.refs_1_, bf16[1536,1024]{1,0:T(8,128)(2,1)} %get-tuple-element.145.refs_2_.refs_4_, f32[256,256]{1,0:T(8,128)} %get-tuple-element.143.refs_2_.refs_14_.refs_3_, ...), custom_call_target="tpu_custom_call" | custom-call | flops 99999997952 | bytes 1024 | tf_op jit(solution)/shard_map/weights/pallas_call | solution.py:302
  152.7 6.2 %latent_grads.1 = (bf16[128,1280]{1,0:T(8,128)(2,1)}, bf16[128,1280]{1,0:T(8,128)(2,1)}, bf16[128,1280]{1,0:T(8,128)(2,1)}, bf16[128,1280]{1,0:T(8,128)(2,1)}, f32[8,160]{1,0:T(8,128)}) custom-call(f32[32,1280]{1,0:T(8,128)} %get-tuple-element.153.refs_0_, bf16[160,1280]{1,0:T(8,128)(2,1)} %refs_1_.11, f32[1280]{0:T(1024)} %refs_2_.6, ...), custom_call_target="tpu_custom_call" | custom-call | flops 99999997952 | bytes 1024 | tf_op jit(solution)/shard_map/latent_grads/pallas_call | solution.py:302
  162.1 3.1 %add4g.1 = (bf16[768,256]{1,0:T(8,128)(2,1)}, bf16[768,256]{1,0:T(8,128)(2,1)}, bf16[768,256]{1,0:T(8,128)(2,1)}, bf16[768,256]{1,0:T(8,128)(2,1)}) custom-call(bf16[4,768,256]{2,1,0:T(8,128)(2,1)} %get-tuple-element.151.refs_0_, bf16[4,768,256]{2,1,0:T(8,128)(2,1)} %copy-done, bf16[128,1280]{1,0:T(8,128)(2,1)} %get-tuple-element.160.refs_2_), custom_call_target="tpu_custom_call" | custom-call | flops 99999997952 | bytes 1024 | tf_op jit(solution)/shard_map/add4g/pallas_call | solution.py:302
  168.7 7.6 %bytes.1.refs_4_ = f32[2,512,768]{2,1,0:T(8,128)} custom-call(bf16[1024,768]{1,0:T(8,128)(2,1)} %bitcast.4, f32[768]{0:T(1024)} %refs_7_.1, bf16[768,256]{1,0:T(8,128)(2,1)} %get-tuple-element.130.refs_2_, bf16[768,1280]{1,0:T(8,128)(2,1)} %get-tuple-element.131.refs_3_, bf16[1536,1024]{1,0:T(8,128)(2,1)} %get-tuple-element.145.refs_2_.refs_4_, ...), custom_call_target="tpu_custom_call" | custom-call | flops 99999997952 | bytes 1024 | tf_op jit(solution)/shard_map/bytes/pallas_call | solution.py:302
  178.6 2.6 %collective-permute-start.45 = (bf16[128,1280]{1,0:T(8,128)(2,1)}, bf16[128,1280]{1,0:T(8,128)(2,1)S(1)}, u32[]{:S(2)}, u32[]{:S(2)}) collective-permute-start(bf16[128,1280]{1,0:T(8,128)(2,1)} %get-tuple-element.176), channel_id=1, source_target_pairs={{0,16},{8,24},{16,0},{24,8},{1,17},{9,25},{17,1},{25,9},{2,18},{10... | collective-permute-start | bytes 983048 | tf_op jit(solution)/shard_map/ppermute | solution.py:278
  181.2 4.3 %collective-permute-done.38.refs_2_ = bf16[768,256]{1,0:T(8,128)(2,1)} collective-permute-done((bf16[768,256]{1,0:T(8,128)(2,1)}, bf16[768,256]{1,0:T(8,128)(2,1)}, u32[]{:S(2)}, u32[]{:S(2)}) %collective-permute-start.38) | collective-permute-done | bytes 393248 | tf_op jit(solution)/shard_map/ppermute | solution.py:270
  185.4 3.7 %gsum.1 = (bf16[192,256]{1,0:T(8,128)(2,1)}, bf16[192,256]{1,0:T(8,128)(2,1)}, bf16[192,256]{1,0:T(8,128)(2,1)}, bf16[192,256]{1,0:T(8,128)(2,1)}, f32[8,1280]{1,0:T(8,128)}) custom-call(bf16[768,256]{1,0:T(8,128)(2,1)} %get-tuple-element.161.refs_5_.refs_0_, bf16[768,256]{1,0:T(8,128)(2,1)} %collective-permute-done.37.refs_1_, ...), custom_call_target="tpu_custom_call" | custom-call | flops 99999997952 | bytes 1024 | tf_op jit(solution)/shard_map/gsum/pallas_call | solution.py:302
  192.8 3.1 %collective-permute-done.45.refs_7_ = bf16[128,1280]{1,0:T(8,128)(2,1)S(1)} collective-permute-done((bf16[128,1280]{1,0:T(8,128)(2,1)}, bf16[128,1280]{1,0:T(8,128)(2,1)S(1)}, u32[]{:S(2)}, u32[]{:S(2)}) %collective-permute-start.45) | collective-permute-done | bytes 327712 | tf_op jit(solution)/shard_map/ppermute | solution.py:278
  196.0 5.0 %collective-permute-done.44.refs_5_ = f32[8,1280]{1,0:T(8,128)S(1)} collective-permute-done((f32[8,1280]{1,0:T(8,128)}, f32[8,1280]{1,0:T(8,128)S(1)}, u32[]{:S(2)}, u32[]{:S(2)}) %collective-permute-start.44) | collective-permute-done | bytes 40992 | tf_op jit(solution)/shard_map/ppermute | solution.py:278
  208.4 13.0 %collective-permute-done.50.refs_3_ = f32[8,1280]{1,0:T(8,128)S(1)} collective-permute-done((f32[8,1280]{1,0:T(8,128)}, f32[8,1280]{1,0:T(8,128)S(1)}, u32[]{:S(2)}, u32[]{:S(2)}) %collective-permute-start.50) | collective-permute-done | bytes 40992 | tf_op jit(solution)/shard_map/ppermute | solution.py:278
  231.2 3.0 %collective-permute-done.53.refs_6_ = bf16[192,256]{1,0:T(8,128)(2,1)} collective-permute-done((bf16[192,256]{1,0:T(8,128)(2,1)}, bf16[192,256]{1,0:T(8,128)(2,1)}, u32[]{:S(2)}, u32[]{:S(2)}) %collective-permute-start.53) | collective-permute-done | bytes 98336 | tf_op jit(solution)/shard_map/ppermute | solution.py:278
  234.2 2.7 %collective-permute-start.54 = (bf16[192,256]{1,0:T(8,128)(2,1)}, bf16[192,256]{1,0:T(8,128)(2,1)}, u32[]{:S(2)}, u32[]{:S(2)}) collective-permute-start(bf16[192,256]{1,0:T(8,128)(2,1)} %collective-permute-done.53.refs_6_), channel_id=1, source_target_pairs={{0,8},{8,0},{16,24},{24,16},{1,9},{9,1},{17,25},{25,17},{2,10},{10... | collective-permute-start | bytes 294920 | tf_op jit(solution)/shard_map/ppermute | solution.py:278
  236.9 8.9 %collective-permute-done.48.refs_3_ = bf16[128,1280]{1,0:T(8,128)(2,1)S(1)} collective-permute-done((bf16[128,1280]{1,0:T(8,128)(2,1)S(1)}, bf16[128,1280]{1,0:T(8,128)(2,1)S(1)}, u32[]{:S(2)}, u32[]{:S(2)}) %collective-permute-start.48) | collective-permute-done | bytes 327712 | tf_op jit(solution)/shard_map/ppermute | solution.py:278
  246.6 2.9 %finish_latent.1 = (f32[160,1280]{1,0:T(8,128)}, f32[160,1280]{1,0:T(8,128)}, f32[160,1280]{1,0:T(8,128)}, f32[32,1280]{1,0:T(8,128)}) custom-call(bf16[128,1280]{1,0:T(8,128)(2,1)} %get-tuple-element.177.refs_0_, bf16[128,1280]{1,0:T(8,128)(2,1)} %copy-done.20, bf16[128,1280]{1,0:T(8,128)(2,1)} %copy-done.18, bf16[128,1280]{1,0:T(8,128)(2,1)} %copy-done.21, ...), custom_call_target="tpu_custom_call" | custom-call | flops 99999997952 | bytes 1024 | tf_op jit(solution)/shard_map/finish_latent/pallas_call | solution.py:302
  252.2 2.6 %finish.1 = (f32[96,256]{1,0:T(8,128)}, f32[96,1280]{1,0:T(8,128)}, f32[160,256]{1,0:T(8,128)}, f32[32,1280]{1,0:T(8,128)}) custom-call(bf16[1280,256]{1,0:T(8,128)(2,1)} %get-tuple-element.162.refs_0_, bf16[32,1280]{1,0:T(8,128)(2,1)} %refs_1_.13, f32[1280]{0:T(1024)} %refs_2_.7, f32[32,1280]{1,0:T(8,128)} %get-tuple-element.182.refs_2_.refs_3_, ...), custom_call_target="tpu_custom_call" | custom-call | flops 99999997952 | bytes 1024 | tf_op jit(solution)/shard_map/finish/pallas_call | solution.py:302
  (188 shorter events, 83.8 us)
Async XLA Ops:
  2.5 14.1 %collective-permute-start = (bf16[896,256]{1,0:T(8,128)(2,1)}, bf16[896,256]{1,0:T(8,128)(2,1)}, u32[]{:S(2)}, u32[]{:S(2)}) collective-permute-start(bf16[896,256]{1,0:T(8,128)(2,1)} %pack.1.refs_3_.refs_2_.refs_1_), channel_id=1, source_target_pairs={{0,2},{1,5},{2,0},{3,7},{4,6},{5,1},{6,4},{7,3},{8,10},{9,13},{10,... | collective-permute-start | bytes 1376264 | tf_op jit(solution)/shard_map/ppermute | solution.py:274
  25.3 17.4 %collective-permute-start.7 = (bf16[480,1280]{1,0:T(8,128)(2,1)}, bf16[480,1280]{1,0:T(8,128)(2,1)}, u32[]{:S(2)}, u32[]{:S(2)}) collective-permute-start(bf16[480,1280]{1,0:T(8,128)(2,1)} %pack_rows.1.refs_2_.refs_7_), channel_id=1, source_target_pairs={{0,1},{1,0},{2,3},{3,2},{4,5},{5,4},{6,7},{7,6},{8,9},{9,8},{10,11... | collective-permute-start | bytes 3686408 | tf_op jit(solution)/shard_map/ppermute | solution.py:270
  25.8 30.6 %collective-permute-start.8 = (bf16[480,1280]{1,0:T(8,128)(2,1)}, bf16[480,1280]{1,0:T(8,128)(2,1)}, u32[]{:S(2)}, u32[]{:S(2)}) collective-permute-start(bf16[480,1280]{1,0:T(8,128)(2,1)} %pack_rows.1.refs_2_.refs_7_), channel_id=1, source_target_pairs={{0,2},{1,5},{2,0},{3,7},{4,6},{5,1},{6,4},{7,3},{8,10},{9,13},{10,... | collective-permute-start | bytes 3686408 | tf_op jit(solution)/shard_map/ppermute | solution.py:274
  28.3 28.1 %collective-permute-start.9 = (bf16[480,1280]{1,0:T(8,128)(2,1)}, bf16[480,1280]{1,0:T(8,128)(2,1)}, u32[]{:S(2)}, u32[]{:S(2)}) collective-permute-start(bf16[480,1280]{1,0:T(8,128)(2,1)} %pack_rows.1.refs_2_.refs_7_), channel_id=1, source_target_pairs={{0,4},{1,3},{2,6},{3,1},{4,0},{5,7},{6,2},{7,5},{8,12},{9,11},{10,... | collective-permute-start | bytes 3686408 | tf_op jit(solution)/shard_map/ppermute | solution.py:274
  61.3 20.9 %collective-permute-start.16 = (bf16[480,1280]{1,0:T(8,128)(2,1)}, bf16[480,1280]{1,0:T(8,128)(2,1)}, u32[]{:S(2)}, u32[]{:S(2)}) collective-permute-start(bf16[480,1280]{1,0:T(8,128)(2,1)} %collective-permute-done.8.refs_9_), channel_id=1, source_target_pairs={{0,4},{1,3},{2,6},{3,1},{4,0},{5,7},{6,2},{7,5},{8,12},{9,11},{10,... | collective-permute-start | bytes 3686408 | tf_op jit(solution)/shard_map/ppermute | solution.py:274
  67.6 14.6 %collective-permute-start.13 = (bf16[64,1408]{1,0:T(8,128)(2,1)}, bf16[64,1408]{1,0:T(8,128)(2,1)S(1)}, u32[]{:S(2)}, u32[]{:S(2)}) collective-permute-start(bf16[64,1408]{1,0:T(8,128)(2,1)} %get-tuple-element.122), channel_id=1, source_target_pairs={{0,2},{1,3},{2,0},{3,1},{4,6},{5,7},{6,4},{7,5},{8,10},{9,11},{10,... | collective-permute-start | bytes 540680 | tf_op jit(solution)/shard_map/ppermute | solution.py:270
  69.3 14.7 %collective-permute-start.14 = (bf16[64,1408]{1,0:T(8,128)(2,1)}, bf16[64,1408]{1,0:T(8,128)(2,1)S(1)}, u32[]{:S(2)}, u32[]{:S(2)}) collective-permute-start(bf16[64,1408]{1,0:T(8,128)(2,1)} %get-tuple-element.123), channel_id=1, source_target_pairs={{0,4},{1,5},{2,6},{3,7},{4,0},{5,1},{6,2},{7,3},{8,12},{9,13},{10,... | collective-permute-start | bytes 540680 | tf_op jit(solution)/shard_map/ppermute | solution.py:270
  70.3 13.7 %collective-permute-start.15 = (bf16[64,1408]{1,0:T(8,128)(2,1)}, bf16[64,1408]{1,0:T(8,128)(2,1)S(1)}, u32[]{:S(2)}, u32[]{:S(2)}) collective-permute-start(bf16[64,1408]{1,0:T(8,128)(2,1)} %get-tuple-element.124), channel_id=1, source_target_pairs={{0,6},{1,7},{2,4},{3,5},{4,2},{5,3},{6,0},{7,1},{8,14},{9,15},{10,... | collective-permute-start | bytes 540680 | tf_op jit(solution)/shard_map/ppermute | solution.py:270
  114.0 11.9 %collective-permute-start.28 = (bf16[4,3,64,160]{3,2,1,0:T(8,128)(2,1)}, bf16[4,3,64,160]{3,2,1,0:T(8,128)(2,1)S(1)}, u32[]{:S(2)}, u32[]{:S(2)}) collective-permute-start(bf16[4,3,64,160]{3,2,1,0:T(8,128)(2,1)} %get-tuple-element.141), channel_id=1, source_target_pairs={{0,1},{1,0},{2,3},{3,2},{4,5},{5,4},{6,7},{7,6},{8,9},{9,8},{10,11... | collective-permute-start | bytes 737288 | tf_op jit(solution)/shard_map/ppermute | solution.py:270
  114.5 14.1 %collective-permute-start.25 = (bf16[3,64,1280]{2,1,0:T(8,128)(2,1)}, bf16[3,64,1280]{2,1,0:T(8,128)(2,1)}, u32[]{:S(2)}, u32[]{:S(2)}) collective-permute-start(bf16[3,64,1280]{2,1,0:T(8,128)(2,1)} %get-tuple-element.140.refs_8_), channel_id=1, source_target_pairs={{0,2},{1,5},{2,0},{3,7},{4,6},{5,1},{6,4},{7,3},{8,10},{9,13},{10,... | collective-permute-start | bytes 1474568 | tf_op jit(solution)/shard_map/ppermute | solution.py:274
  115.7 12.9 %collective-permute-start.26 = (bf16[3,64,1280]{2,1,0:T(8,128)(2,1)}, bf16[3,64,1280]{2,1,0:T(8,128)(2,1)S(1)}, u32[]{:S(2)}, u32[]{:S(2)}) collective-permute-start(bf16[3,64,1280]{2,1,0:T(8,128)(2,1)} %get-tuple-element.140.refs_8_), channel_id=1, source_target_pairs={{0,4},{1,3},{2,6},{3,1},{4,0},{5,7},{6,2},{7,5},{8,12},{9,11},{10,... | collective-permute-start | bytes 1474568 | tf_op jit(solution)/shard_map/ppermute | solution.py:274
  116.4 12.1 %collective-permute-start.27 = (bf16[3,64,1280]{2,1,0:T(8,128)(2,1)}, bf16[3,64,1280]{2,1,0:T(8,128)(2,1)S(1)}, u32[]{:S(2)}, u32[]{:S(2)}) collective-permute-start(bf16[3,64,1280]{2,1,0:T(8,128)(2,1)} %get-tuple-element.140.refs_8_), channel_id=1, source_target_pairs={{0,1},{1,0},{2,3},{3,2},{4,5},{5,4},{6,7},{7,6},{8,9},{9,8},{10,11... | collective-permute-start | bytes 1474568 | tf_op jit(solution)/shard_map/ppermute | solution.py:270
  128.6 15.3 %collective-permute-start.29 = (bf16[3,64,1280]{2,1,0:T(8,128)(2,1)}, bf16[3,64,1280]{2,1,0:T(8,128)(2,1)}, u32[]{:S(2)}, u32[]{:S(2)}) collective-permute-start(bf16[3,64,1280]{2,1,0:T(8,128)(2,1)} %collective-permute-done.25.refs_10_), channel_id=1, source_target_pairs={{0,4},{1,3},{2,6},{3,1},{4,0},{5,7},{6,2},{7,5},{8,12},{9,11},{10,... | collective-permute-start | bytes 1474568 | tf_op jit(solution)/shard_map/ppermute | solution.py:274
  130.1 13.8 %collective-permute-start.30 = (bf16[3,64,1280]{2,1,0:T(8,128)(2,1)}, bf16[3,64,1280]{2,1,0:T(8,128)(2,1)}, u32[]{:S(2)}, u32[]{:S(2)}) collective-permute-start(bf16[3,64,1280]{2,1,0:T(8,128)(2,1)} %collective-permute-done.25.refs_10_), channel_id=1, source_target_pairs={{0,1},{1,0},{2,3},{3,2},{4,5},{5,4},{6,7},{7,6},{8,9},{9,8},{10,11... | collective-permute-start | bytes 1474568 | tf_op jit(solution)/shard_map/ppermute | solution.py:270
  132.0 19.6 %collective-permute-start.32 = (bf16[2,3,64,160]{3,2,1,0:T(8,128)(2,1)}, bf16[2,3,64,160]{3,2,1,0:T(8,128)(2,1)}, u32[]{:S(2)}, u32[]{:S(2)}) collective-permute-start(bf16[2,3,64,160]{3,2,1,0:T(8,128)(2,1)} %get-tuple-element.144.refs_13_), channel_id=1, source_target_pairs={{0,2},{1,3},{2,0},{3,1},{4,6},{5,7},{6,4},{7,5},{8,10},{9,11},{10,... | collective-permute-start | bytes 368648 | tf_op jit(solution)/shard_map/ppermute | solution.py:270
  132.7 19.0 %collective-permute-start.33 = (bf16[2,3,64,160]{3,2,1,0:T(8,128)(2,1)}, bf16[2,3,64,160]{3,2,1,0:T(8,128)(2,1)}, u32[]{:S(2)}, u32[]{:S(2)}) collective-permute-start(bf16[2,3,64,160]{3,2,1,0:T(8,128)(2,1)} %get-tuple-element.154), channel_id=1, source_target_pairs={{0,4},{1,5},{2,6},{3,7},{4,0},{5,1},{6,2},{7,3},{8,12},{9,13},{10,... | collective-permute-start | bytes 368648 | tf_op jit(solution)/shard_map/ppermute | solution.py:270
  133.7 18.0 %collective-permute-start.34 = (bf16[2,3,64,160]{3,2,1,0:T(8,128)(2,1)}, bf16[2,3,64,160]{3,2,1,0:T(8,128)(2,1)}, u32[]{:S(2)}, u32[]{:S(2)}) collective-permute-start(bf16[2,3,64,160]{3,2,1,0:T(8,128)(2,1)} %get-tuple-element.155), channel_id=1, source_target_pairs={{0,6},{1,7},{2,4},{3,5},{4,2},{5,3},{6,0},{7,1},{8,14},{9,15},{10,... | collective-permute-start | bytes 368648 | tf_op jit(solution)/shard_map/ppermute | solution.py:270
  158.9 17.5 %collective-permute-start.40 = (bf16[128,1280]{1,0:T(8,128)(2,1)}, bf16[128,1280]{1,0:T(8,128)(2,1)}, u32[]{:S(2)}, u32[]{:S(2)}) collective-permute-start(bf16[128,1280]{1,0:T(8,128)(2,1)} %get-tuple-element.168), channel_id=1, source_target_pairs={{0,8},{8,0},{16,24},{24,16},{1,9},{9,1},{17,25},{25,17},{2,10},{10... | collective-permute-start | bytes 983048 | tf_op jit(solution)/shard_map/ppermute | solution.py:278
  160.5 15.8 %collective-permute-start.41 = (bf16[128,1280]{1,0:T(8,128)(2,1)}, bf16[128,1280]{1,0:T(8,128)(2,1)}, u32[]{:S(2)}, u32[]{:S(2)}) collective-permute-start(bf16[128,1280]{1,0:T(8,128)(2,1)} %get-tuple-element.169), channel_id=1, source_target_pairs={{0,8},{8,0},{16,24},{24,16},{1,9},{9,1},{17,25},{25,17},{2,10},{10... | collective-permute-start | bytes 983048 | tf_op jit(solution)/shard_map/ppermute | solution.py:278
  165.2 15.9 %collective-permute-start.37 = (bf16[768,256]{1,0:T(8,128)(2,1)}, bf16[768,256]{1,0:T(8,128)(2,1)}, u32[]{:S(2)}, u32[]{:S(2)}) collective-permute-start(bf16[768,256]{1,0:T(8,128)(2,1)} %get-tuple-element.163), channel_id=1, source_target_pairs={{0,2},{1,3},{2,0},{3,1},{4,6},{5,7},{6,4},{7,5},{8,10},{9,11},{10,... | collective-permute-start | bytes 1179656 | tf_op jit(solution)/shard_map/ppermute | solution.py:270
  165.9 19.6 %collective-permute-start.38 = (bf16[768,256]{1,0:T(8,128)(2,1)}, bf16[768,256]{1,0:T(8,128)(2,1)}, u32[]{:S(2)}, u32[]{:S(2)}) collective-permute-start(bf16[768,256]{1,0:T(8,128)(2,1)} %get-tuple-element.164), channel_id=1, source_target_pairs={{0,4},{1,5},{2,6},{3,7},{4,0},{5,1},{6,2},{7,3},{8,12},{9,13},{10,... | collective-permute-start | bytes 1179656 | tf_op jit(solution)/shard_map/ppermute | solution.py:270
  166.9 18.5 %collective-permute-start.39 = (bf16[768,256]{1,0:T(8,128)(2,1)}, bf16[768,256]{1,0:T(8,128)(2,1)}, u32[]{:S(2)}, u32[]{:S(2)}) collective-permute-start(bf16[768,256]{1,0:T(8,128)(2,1)} %get-tuple-element.165), channel_id=1, source_target_pairs={{0,6},{1,7},{2,4},{3,5},{4,2},{5,3},{6,0},{7,1},{8,14},{9,15},{10,... | collective-permute-start | bytes 1179656 | tf_op jit(solution)/shard_map/ppermute | solution.py:270
  178.6 17.4 %collective-permute-start.45 = (bf16[128,1280]{1,0:T(8,128)(2,1)}, bf16[128,1280]{1,0:T(8,128)(2,1)S(1)}, u32[]{:S(2)}, u32[]{:S(2)}) collective-permute-start(bf16[128,1280]{1,0:T(8,128)(2,1)} %get-tuple-element.176), channel_id=1, source_target_pairs={{0,16},{8,24},{16,0},{24,8},{1,17},{9,25},{17,1},{25,9},{2,18},{10... | collective-permute-start | bytes 983048 | tf_op jit(solution)/shard_map/ppermute | solution.py:278
  189.2 11.8 %collective-permute-start.42 = (bf16[192,256]{1,0:T(8,128)(2,1)}, bf16[192,256]{1,0:T(8,128)(2,1)S(1)}, u32[]{:S(2)}, u32[]{:S(2)}) collective-permute-start(bf16[192,256]{1,0:T(8,128)(2,1)} %get-tuple-element.172), channel_id=1, source_target_pairs={{0,8},{8,0},{16,24},{24,16},{1,9},{9,1},{17,25},{25,17},{2,10},{10... | collective-permute-start | bytes 294920 | tf_op jit(solution)/shard_map/ppermute | solution.py:278
  203.8 17.7 %collective-permute-start.49 = (bf16[192,256]{1,0:T(8,128)(2,1)}, bf16[192,256]{1,0:T(8,128)(2,1)S(1)}, u32[]{:S(2)}, u32[]{:S(2)}) collective-permute-start(bf16[192,256]{1,0:T(8,128)(2,1)} %get-tuple-element.179), channel_id=1, source_target_pairs={{0,16},{8,24},{16,0},{24,8},{1,17},{9,25},{17,1},{25,9},{2,18},{10... | collective-permute-start | bytes 294920 | tf_op jit(solution)/shard_map/ppermute | solution.py:278
  205.5 16.0 %collective-permute-start.50 = (f32[8,1280]{1,0:T(8,128)}, f32[8,1280]{1,0:T(8,128)S(1)}, u32[]{:S(2)}, u32[]{:S(2)}) collective-permute-start(f32[8,1280]{1,0:T(8,128)} %get-tuple-element.180.refs_2_), channel_id=1, source_target_pairs={{0,16},{8,24},{16,0},{24,8},{1,17},{9,25},{17,1},{25,9},{2,18},{10... | collective-permute-start | bytes 122888 | tf_op jit(solution)/shard_map/ppermute | solution.py:278
  206.7 20.9 %collective-permute-start.47 = (bf16[128,1280]{1,0:T(8,128)(2,1)}, bf16[128,1280]{1,0:T(8,128)(2,1)S(1)}, u32[]{:S(2)}, u32[]{:S(2)}) collective-permute-start(bf16[128,1280]{1,0:T(8,128)(2,1)} %get-tuple-element.177.refs_0_), channel_id=1, source_target_pairs={{0,16},{8,24},{16,0},{24,8},{1,17},{9,25},{17,1},{25,9},{2,18},{10... | collective-permute-start | bytes 983048 | tf_op jit(solution)/shard_map/ppermute | solution.py:278
  223.8 13.1 %collective-permute-start.46 = (bf16[128,1280]{1,0:T(8,128)(2,1)S(1)}, bf16[128,1280]{1,0:T(8,128)(2,1)S(1)}, u32[]{:S(2)}, u32[]{:S(2)}) collective-permute-start(bf16[128,1280]{1,0:T(8,128)(2,1)S(1)} %copy-done.17), channel_id=1, source_target_pairs={{0,8},{8,0},{16,24},{24,16},{1,9},{9,1},{17,25},{25,17},{2,10},{10... | collective-permute-start | bytes 983048 | tf_op jit(solution)/shard_map/ppermute | solution.py:278
  226.1 26.1 %collective-permute-start.52 = (bf16[192,256]{1,0:T(8,128)(2,1)}, bf16[192,256]{1,0:T(8,128)(2,1)}, u32[]{:S(2)}, u32[]{:S(2)}) collective-permute-start(bf16[192,256]{1,0:T(8,128)(2,1)} %get-tuple-element.183.refs_4_), channel_id=1, source_target_pairs={{0,8},{8,0},{16,24},{24,16},{1,9},{9,1},{17,25},{25,17},{2,10},{10... | collective-permute-start | bytes 294920 | tf_op jit(solution)/shard_map/ppermute | solution.py:278
  227.6 18.2 %collective-permute-start.48 = (bf16[128,1280]{1,0:T(8,128)(2,1)S(1)}, bf16[128,1280]{1,0:T(8,128)(2,1)S(1)}, u32[]{:S(2)}, u32[]{:S(2)}) collective-permute-start(bf16[128,1280]{1,0:T(8,128)(2,1)S(1)} %collective-permute-done.47.refs_2_), channel_id=1, source_target_pairs={{0,8},{8,0},{16,24},{24,16},{1,9},{9,1},{17,25},{25,17},{2,10},{10... | collective-permute-start | bytes 983048 | tf_op jit(solution)/shard_map/ppermute | solution.py:278
  230.2 19.3 %collective-permute-start.55 = (f32[8,1280]{1,0:T(8,128)}, f32[8,1280]{1,0:T(8,128)S(1)}, u32[]{:S(2)}, u32[]{:S(2)}) collective-permute-start(f32[8,1280]{1,0:T(8,128)} %nsum.2.refs_4_.refs_0_), channel_id=1, source_target_pairs={{0,2},{1,3},{2,0},{3,1},{4,6},{5,7},{6,4},{7,5},{8,10},{9,11},{10,... | collective-permute-start | bytes 122888 | tf_op jit(solution)/shard_map/ppermute | solution.py:270
  234.2 18.0 %collective-permute-start.54 = (bf16[192,256]{1,0:T(8,128)(2,1)}, bf16[192,256]{1,0:T(8,128)(2,1)}, u32[]{:S(2)}, u32[]{:S(2)}) collective-permute-start(bf16[192,256]{1,0:T(8,128)(2,1)} %collective-permute-done.53.refs_6_), channel_id=1, source_target_pairs={{0,8},{8,0},{16,24},{24,16},{1,9},{9,1},{17,25},{25,17},{2,10},{10... | collective-permute-start | bytes 294920 | tf_op jit(solution)/shard_map/ppermute | solution.py:278
  (65 other events, 284.1 us)

commit v3 on v2

--- a/solution.py
+++ b/solution.py
@@ -255,7 +255,7 @@
 F32 = jnp.float32
 N = 8
 NZ = 4
-COST = pl.CostEstimate(flops=100_000_000_000, bytes_accessed=1024, transcendentals=0)
+COST = 100_000_000_000
 LOG2E = 1.4426950408889634
 ANY = pl.BlockSpec(memory_space=pl.ANY)
 VMEM = pl.BlockSpec(memory_space=pltpu.VMEM)
@@ -293,23 +293,23 @@
     return me ^ jnp.where((me & 1) == 0, even, odd)
 
 
-def call(body, out, ins, specs, scratch=(), name=None, grid=(), deps=(), out_specs=None, aliases=None):
-    n, skip = len(ins), len(deps)
+def call(body, out, ins, specs, scratch=(), name=None, grid=(), deps=(), out_specs=None, aliases=None, cost=COST, lead=()):
+    n, skip, ahead = len(ins), len(deps), len(lead)
 
     def run(*refs):
-        return body(*refs[:n], *refs[n + skip :])
+        return body(*refs[ahead : ahead + n], *refs[ahead + n + skip :])
 
     return pl.pallas_call(
         run,
         grid=grid,
         out_shape=out,
-        in_specs=list(specs) + [ANY] * skip,
+        in_specs=[ANY] * ahead + list(specs) + [ANY] * skip,
         out_specs=jax.tree.map(lambda _: VMEM, out) if out_specs is None else out_specs,
         scratch_shapes=list(scratch),
         input_output_aliases=aliases or {},
         name=name,
-        cost_estimate=COST,
-    )(*ins, *deps)
+        cost_estimate=pl.CostEstimate(flops=cost, bytes_accessed=1024, transcendentals=0),
+    )(*lead, *ins, *deps)
 
 
 def sds(shape, dtype):
@@ -522,20 +522,17 @@
                 theirs_o[kk, n] = v[:, cols]
 
 
-def stack_kernel(mine, other, *outs):
-    for kk in range(1, 4):
-        outs[kk - 1][0] = mine[kk]
-        outs[kk - 1][1] = other[kk]
-
-
 def backward_kernel(s, k, vt, q, e, *rest):
-    pieces, rest = rest[:N], rest[N + s :]
-    dkvt_o, dq_o = rest[:2]
-    dabx, dabt, qt, sem = rest[2:]
+    pieces = rest[:N]
+    dkvt_o, dq_o, dabx, dabt, qt, sem = rest[-6:] if s else (*rest[N + 2 : N + 4], *rest[-4:])
     me, _ = me_z()
     handles = run_copies(
         [(p.at[pl.ds(32 * s, 32), :], dabx.at[rows_of(owner(me, rel), 32), :]) for p, rel in zip(pieces, DIRECT)], sem
     )
+    if s == 0:
+        for kk in range(1, 4):
+            for n in range(2):
+                rest[N + 3 + kk][n] = rest[N + n][kk]
     qt[...] = q[...].T
     dq_o[...] = jnp.zeros_like(dq_o)
     wait_all(handles)
@@ -584,12 +581,14 @@
 
 
 def sum_slots_kernel(a, b, c, d, wk, wv, wq, bg, qg, mix, *rest):
-    outs, norm_o, acc = rest[:NZ], rest[NZ], rest[NZ + 1]
+    near_o, far_o, send_o, acc = rest
     me, zi = me_z()
     total = (a[...].astype(F32) + b[...].astype(F32)) + (c[...].astype(F32) + d[...].astype(F32))
     acc[...] = total.astype(BF)
-    for r in range(NZ):
-        outs[r][...] = acc[rows_of(zi ^ r, 192), :]
+    near_o[...] = acc[rows_of(zi, 192), :]
+    far_o[...] = acc[rows_of(zi ^ 2, 192), :]
+    send_o[0:192, :] = acc[rows_of(zi ^ 1, 192), :]
+    send_o[192:384, :] = acc[rows_of(zi ^ 3, 192), :]
     prod = total[0:96] * wk[...].astype(F32)
     for n in range(5):
         prod += total[96 * (n + 1) : 96 * (n + 2)] * wv[:, 256 * n : 256 * (n + 1)].astype(F32)
@@ -598,16 +597,10 @@
         (mix[...], 160),
         (row_sums(total[576:736] * wq[...].astype(F32)) / own_part(qg[...], me, 160), 160),
     )
-    row = lax.broadcasted_iota(jnp.int32, (8, 1280), 0)
-    placed = jnp.zeros((8, 1280), F32)
-    for n, (v, size) in enumerate(parts):
-        at = lax.broadcasted_iota(jnp.int32, (size, 1280), 1)
-        pick = (at == lax.broadcasted_iota(jnp.int32, (size, 1280), 0) + size * me).astype(F32)
-        wide = lax.dot_general(
-            v, pick, (((1,), (0,)), ((), ())), precision=lax.Precision.HIGHEST, preferred_element_type=F32
-        )
-        placed = jnp.where(row == n, wide, placed)
-    norm_o[...] = placed
+    padded = [v if size == 160 else jnp.concatenate([v, jnp.zeros((8, 160 - size), F32)], axis=1) for v, size in parts]
+    joined = jnp.concatenate(padded + [jnp.zeros((8, 32), F32)], axis=1)
+    placed = jnp.where(lax.broadcasted_iota(jnp.int32, (8, 512), 0) == me, joined, 0.0)
+    send_o[384:400, :] = jnp.concatenate([placed[:, 0:256], placed[:, 256:512]], axis=0).astype(BF)
 
 
 def bytes_kernel(x, bg, wk, wv, dkvt, *rest):
@@ -617,7 +610,8 @@
     out[...] = ln_back(dxn, hat, inverse, bg[...][None, :])
 
 
-def latent_grads_kernel(init, wup, mg, amine, at, b1, b2, b3, *rest):
+def latent_grads_kernel(init, wup, mg, *rest):
+    (amine, at, b1, b2, b3), rest = rest[N : N + 5], rest[:N] + rest[N + 5 :]
     rows, outs, mix_o, (xs, ys, acc, sem) = rest[:N], rest[N : N + 4], rest[N + 4], rest[N + 5 :]
     me, zi = me_z()
     copies = []
@@ -668,11 +662,41 @@
     init_o[...] = init[...] + ln_back(dzn, hat, inverse, qg[...][None, :])
 
 
-def norms_kernel(a, b, byte_o, mixer_o, query_o):
-    total = a[...] + b[...]
-    row = lax.broadcasted_iota(jnp.int32, (8, 1280), 0)
-    for n, out in enumerate((byte_o, mixer_o, query_o)):
-        out[...] = jnp.sum(jnp.where(row == n, total, 0.0), axis=0)[: out.shape[0]]
+def norms_kernel(a, b, c, d, *outs):
+    both = (a[...].astype(F32) + b[...].astype(F32)) + (c[...].astype(F32) + d[...].astype(F32))
+    total = jnp.concatenate([both[0:8], both[8:16]], axis=1)
+    for n, (out, size) in enumerate(zip(outs, (96, 160, 160))):
+        width = out.shape[0]
+        at = lax.broadcasted_iota(jnp.int32, (160, width), 1)
+        pick = (at % size == lax.broadcasted_iota(jnp.int32, (160, width), 0)).astype(F32)
+        wide = lax.dot_general(
+            total[:, 160 * n : 160 * (n + 1)],
+            pick,
+            (((1,), (0,)), ((), ())),
+            precision=lax.Precision.HIGHEST,
+            preferred_element_type=F32,
+        )
+        mine = lax.broadcasted_iota(jnp.int32, (8, width), 0) == lax.broadcasted_iota(jnp.int32, (8, width), 1) // size
+        out[...] = jnp.sum(jnp.where(mine, wide, 0.0), axis=0)
+
+
+def plus(a, b):
+    return (a.astype(F32) + b.astype(F32)).astype(BF)
+
+
+def sum_of_three_kernel(a, b, c, out):
+    out[...] = (a[...].astype(F32) + b[...].astype(F32) + c[...].astype(F32)).astype(BF)
+
+
+def first_zq_kernel(near, far, mine, got, near_o, far_o):
+    near_o[...] = plus(near[...], got[0:192, :])
+    far_o[0:192, :] = plus(far[...], got[192:384, :])
+    far_o[192:208, :] = plus(mine[384:400, :], got[384:400, :])
+
+
+def second_zq_kernel(near, mine, got, near_o, norm_o):
+    near_o[...] = plus(near[...], got[0:192, :])
+    norm_o[...] = plus(mine[192:208, :], got[192:208, :])
 
 
 def sums_of_pairs_kernel(*refs):
@@ -682,10 +706,10 @@
         out[...] = (a[...].astype(F32) + b[...].astype(F32)).astype(out.dtype)
 
 
-def sums_of_pairs(pairs, name, deps=()):
+def sums_of_pairs(pairs, name, deps=(), cost=COST):
     flat = [x for pair in pairs for x in pair]
     out = [sds(a.shape, a.dtype) for a, _ in pairs]
-    return call(sums_of_pairs_kernel, out, flat, [VMEM] * len(flat), name=name, deps=deps)
+    return call(sums_of_pairs_kernel, out, flat, [VMEM] * len(flat), name=name, deps=deps, cost=cost)
 
 
 def part(f, *args):
@@ -730,13 +754,13 @@
         pack_rows_kernel, sds((480, 1280), BF), (out_weight, up_weight, down_weight), [VMEM] * 3, name="pack_rows", deps=(packed,)
     )
     xn = call(norm_kernel, sds((1024, 768), BF), (x, byte_gain), [VMEM] * 2, name="norm", deps=(wcat,))
-    pa, pb, xn, near = tie(pa, pb, xn, packed)
+    pa, pb, xn, near, wcat = tie(pa, pb, xn, packed, wcat)
+    wa = send_split(wcat, 2, 4)
     pd = send_split(pa, 4, 2)
     pn, pna, pnb = send(near, 1), send(pa, 1), send(pb, 1)
-    pd, wcat = tie(pd, wcat)
+    pd, pn, wcat = tie(pd, pn, wcat)
     pnd = send(pd, 1)
-    wa, wb = first(wcat)
-    wn = send(wcat, 1)
+    wb = send_split(wcat, 4, 2)
     pieces = (packed, pn, pa, pb, pd, pna, pnb, pnd)
     k, wk, wq_full, q, zn = call(
         query_kernel,
@@ -746,6 +770,8 @@
         [pltpu.VMEM((256, 1280), BF), pltpu.SemaphoreType.DMA((7 * N,))],
         name="query",
     )
+    q, wcat = tie(q, wcat)
+    wn = send(wcat, 1)
     e, ll = call(
         scores_kernel,
         (sds((2, 8, 256, 512), BF), sds((2, 256, 128), F32)),
@@ -780,17 +806,17 @@
             grid=(1,),
         )
 
+    vt, wa, wb = tie(vt, wa, wb)
     mine, theirs = sums(0)
-    mine, wa, wb = tie(mine, wa, wb)
     wd = send_split(wa, 4, 2)
     wna, wnb = send(wa, 1), send(wb, 1)
     mine, theirs = sums(1, mine, theirs)
     got = send(theirs, 1)
     m0, m1, m2, m3 = call(
-        add4_kernel, (sds((64, 1408), BF),) * 4, (mine, got), [VMEM] * 2, name="add4", deps=(wna, wnb)
+        add4_kernel, (sds((64, 1408), BF),) * 4, (mine, got), [VMEM] * 2, name="add4", deps=(wna, wnb), cost=1024
     )
     r1, r2, r3 = send(m1, 2), send(m2, 4), send(m3, 6)
-    r1, r2, r3, wd = tie(r1, r2, r3, wd)
+    m0, wd = tie(m0, wd)
     wnd = send(wd, 1)
     latents, agb, amine, atheirs, dabx, init = call(
         latent_kernel,
@@ -811,38 +837,37 @@
     ga, gb = first(agb)
     gn = send(agb, 1)
 
-    def backward(s, *prev):
+    def backward(s, *extra, deps=()):
+        both = [sds((2, 3, 64, 160), BF)] * (0 if s else 3)
         return call(
             part(backward_kernel, s),
-            (sds((1536, 1024), BF), sds((256, 256), F32)),
-            (k, vt, q, e, *dab_p, *prev),
+            (sds((1536, 1024), BF), sds((256, 256), F32), *both),
+            (k, vt, q, e, *dab_p, *extra),
             [
                 pl.BlockSpec((512, 256), lambda g: (s, 0)),
                 pl.BlockSpec((1280, 512), lambda g: (0, s)),
                 VMEM,
                 pl.BlockSpec((None, 8, 256, 512), lambda g: (s, 0, 0, 0)),
             ]
-            + [ANY] * (N + len(prev)),
+            + [ANY] * N + [ANY if s else VMEM] * len(extra),
             [
                 pltpu.VMEM((256, 1408), BF), pltpu.VMEM((1280, 256), BF), pltpu.VMEM((256, 256), BF),
                 pltpu.SemaphoreType.DMA((N,)),
             ],
-            out_specs=(pl.BlockSpec((1536, 512), lambda g: (0, s)), VMEM),
-            aliases={4 + N: 0} if prev else {},
+            out_specs=(pl.BlockSpec((1536, 512), lambda g: (0, s)), VMEM, *[VMEM] * len(both)),
+            aliases={4 + N: 0} if s else {},
             name="backward",
             grid=(1,),
-            deps=deps_of[s],
+            deps=deps,
+            cost=1024 if s else COST,
         )
 
-    deps_of = {0: ()}
-    dkvt, dq0 = backward(0)
-    dq0, ga, gb, gn, at = tie(dq0, ga, gb, gn, at)
+    dkvt, dq0, *both = backward(0, amine, at)
+    dq0, ga, gb, gn = tie(dq0, ga, gb, gn)
     gd = send_split(ga, 4, 2)
     gna = send(ga, 1)
-    both = call(stack_kernel, (sds((2, 3, 64, 160), BF),) * 3, (amine, at), [VMEM] * 2, name="stack", deps=(dq0,))
     both_s = [send(b, 2 * kk + 2) for kk, b in enumerate(both)]
-    deps_of[1] = (both[0], dq0)
-    dkvt, dq1 = backward(1, dkvt)
+    dkvt, dq1 = backward(1, dkvt, deps=(dq0,))
     dq1, gd, gna, gb = tie(dq1, gd, gna, gb)
     gnb, gnd = send(gb, 1), send(gd, 1)
     gmine, gtheirs = call(
@@ -862,7 +887,7 @@
     *oud, mix = call(
         latent_grads_kernel,
         (sds((128, 1280), BF),) * NZ + (sds((8, 160), F32),),
-        (init, up_weight, mixer_gain, amine, at, *both_s, agb, gn, ga, gb, gd, gna, gnb, gnd),
+        (init, up_weight, mixer_gain, agb, gn, ga, gb, gd, gna, gnb, gnd, amine, at, *both_s),
         [VMEM] * 3 + [ANY] * (5 + N),
         [
             pltpu.VMEM((3, 512, 160), BF), pltpu.VMEM((3, 512, 1280), BF), pltpu.VMEM((512, 1280), BF),
@@ -871,9 +896,12 @@
         name="latent_grads",
         deps=(gtheirs,),
     )
-    o3, o1 = send_z(oud[3], 1), send_z(oud[1], 1)
+    o3 = send_z(oud[3], 1)
     gm = call(add4_kernel, (sds((768, 256), BF),) * 4, (gmine, gg), [VMEM] * 2, name="add4g", deps=(oud[0],))
     g1, g2, g3 = send(gm[1], 2), send(gm[2], 4), send(gm[3], 6)
+    (ofar,) = sums_of_pairs(((oud[2], o3),), "osum", deps=(gm[0],))
+    ofar, o1 = tie(ofar, oud[1])
+    o22, o1 = send_z(ofar, 2), send_z(o1, 1)
     byte_grads = call(
         bytes_kernel,
         sds((2, 512, 768), F32),
@@ -888,56 +916,76 @@
         out_specs=pl.BlockSpec((None, 256, 768), lambda b: (b // 2, b % 2, 0)),
         name="bytes",
         grid=(4,),
-        deps=(gm[0],),
-    )
-    o2, o0 = sums_of_pairs(((oud[2], o3), (oud[0], o1)), "osum", deps=(byte_grads,))
-    o22 = send_z(o2, 2)
-    *gq, norm = call(
+        deps=(ofar,),
+        cost=1024,
+    )
+    qnear, qfar, qsend = call(
         sum_slots_kernel,
-        (sds((192, 256), BF),) * NZ + (sds((8, 1280), F32),),
+        (sds((192, 256), BF), sds((192, 256), BF), sds((400, 256), BF)),
         (gm[0], g1, g2, g3, key_weight, value_weight, query_weight, byte_gain, query_gain, mix),
         [VMEM] * 10,
         [pltpu.VMEM((768, 256), BF)],
         name="gsum",
-        deps=(o0,),
-    )
-    q3, q1, n1 = send_z(gq[3], 1), send_z(gq[1], 1), send_z(norm, 1)
-    q2, q0, norm, ototal = sums_of_pairs(((gq[2], q3), (gq[0], q1), (norm, n1), (o0, o22)), "qsum")
-    ofar, onear = send_z(ototal, 2), send_z(ototal, 1)
-    q22, n2 = send_z(q2, 2), send_z(norm, 2)
-    qtotal, norm = sums_of_pairs(((q0, q22), (norm, n2)), "qtotal")
-    qfar, qnear, n3 = send_z(qtotal, 2), send_z(qtotal, 1), send(norm, 1)
-    ofar2 = send_z(ofar, 1)
-    (norm,) = sums_of_pairs(((norm, n3),), "nsum")
-    n4 = send(norm, 2)
-    qfar2 = send_z(qfar, 1)
+        deps=(byte_grads,),
+    )
+    qgot = send_z(qsend, 1)
+    ototal = call(
+        sum_of_three_kernel, sds((128, 1280), BF), (oud[0], o1, o22), [VMEM] * 3, name="ototal", lead=(qnear,)
+    )
+    o2 = send_z(ototal, 2)
+    qnear, qfar = call(
+        first_zq_kernel,
+        (sds((192, 256), BF), sds((208, 256), BF)),
+        (qnear, qfar, qsend, qgot),
+        [VMEM] * 4,
+        name="qsum",
+        deps=(ototal,),
+    )
+    qfar, oshare = tie(qfar, ototal)
+    qgot, o1 = send_z(qfar, 2), send_z(oshare, 1)
+    qtotal, norm = call(
+        second_zq_kernel,
+        (sds((192, 256), BF), sds((16, 256), BF)),
+        (qnear, qfar, qgot),
+        [VMEM] * 3,
+        name="qtotal",
+        deps=(o2,),
+        cost=1024,
+    )
+    qtotal, o2 = tie(qtotal, o2)
+    q2, n3 = send_z(qtotal, 2), send(norm, 1)
+    ofar2 = send_z(o2, 1)
+    (norm,) = sums_of_pairs(((norm, n3),), "nsum", cost=1024)
+    norm, qshare = tie(norm, qtotal)
+    q1 = send_z(qshare, 1)
+    n4, n5, n6 = send(norm, 2), send(norm, 4), send(norm, 6)
+    q3 = send_z(q2, 1)
     out_g, up_g, down_g, init_sum = call(
         finish_latent_kernel,
         (sds((160, 1280), F32),) * 3 + (sds((32, 1280), F32),),
-        (ototal, onear, ofar, ofar2),
+        (ototal, o1, o2, ofar2),
         [VMEM] * NZ,
         [pltpu.VMEM((512, 1280), BF)],
         name="finish_latent",
-        deps=(norm,),
-    )
-    (norm,) = sums_of_pairs(((norm, n4),), "nsum", deps=(init_sum,))
-    n5 = send(norm, 4)
+    )
+    byte_n, mixer_n, query_n = call(
+        norms_kernel,
+        (sds((768,), F32), sds((1280,), F32), sds((1280,), F32)),
+        (norm, n4, n5, n6),
+        [VMEM] * 4,
+        name="norms",
+        deps=(init_sum,),
+        cost=1024,
+    )
     key_g, value_g, query_g, init_g = call(
         finish_kernel,
         (sds((96, 256), F32), sds((96, 1280), F32), sds((160, 256), F32), sds((32, 1280), F32)),
-        (wq_full, latent_init, query_gain, init_sum, qtotal, qnear, qfar, qfar2),
+        (wq_full, latent_init, query_gain, init_sum, qtotal, q1, q2, q3),
         [VMEM] * (4 + NZ),
         [pltpu.VMEM((768, 256), BF)],
         name="finish",
-        deps=(norm,),
-    )
-    byte_n, mixer_n, query_n = call(
-        norms_kernel,
-        (sds((768,), F32), sds((1280,), F32), sds((1280,), F32)),
-        (norm, n5),
-        [VMEM] * 2,
-        name="norms",
-        deps=(init_g,),
+        deps=(byte_n,),
+        cost=1024,
     )
     return (
         latents.reshape(seqs, own, DL),

time: 259 us -> 235 us (0.907)
  waiting for transfers between devices: 79.8 us -> 55.6 us
    ppermute x14 -> x11, waiting for transfers between devices: 34.5 us -> 15.4 us  [send_z(): return lax.ppermute(x, 'rep', [(i, i ^ k) for i in range(NZ)])]
    ppermute x9, waiting for transfers between devices: 25.4 us -> 18.4 us  [send_split(): lax.ppermute(x, 'fsdp', [(i, i ^ (odd if i & 1 else even)) for i in range...]
    unnamed x80 -> x98, local copies, waits for them, and re-layouts: 11.5 us -> 13.7 us
    ppermute x34 -> x35, waiting for transfers between devices: 19.9 us -> 21.7 us  [send(): return lax.ppermute(x, 'fsdp', [(i, i ^ k) for i in range(N)])]
    pallas_call x26 -> x25, Pallas kernels: 111 us -> 110 us  [call(): pl.pallas_call(run, grid=grid, out_shape=out, in_specs=[ANY] * ahead + li...]
    ppermute x34 -> x35, starting transfers between devices: 21.5 us -> 20.9 us  [send(): return lax.ppermute(x, 'fsdp', [(i, i ^ k) for i in range(N)])]
    ppermute x14 -> x11, starting transfers between devices: 18.7 us -> 19.2 us  [send_z(): return lax.ppermute(x, 'rep', [(i, i ^ k) for i in range(NZ)])]
  transfers between devices with their start and end apart: 57 -> 55, of which waited for: 18 -> 20; matrix products, arithmetic and copies ran while one was open for 0% -> 0% of each run, Pallas kernels for 37% -> 40%
where the time goes in v3:
time: 235 us; the launch traced here: 234 us
  Pallas kernels  110 us (47%)
  waiting for transfers between devices  55.6 us (24%)
  starting transfers between devices  54.1 us (23%)
  local copies, waits for them, and re-layouts  13.7 us (6%)
    pallas_call x25, Pallas kernels, call(): pl.pallas_call(run, grid=grid, out_shape=out, in_specs=[ANY] * ahead + li...  110 us
    ppermute x35, waiting for transfers between devices, send(): return lax.ppermute(x, 'fsdp', [(i, i ^ k) for i in range(N)])  21.7 us
    ppermute x35, starting transfers between devices, send(): return lax.ppermute(x, 'fsdp', [(i, i ^ k) for i in range(N)])  20.9 us
    ppermute x11, starting transfers between devices, send_z(): return lax.ppermute(x, 'rep', [(i, i ^ k) for i in range(NZ)])  19.2 us
    ppermute x9, waiting for transfers between devices, send_split(): lax.ppermute(x, 'fsdp', [(i, i ^ (odd if i & 1 else even)) for i in range...  18.4 us
    ppermute x11, waiting for transfers between devices, send_z(): return lax.ppermute(x, 'rep', [(i, i ^ k) for i in range(NZ)])  15.4 us
    ppermute x9, starting transfers between devices, send_split(): lax.ppermute(x, 'fsdp', [(i, i ^ (odd if i & 1 else even)) for i in range...  14 us
    unnamed x98, local copies, waits for them, and re-layouts  13.7 us
  transfers between devices with their start and end apart: 55, of which 20 were waited for; matrix products, arithmetic and copies ran while one was open for 0% of the time, Pallas kernels for 40%

profile of v3, /device:TPU:0, one launch (start us, length us, event | category | flops | bytes accessed | tf_op | source)
XLA Modules:
  0.0 234.3 jit_solution(16953163896180489356)
XLA Ops:
  2.5 3.0 %collective-permute-start.1 = (bf16[896,256]{1,0:T(8,128)(2,1)}, bf16[896,256]{1,0:T(8,128)(2,1)}, u32[]{:S(2)}, u32[]{:S(2)}) collective-permute-start(bf16[896,256]{1,0:T(8,128)(2,1)} %pack.1.refs_3_.refs_2_.refs_1_), channel_id=1, source_target_pairs={{0,4},{1,3},{2,6},{3,1},{4,0},{5,7},{6,2},{7,5},{8,12},{9,11},{10,... | collective-permute-start | bytes 1376264 | tf_op jit(solution)/shard_map/ppermute | solution.py:274
  9.4 3.7 %norm.1.refs_0_ = bf16[1024,768]{1,0:T(8,128)(2,1)} custom-call(bf16[1024,768]{1,0:T(8,128)(2,1)} %bitcast.3, f32[768]{0:T(1024)} %refs_7_.1, bf16[480,1280]{1,0:T(8,128)(2,1)} %pack_rows.1.refs_2_.refs_7_), custom_call_target="tpu_custom_call" | custom-call | flops 99999997952 | bytes 1024 | tf_op jit(solution)/shard_map/norm/pallas_call | solution.py:302
  13.0 3.6 %collective-permute-done.1.refs_5_.refs_4_ = bf16[896,256]{1,0:T(8,128)(2,1)} collective-permute-done((bf16[896,256]{1,0:T(8,128)(2,1)}, bf16[896,256]{1,0:T(8,128)(2,1)}, u32[]{:S(2)}, u32[]{:S(2)}) %collective-permute-start.1) | collective-permute-done | bytes 458784 | tf_op jit(solution)/shard_map/ppermute | solution.py:274
  19.8 6.1 %collective-permute-done.2.refs_6_.refs_5_ = bf16[896,256]{1,0:T(8,128)(2,1)S(1)} collective-permute-done((bf16[896,256]{1,0:T(8,128)(2,1)}, bf16[896,256]{1,0:T(8,128)(2,1)S(1)}, u32[]{:S(2)}, u32[]{:S(2)}) %collective-permute-start.2) | collective-permute-done | bytes 458784 | tf_op jit(solution)/shard_map/ppermute | solution.py:274
  30.3 5.2 %query.1 = (bf16[1024,256]{1,0:T(8,128)(2,1)}, bf16[768,256]{1,0:T(8,128)(2,1)}, bf16[1280,256]{1,0:T(8,128)(2,1)}, bf16[256,256]{1,0:T(8,128)(2,1)}, bf16[256,1280]{1,0:T(8,128)(2,1)}) custom-call(bf16[1024,768]{1,0:T(8,128)(2,1)} %norm.1.refs_0_, f32[1280]{0:T(1024)} %refs_2_.7, bf16[896,256]{1,0:T(8,128)(2,1)} %pack.1.refs_3_.refs_2_.refs_1_, ...), custom_call_target="tpu_custom_call" | custom-call | flops 99999997952 | bytes 1024 | tf_op jit(solution)/shard_map/query/pallas_call | solution.py:302
  35.6 6.8 %scores.1 = (bf16[2,8,256,512]{3,2,1,0:T(8,128)(2,1)}, f32[2,256,128]{2,1,0:T(8,128)}) custom-call(s32[2]{0:T(128)} %refs_0_.5, bf16[1024,256]{1,0:T(8,128)(2,1)} %get-tuple-element.113.refs_1_.refs_0_, bf16[256,256]{1,0:T(8,128)(2,1)} %get-tuple-element.116.refs_2_), custom_call_target="tpu_custom_call" | custom-call | flops 99999997952 | bytes 1024 | tf_op jit(solution)/shard_map/scores/pallas_call | solution.py:302
  43.5 7.0 %values.1 = (bf16[1280,1024]{1,0:T(8,128)(2,1)}, bf16[768,1280]{1,0:T(8,128)(2,1)}) custom-call(bf16[1024,768]{1,0:T(8,128)(2,1)} %norm.1.refs_0_, bf16[896,256]{1,0:T(8,128)(2,1)} %pack.1.refs_3_.refs_2_.refs_1_, bf16[896,256]{1,0:T(8,128)(2,1)} %copy-done.27, bf16[896,256]{1,0:T(8,128)(2,1)} %collective-permute-done.refs_4_.refs_3_, ...), custom_call_target="tpu_custom_call" | custom-call | flops 99999997952 | bytes 1024 | tf_op jit(solution)/shard_map/values/pallas_call | solution.py:302
  50.5 4.4 %collective-permute-done.8.refs_9_ = bf16[480,1280]{1,0:T(8,128)(2,1)} collective-permute-done((bf16[480,1280]{1,0:T(8,128)(2,1)}, bf16[480,1280]{1,0:T(8,128)(2,1)}, u32[]{:S(2)}, u32[]{:S(2)}) %collective-permute-start.8) | collective-permute-done | bytes 1228832 | tf_op jit(solution)/shard_map/ppermute | solution.py:274
  58.2 4.4 %sums.2 = (bf16[4,64,1408]{2,1,0:T(8,128)(2,1)}, bf16[4,64,1408]{2,1,0:T(8,128)(2,1)}) custom-call(bf16[1280,1024]{1,0:T(8,128)(2,1)} %get-tuple-element.120.refs_0_.refs_1_, bf16[2,8,256,512]{3,2,1,0:T(8,128)(2,1)} %get-tuple-element.117.refs_9_.refs_1_.refs_3_, f32[2,256,128]{2,1,0:T(8,128)} %get-tuple-element.121.refs_2_), custom_call_target="tpu_custom_call" | custom-call | flops 99999997952 | bytes 1024 | tf_op jit(solution)/shard_map/sums/pallas_call | solution.py:302
  62.6 4.4 %sums.3 = (bf16[4,64,1408]{2,1,0:T(8,128)(2,1)}, bf16[4,64,1408]{2,1,0:T(8,128)(2,1)}) custom-call(bf16[1280,1024]{1,0:T(8,128)(2,1)} %get-tuple-element.120.refs_0_.refs_1_, bf16[2,8,256,512]{3,2,1,0:T(8,128)(2,1)} %get-tuple-element.117.refs_9_.refs_1_.refs_3_, ...), custom_call_target="tpu_custom_call", output_to_operand_aliasing={{0}: (3, {}), {1}: (4, {})} | custom-call | flops 99999997952 | bytes 1024 | tf_op jit(solution)/shard_map/sums/pallas_call | solution.py:302
  67.0 2.4 %collective-permute-done.10.refs_1_ = bf16[4,64,1408]{2,1,0:T(8,128)(2,1)S(1)} collective-permute-done((bf16[4,64,1408]{2,1,0:T(8,128)(2,1)}, bf16[4,64,1408]{2,1,0:T(8,128)(2,1)S(1)}, u32[]{:S(2)}, u32[]{:S(2)}) %collective-permute-start.10) | collective-permute-done | bytes 720928 | tf_op jit(solution)/shard_map/ppermute | solution.py:270
  76.5 4.1 %collective-permute-done.14.refs_1_ = bf16[64,1408]{1,0:T(8,128)(2,1)S(1)} collective-permute-done((bf16[64,1408]{1,0:T(8,128)(2,1)}, bf16[64,1408]{1,0:T(8,128)(2,1)S(1)}, u32[]{:S(2)}, u32[]{:S(2)}) %collective-permute-start.14) | collective-permute-done | bytes 180256 | tf_op jit(solution)/shard_map/ppermute | solution.py:270
  80.6 3.2 %collective-permute-done.15.refs_2_ = bf16[64,1408]{1,0:T(8,128)(2,1)S(1)} collective-permute-done((bf16[64,1408]{1,0:T(8,128)(2,1)}, bf16[64,1408]{1,0:T(8,128)(2,1)S(1)}, u32[]{:S(2)}, u32[]{:S(2)}) %collective-permute-start.15) | collective-permute-done | bytes 180256 | tf_op jit(solution)/shard_map/ppermute | solution.py:270
  86.3 11.4 %latent.1 = (bf16[64,1280]{1,0:T(8,128)(2,1)}, bf16[3,64,1280]{2,1,0:T(8,128)(2,1)}, bf16[4,3,64,160]{3,2,1,0:T(8,128)(2,1)}, bf16[4,3,64,160]{3,2,1,0:T(8,128)(...) custom-call(bf16[64,1408]{1,0:T(8,128)(2,1)} %get-tuple-element.129.refs_0_, bf16[64,1408]{1,0:T(8,128)(2,1)} %copy-done.46, ...), custom_call_target="tpu_custom_call" | custom-call | flops 99999997952 | bytes 1024 | tf_op jit(solution)/shard_map/latent/pallas_call | solution.py:302
  101.8 4.6 %collective-permute-done.21.refs_10_ = bf16[64,1408]{1,0:T(8,128)(2,1)S(1)} collective-permute-done((bf16[64,1408]{1,0:T(8,128)(2,1)}, bf16[64,1408]{1,0:T(8,128)(2,1)S(1)}, u32[]{:S(2)}, u32[]{:S(2)}) %collective-permute-start.21) | collective-permute-done | bytes 180256 | tf_op jit(solution)/shard_map/ppermute | solution.py:270
  106.4 2.5 %collective-permute-done.20.refs_8_ = bf16[64,1408]{1,0:T(8,128)(2,1)S(1)} collective-permute-done((bf16[64,1408]{1,0:T(8,128)(2,1)}, bf16[64,1408]{1,0:T(8,128)(2,1)S(1)}, u32[]{:S(2)}, u32[]{:S(2)}) %collective-permute-start.20) | collective-permute-done | bytes 180256 | tf_op jit(solution)/shard_map/ppermute | solution.py:270
  112.9 8.4 %backward.2 = (bf16[1536,1024]{1,0:T(8,128)(2,1)}, f32[256,256]{1,0:T(8,128)}, bf16[2,3,64,160]{3,2,1,0:T(8,128)(2,1)}, bf16[2,3,64,160]{3,2,1,0:T(8,128)(2,1)}, bf16[2,3,64,160]{3,2,1,0:T(8,128)(2,1)}) custom-call(bf16[1024,256]{1,0:T(8,128)(2,1)} %get-tuple-element.113.refs_1_.refs_0_, bf16[1280,1024]{1,0:T(8,128)(2,1)} %get-tuple-element.120.refs_0_.refs_1_, ...), custom_call_target="tpu_custom_call" | custom-call | flops 99999997952 | bytes 1024 | tf_op jit(solution)/shard_map/backward/pallas_call | solution.py:302
  121.3 2.5 %collective-permute-done.27.refs_6_ = bf16[3,64,1280]{2,1,0:T(8,128)(2,1)S(1)} collective-permute-done((bf16[3,64,1280]{2,1,0:T(8,128)(2,1)}, bf16[3,64,1280]{2,1,0:T(8,128)(2,1)S(1)}, u32[]{:S(2)}, u32[]{:S(2)}) %collective-permute-start.27) | collective-permute-done | bytes 491552 | tf_op jit(solution)/shard_map/ppermute | solution.py:274
  128.2 8.2 %backward.3 = (bf16[1536,1024]{1,0:T(8,128)(2,1)}, f32[256,256]{1,0:T(8,128)}) custom-call(bf16[1024,256]{1,0:T(8,128)(2,1)} %get-tuple-element.113.refs_1_.refs_0_, bf16[1280,1024]{1,0:T(8,128)(2,1)} %get-tuple-element.120.refs_0_.refs_1_, bf16[256,256]{1,0:T(8,128)(2,1)} %get-tuple-element.116.refs_2_, ...), custom_call_target="tpu_custom_call", output_to_operand_aliasing={{0}: (12, {})} | custom-call | flops 1024 | bytes 1024 | tf_op jit(solution)/shard_map/backward/pallas_call | solution.py:302
  137.1 7.2 %weights.1 = (bf16[4,768,256]{2,1,0:T(8,128)(2,1)}, bf16[4,768,256]{2,1,0:T(8,128)(2,1)}) custom-call(bf16[1024,768]{1,0:T(8,128)(2,1)} %norm.1.refs_0_, bf16[256,1280]{1,0:T(8,128)(2,1)} %get-tuple-element.160.refs_1_, bf16[1536,1024]{1,0:T(8,128)(2,1)} %get-tuple-element.148.refs_2_.refs_4_, f32[256,256]{1,0:T(8,128)} %get-tuple-element.147.refs_13_.refs_3_, ...), custom_call_target="tpu_custom_call" | custom-call | flops 99999997952 | bytes 1024 | tf_op jit(solution)/shard_map/weights/pallas_call | solution.py:302
  145.5 6.2 %latent_grads.1 = (bf16[128,1280]{1,0:T(8,128)(2,1)}, bf16[128,1280]{1,0:T(8,128)(2,1)}, bf16[128,1280]{1,0:T(8,128)(2,1)}, bf16[128,1280]{1,0:T(8,128)(2,1)}, f32[8,160]{1,0:T(8,128)}) custom-call(f32[32,1280]{1,0:T(8,128)} %get-tuple-element.149.refs_0_, bf16[160,1280]{1,0:T(8,128)(2,1)} %refs_1_.11, f32[1280]{0:T(1024)} %refs_2_.6, ...), custom_call_target="tpu_custom_call" | custom-call | flops 99999997952 | bytes 1024 | tf_op jit(solution)/shard_map/latent_grads/pallas_call | solution.py:302
  154.6 3.1 %add4g.1 = (bf16[768,256]{1,0:T(8,128)(2,1)}, bf16[768,256]{1,0:T(8,128)(2,1)}, bf16[768,256]{1,0:T(8,128)(2,1)}, bf16[768,256]{1,0:T(8,128)(2,1)}) custom-call(bf16[4,768,256]{2,1,0:T(8,128)(2,1)} %get-tuple-element.165.refs_0_, bf16[4,768,256]{2,1,0:T(8,128)(2,1)} %copy-done.17, bf16[128,1280]{1,0:T(8,128)(2,1)} %get-tuple-element.166.refs_2_.refs_1_), custom_call_target="tpu_custom_call" | custom-call | flops 99999997952 | bytes 1024 | tf_op jit(solution)/shard_map/add4g/pallas_call | solution.py:302
  166.4 2.6 %collective-permute-start.42 = (bf16[128,1280]{1,0:T(8,128)(2,1)}, bf16[128,1280]{1,0:T(8,128)(2,1)S(1)}, u32[]{:S(2)}, u32[]{:S(2)}) collective-permute-start(bf16[128,1280]{1,0:T(8,128)(2,1)} %osum.1.refs_5_), channel_id=1, source_target_pairs={{0,16},{8,24},{16,0},{24,8},{1,17},{9,25},{17,1},{25,9},{2,18},{10... | collective-permute-start | bytes 983048 | tf_op jit(solution)/shard_map/ppermute | solution.py:278
  169.0 7.6 %bytes.1.refs_10_ = f32[2,512,768]{2,1,0:T(8,128)} custom-call(bf16[1024,768]{1,0:T(8,128)(2,1)} %bitcast.4, f32[768]{0:T(1024)} %refs_7_.1, bf16[768,256]{1,0:T(8,128)(2,1)} %get-tuple-element.135.refs_2_, bf16[768,1280]{1,0:T(8,128)(2,1)} %get-tuple-element.136.refs_3_, bf16[1536,1024]{1,0:T(8,128)(2,1)} %get-tuple-element.148.refs_2_.refs_4_, ...), custom_call_target="tpu_custom_call" | custom-call | flops 1024 | bytes 1024 | tf_op jit(solution)/shard_map/bytes/pallas_call | solution.py:302
  179.6 2.8 %gsum.1 = (bf16[192,256]{1,0:T(8,128)(2,1)}, bf16[192,256]{1,0:T(8,128)(2,1)}, bf16[400,256]{1,0:T(8,128)(2,1)}) custom-call(bf16[768,256]{1,0:T(8,128)(2,1)} %get-tuple-element.167.refs_2_.refs_0_, bf16[768,256]{1,0:T(8,128)(2,1)} %copy-done.33, bf16[768,256]{1,0:T(8,128)(2,1)} %copy-done.34, bf16[768,256]{1,0:T(8,128)(2,1)} %copy-done.35, ...), custom_call_target="tpu_custom_call" | custom-call | flops 99999997952 | bytes 1024 | tf_op jit(solution)/shard_map/gsum/pallas_call | solution.py:302
  192.5 2.6 %collective-permute-start.45 = (bf16[208,256]{1,0:T(8,128)(2,1)}, bf16[208,256]{1,0:T(8,128)(2,1)S(1)}, u32[]{:S(2)}, u32[]{:S(2)}) collective-permute-start(bf16[208,256]{1,0:T(8,128)(2,1)} %get-tuple-element.182.refs_1_), channel_id=1, source_target_pairs={{0,16},{8,24},{16,0},{24,8},{1,17},{9,25},{17,1},{25,9},{2,18},{10... | collective-permute-start | bytes 319496 | tf_op jit(solution)/shard_map/ppermute | solution.py:278
  195.1 11.6 %collective-permute-done.45.refs_2_ = bf16[208,256]{1,0:T(8,128)(2,1)S(1)} collective-permute-done((bf16[208,256]{1,0:T(8,128)(2,1)}, bf16[208,256]{1,0:T(8,128)(2,1)S(1)}, u32[]{:S(2)}, u32[]{:S(2)}) %collective-permute-start.45) | collective-permute-done | bytes 106528 | tf_op jit(solution)/shard_map/ppermute | solution.py:278
  209.9 3.3 %collective-permute-start.50 = (bf16[192,256]{1,0:T(8,128)(2,1)}, bf16[192,256]{1,0:T(8,128)(2,1)S(1)}, u32[]{:S(2)}, u32[]{:S(2)}) collective-permute-start(bf16[192,256]{1,0:T(8,128)(2,1)} %get-tuple-element.188.refs_4_), channel_id=1, source_target_pairs={{0,16},{8,24},{16,0},{24,8},{1,17},{9,25},{17,1},{25,9},{2,18},{10... | collective-permute-start | bytes 294920 | tf_op jit(solution)/shard_map/ppermute | solution.py:278
  220.3 3.9 %collective-permute-start.49 = (bf16[192,256]{1,0:T(8,128)(2,1)}, bf16[192,256]{1,0:T(8,128)(2,1)S(1)}, u32[]{:S(2)}, u32[]{:S(2)}) collective-permute-start(bf16[192,256]{1,0:T(8,128)(2,1)} %get-tuple-element.188.refs_4_), channel_id=1, source_target_pairs={{0,8},{8,0},{16,24},{24,16},{1,9},{9,1},{17,25},{25,17},{2,10},{10... | collective-permute-start | bytes 294920 | tf_op jit(solution)/shard_map/ppermute | solution.py:278
  224.9 2.9 %finish_latent.1 = (f32[160,1280]{1,0:T(8,128)}, f32[160,1280]{1,0:T(8,128)}, f32[160,1280]{1,0:T(8,128)}, f32[32,1280]{1,0:T(8,128)}) custom-call(bf16[128,1280]{1,0:T(8,128)(2,1)} %ototal.1.refs_4_.refs_0_, bf16[128,1280]{1,0:T(8,128)(2,1)} %copy-done.38, bf16[128,1280]{1,0:T(8,128)(2,1)} %copy-done.1, bf16[128,1280]{1,0:T(8,128)(2,1)} %copy-done.39), custom_call_target="tpu_custom_call" | custom-call | flops 99999997952 | bytes 1024 | tf_op jit(solution)/shard_map/finish_latent/pallas_call | solution.py:302
  228.5 2.5 %norms.1 = (f32[768]{0:T(1024)}, f32[1280]{0:T(1024)}, f32[1280]{0:T(1024)}) custom-call(bf16[16,256]{1,0:T(8,128)(2,1)} %nsum.1.refs_0_, bf16[16,256]{1,0:T(8,128)(2,1)} %copy-done.15, bf16[16,256]{1,0:T(8,128)(2,1)} %copy-done.14, bf16[16,256]{1,0:T(8,128)(2,1)} %copy-done.13, f32[32,1280]{1,0:T(8,128)} %get-tuple-element.185.refs_4_.refs_3_), custom_call_target="tpu_custom_call" | custom-call | flops 1024 | bytes 1024 | tf_op jit(solution)/shard_map/norms/pallas_call | solution.py:302
  231.6 2.6 %finish.1 = (f32[96,256]{1,0:T(8,128)}, f32[96,1280]{1,0:T(8,128)}, f32[160,256]{1,0:T(8,128)}, f32[32,1280]{1,0:T(8,128)}) custom-call(bf16[1280,256]{1,0:T(8,128)(2,1)} %get-tuple-element.170.refs_0_, bf16[32,1280]{1,0:T(8,128)(2,1)} %refs_1_.13, f32[1280]{0:T(1024)} %refs_2_.7, f32[32,1280]{1,0:T(8,128)} %get-tuple-element.185.refs_4_.refs_3_, ...), custom_call_target="tpu_custom_call" | custom-call | flops 1024 | bytes 1024 | tf_op jit(solution)/shard_map/finish/pallas_call | solution.py:302
  (201 shorter events, 78.1 us)
Async XLA Ops:
  2.5 14.1 %collective-permute-start.1 = (bf16[896,256]{1,0:T(8,128)(2,1)}, bf16[896,256]{1,0:T(8,128)(2,1)}, u32[]{:S(2)}, u32[]{:S(2)}) collective-permute-start(bf16[896,256]{1,0:T(8,128)(2,1)} %pack.1.refs_3_.refs_2_.refs_1_), channel_id=1, source_target_pairs={{0,4},{1,3},{2,6},{3,1},{4,0},{5,7},{6,2},{7,5},{8,12},{9,11},{10,... | collective-permute-start | bytes 1376264 | tf_op jit(solution)/shard_map/ppermute | solution.py:274
  5.5 11.2 %collective-permute-start = (bf16[896,256]{1,0:T(8,128)(2,1)}, bf16[896,256]{1,0:T(8,128)(2,1)}, u32[]{:S(2)}, u32[]{:S(2)}) collective-permute-start(bf16[896,256]{1,0:T(8,128)(2,1)} %pack.1.refs_3_.refs_2_.refs_1_), channel_id=1, source_target_pairs={{0,2},{1,5},{2,0},{3,7},{4,6},{5,1},{6,4},{7,3},{8,10},{9,13},{10,... | collective-permute-start | bytes 1376264 | tf_op jit(solution)/shard_map/ppermute | solution.py:274
  25.9 28.9 %collective-permute-start.8 = (bf16[480,1280]{1,0:T(8,128)(2,1)}, bf16[480,1280]{1,0:T(8,128)(2,1)}, u32[]{:S(2)}, u32[]{:S(2)}) collective-permute-start(bf16[480,1280]{1,0:T(8,128)(2,1)} %pack_rows.1.refs_2_.refs_7_), channel_id=1, source_target_pairs={{0,2},{1,5},{2,0},{3,7},{4,6},{5,1},{6,4},{7,3},{8,10},{9,13},{10,... | collective-permute-start | bytes 3686408 | tf_op jit(solution)/shard_map/ppermute | solution.py:274
  26.9 29.1 %collective-permute-start.9 = (bf16[480,1280]{1,0:T(8,128)(2,1)}, bf16[480,1280]{1,0:T(8,128)(2,1)}, u32[]{:S(2)}, u32[]{:S(2)}) collective-permute-start(bf16[480,1280]{1,0:T(8,128)(2,1)} %pack_rows.1.refs_2_.refs_7_), channel_id=1, source_target_pairs={{0,4},{1,3},{2,6},{3,1},{4,0},{5,7},{6,2},{7,5},{8,12},{9,11},{10,... | collective-permute-start | bytes 3686408 | tf_op jit(solution)/shard_map/ppermute | solution.py:274
  55.9 17.0 %collective-permute-start.13 = (bf16[480,1280]{1,0:T(8,128)(2,1)}, bf16[480,1280]{1,0:T(8,128)(2,1)}, u32[]{:S(2)}, u32[]{:S(2)}) collective-permute-start(bf16[480,1280]{1,0:T(8,128)(2,1)} %collective-permute-done.8.refs_9_), channel_id=1, source_target_pairs={{0,4},{1,3},{2,6},{3,1},{4,0},{5,7},{6,2},{7,5},{8,12},{9,11},{10,... | collective-permute-start | bytes 3686408 | tf_op jit(solution)/shard_map/ppermute | solution.py:274
  57.7 11.7 %collective-permute-start.11 = (bf16[480,1280]{1,0:T(8,128)(2,1)}, bf16[480,1280]{1,0:T(8,128)(2,1)}, u32[]{:S(2)}, u32[]{:S(2)}) collective-permute-start(bf16[480,1280]{1,0:T(8,128)(2,1)} %collective-permute-done.8.refs_9_), channel_id=1, source_target_pairs={{0,1},{1,0},{2,3},{3,2},{4,5},{5,4},{6,7},{7,6},{8,9},{9,8},{10,11... | collective-permute-start | bytes 3686408 | tf_op jit(solution)/shard_map/ppermute | solution.py:270
  57.7 11.7 %collective-permute-start.12 = (bf16[480,1280]{1,0:T(8,128)(2,1)}, bf16[480,1280]{1,0:T(8,128)(2,1)}, u32[]{:S(2)}, u32[]{:S(2)}) collective-permute-start(bf16[480,1280]{1,0:T(8,128)(2,1)} %collective-permute-done.9.refs_10_), channel_id=1, source_target_pairs={{0,1},{1,0},{2,3},{3,2},{4,5},{5,4},{6,7},{7,6},{8,9},{9,8},{10,11... | collective-permute-start | bytes 3686408 | tf_op jit(solution)/shard_map/ppermute | solution.py:270
  73.0 12.2 %collective-permute-start.17 = (bf16[480,1280]{1,0:T(8,128)(2,1)}, bf16[480,1280]{1,0:T(8,128)(2,1)S(1)}, u32[]{:S(2)}, u32[]{:S(2)}) collective-permute-start(bf16[480,1280]{1,0:T(8,128)(2,1)} %collective-permute-done.13.refs_11_), channel_id=1, source_target_pairs={{0,1},{1,0},{2,3},{3,2},{4,5},{5,4},{6,7},{7,6},{8,9},{9,8},{10,11... | collective-permute-start | bytes 3686408 | tf_op jit(solution)/shard_map/ppermute | solution.py:270
  73.7 10.2 %collective-permute-start.15 = (bf16[64,1408]{1,0:T(8,128)(2,1)}, bf16[64,1408]{1,0:T(8,128)(2,1)S(1)}, u32[]{:S(2)}, u32[]{:S(2)}) collective-permute-start(bf16[64,1408]{1,0:T(8,128)(2,1)} %get-tuple-element.131), channel_id=1, source_target_pairs={{0,4},{1,5},{2,6},{3,7},{4,0},{5,1},{6,2},{7,3},{8,12},{9,13},{10,... | collective-permute-start | bytes 540680 | tf_op jit(solution)/shard_map/ppermute | solution.py:270
  75.4 9.8 %collective-permute-start.16 = (bf16[64,1408]{1,0:T(8,128)(2,1)}, bf16[64,1408]{1,0:T(8,128)(2,1)S(1)}, u32[]{:S(2)}, u32[]{:S(2)}) collective-permute-start(bf16[64,1408]{1,0:T(8,128)(2,1)} %get-tuple-element.132), channel_id=1, source_target_pairs={{0,6},{1,7},{2,4},{3,5},{4,2},{5,3},{6,0},{7,1},{8,14},{9,15},{10,... | collective-permute-start | bytes 540680 | tf_op jit(solution)/shard_map/ppermute | solution.py:270
  109.6 11.7 %collective-permute-start.28 = (bf16[3,64,1280]{2,1,0:T(8,128)(2,1)}, bf16[3,64,1280]{2,1,0:T(8,128)(2,1)S(1)}, u32[]{:S(2)}, u32[]{:S(2)}) collective-permute-start(bf16[3,64,1280]{2,1,0:T(8,128)(2,1)} %get-tuple-element.146.refs_3_), channel_id=1, source_target_pairs={{0,1},{1,0},{2,3},{3,2},{4,5},{5,4},{6,7},{7,6},{8,9},{9,8},{10,11... | collective-permute-start | bytes 1474568 | tf_op jit(solution)/shard_map/ppermute | solution.py:270
  110.0 13.9 %collective-permute-start.27 = (bf16[3,64,1280]{2,1,0:T(8,128)(2,1)}, bf16[3,64,1280]{2,1,0:T(8,128)(2,1)S(1)}, u32[]{:S(2)}, u32[]{:S(2)}) collective-permute-start(bf16[3,64,1280]{2,1,0:T(8,128)(2,1)} %get-tuple-element.146.refs_3_), channel_id=1, source_target_pairs={{0,4},{1,3},{2,6},{3,1},{4,0},{5,7},{6,2},{7,5},{8,12},{9,11},{10,... | collective-permute-start | bytes 1474568 | tf_op jit(solution)/shard_map/ppermute | solution.py:274
  110.6 13.3 %collective-permute-start.26 = (bf16[3,64,1280]{2,1,0:T(8,128)(2,1)}, bf16[3,64,1280]{2,1,0:T(8,128)(2,1)S(1)}, u32[]{:S(2)}, u32[]{:S(2)}) collective-permute-start(bf16[3,64,1280]{2,1,0:T(8,128)(2,1)} %get-tuple-element.146.refs_3_), channel_id=1, source_target_pairs={{0,2},{1,5},{2,0},{3,7},{4,6},{5,1},{6,4},{7,3},{8,10},{9,13},{10,... | collective-permute-start | bytes 1474568 | tf_op jit(solution)/shard_map/ppermute | solution.py:274
  123.9 12.5 %collective-permute-start.30 = (bf16[3,64,1280]{2,1,0:T(8,128)(2,1)S(1)}, bf16[3,64,1280]{2,1,0:T(8,128)(2,1)S(1)}, u32[]{:S(2)}, u32[]{:S(2)}) collective-permute-start(bf16[3,64,1280]{2,1,0:T(8,128)(2,1)S(1)} %collective-permute-done.26.refs_5_), channel_id=1, source_target_pairs={{0,1},{1,0},{2,3},{3,2},{4,5},{5,4},{6,7},{7,6},{8,9},{9,8},{10,11... | collective-permute-start | bytes 1474568 | tf_op jit(solution)/shard_map/ppermute | solution.py:270
  124.0 12.6 %collective-permute-start.29 = (bf16[3,64,1280]{2,1,0:T(8,128)(2,1)S(1)}, bf16[3,64,1280]{2,1,0:T(8,128)(2,1)}, u32[]{:S(2)}, u32[]{:S(2)}) collective-permute-start(bf16[3,64,1280]{2,1,0:T(8,128)(2,1)S(1)} %collective-permute-done.26.refs_5_), channel_id=1, source_target_pairs={{0,4},{1,3},{2,6},{3,1},{4,0},{5,7},{6,2},{7,5},{8,12},{9,11},{10,... | collective-permute-start | bytes 1474568 | tf_op jit(solution)/shard_map/ppermute | solution.py:274
  124.7 19.6 %collective-permute-start.33 = (bf16[2,3,64,160]{3,2,1,0:T(8,128)(2,1)}, bf16[2,3,64,160]{3,2,1,0:T(8,128)(2,1)S(1)}, u32[]{:S(2)}, u32[]{:S(2)}) collective-permute-start(bf16[2,3,64,160]{3,2,1,0:T(8,128)(2,1)} %get-tuple-element.157), channel_id=1, source_target_pairs={{0,2},{1,3},{2,0},{3,1},{4,6},{5,7},{6,4},{7,5},{8,10},{9,11},{10,... | collective-permute-start | bytes 368648 | tf_op jit(solution)/shard_map/ppermute | solution.py:270
  126.1 18.3 %collective-permute-start.34 = (bf16[2,3,64,160]{3,2,1,0:T(8,128)(2,1)}, bf16[2,3,64,160]{3,2,1,0:T(8,128)(2,1)S(1)}, u32[]{:S(2)}, u32[]{:S(2)}) collective-permute-start(bf16[2,3,64,160]{3,2,1,0:T(8,128)(2,1)} %get-tuple-element.158), channel_id=1, source_target_pairs={{0,4},{1,5},{2,6},{3,7},{4,0},{5,1},{6,2},{7,3},{8,12},{9,13},{10,... | collective-permute-start | bytes 368648 | tf_op jit(solution)/shard_map/ppermute | solution.py:270
  126.9 17.6 %collective-permute-start.35 = (bf16[2,3,64,160]{3,2,1,0:T(8,128)(2,1)}, bf16[2,3,64,160]{3,2,1,0:T(8,128)(2,1)}, u32[]{:S(2)}, u32[]{:S(2)}) collective-permute-start(bf16[2,3,64,160]{3,2,1,0:T(8,128)(2,1)} %get-tuple-element.159), channel_id=1, source_target_pairs={{0,6},{1,7},{2,4},{3,5},{4,2},{5,3},{6,0},{7,1},{8,14},{9,15},{10,... | collective-permute-start | bytes 368648 | tf_op jit(solution)/shard_map/ppermute | solution.py:270
  151.6 10.4 %collective-permute-start.36 = (bf16[128,1280]{1,0:T(8,128)(2,1)}, bf16[128,1280]{1,0:T(8,128)(2,1)S(1)}, u32[]{:S(2)}, u32[]{:S(2)}) collective-permute-start(bf16[128,1280]{1,0:T(8,128)(2,1)} %get-tuple-element.164), channel_id=1, source_target_pairs={{0,8},{8,0},{16,24},{24,16},{1,9},{9,1},{17,25},{25,17},{2,10},{10... | collective-permute-start | bytes 983048 | tf_op jit(solution)/shard_map/ppermute | solution.py:278
  157.8 18.9 %collective-permute-start.38 = (bf16[768,256]{1,0:T(8,128)(2,1)}, bf16[768,256]{1,0:T(8,128)(2,1)S(1)}, u32[]{:S(2)}, u32[]{:S(2)}) collective-permute-start(bf16[768,256]{1,0:T(8,128)(2,1)} %get-tuple-element.171), channel_id=1, source_target_pairs={{0,2},{1,3},{2,0},{3,1},{4,6},{5,7},{6,4},{7,5},{8,10},{9,11},{10,... | collective-permute-start | bytes 1179656 | tf_op jit(solution)/shard_map/ppermute | solution.py:270
  159.2 19.5 %collective-permute-start.39 = (bf16[768,256]{1,0:T(8,128)(2,1)}, bf16[768,256]{1,0:T(8,128)(2,1)S(1)}, u32[]{:S(2)}, u32[]{:S(2)}) collective-permute-start(bf16[768,256]{1,0:T(8,128)(2,1)} %get-tuple-element.172), channel_id=1, source_target_pairs={{0,4},{1,5},{2,6},{3,7},{4,0},{5,1},{6,2},{7,3},{8,12},{9,13},{10,... | collective-permute-start | bytes 1179656 | tf_op jit(solution)/shard_map/ppermute | solution.py:270
  160.0 18.8 %collective-permute-start.40 = (bf16[768,256]{1,0:T(8,128)(2,1)}, bf16[768,256]{1,0:T(8,128)(2,1)S(1)}, u32[]{:S(2)}, u32[]{:S(2)}) collective-permute-start(bf16[768,256]{1,0:T(8,128)(2,1)} %get-tuple-element.173), channel_id=1, source_target_pairs={{0,6},{1,7},{2,4},{3,5},{4,2},{5,3},{6,0},{7,1},{8,14},{9,15},{10,... | collective-permute-start | bytes 1179656 | tf_op jit(solution)/shard_map/ppermute | solution.py:270
  164.7 18.0 %collective-permute-start.41 = (bf16[128,1280]{1,0:T(8,128)(2,1)S(1)}, bf16[128,1280]{1,0:T(8,128)(2,1)S(1)}, u32[]{:S(2)}, u32[]{:S(2)}) collective-permute-start(bf16[128,1280]{1,0:T(8,128)(2,1)S(1)} %copy-done.37), channel_id=1, source_target_pairs={{0,8},{8,0},{16,24},{24,16},{1,9},{9,1},{17,25},{25,17},{2,10},{10... | collective-permute-start | bytes 983048 | tf_op jit(solution)/shard_map/ppermute | solution.py:278
  166.4 17.1 %collective-permute-start.42 = (bf16[128,1280]{1,0:T(8,128)(2,1)}, bf16[128,1280]{1,0:T(8,128)(2,1)S(1)}, u32[]{:S(2)}, u32[]{:S(2)}) collective-permute-start(bf16[128,1280]{1,0:T(8,128)(2,1)} %osum.1.refs_5_), channel_id=1, source_target_pairs={{0,16},{8,24},{16,0},{24,8},{1,17},{9,25},{17,1},{25,9},{2,18},{10... | collective-permute-start | bytes 983048 | tf_op jit(solution)/shard_map/ppermute | solution.py:278
  186.3 20.4 %collective-permute-start.46 = (bf16[128,1280]{1,0:T(8,128)(2,1)}, bf16[128,1280]{1,0:T(8,128)(2,1)S(1)}, u32[]{:S(2)}, u32[]{:S(2)}) collective-permute-start(bf16[128,1280]{1,0:T(8,128)(2,1)} %ototal.1.refs_4_.refs_0_), channel_id=1, source_target_pairs={{0,16},{8,24},{16,0},{24,8},{1,17},{9,25},{17,1},{25,9},{2,18},{10... | collective-permute-start | bytes 983048 | tf_op jit(solution)/shard_map/ppermute | solution.py:278
  192.5 14.2 %collective-permute-start.45 = (bf16[208,256]{1,0:T(8,128)(2,1)}, bf16[208,256]{1,0:T(8,128)(2,1)S(1)}, u32[]{:S(2)}, u32[]{:S(2)}) collective-permute-start(bf16[208,256]{1,0:T(8,128)(2,1)} %get-tuple-element.182.refs_1_), channel_id=1, source_target_pairs={{0,16},{8,24},{16,0},{24,8},{1,17},{9,25},{17,1},{25,9},{2,18},{10... | collective-permute-start | bytes 319496 | tf_op jit(solution)/shard_map/ppermute | solution.py:278
  195.1 25.2 %collective-permute-start.44 = (bf16[128,1280]{1,0:T(8,128)(2,1)S(1)}, bf16[128,1280]{1,0:T(8,128)(2,1)S(1)}, u32[]{:S(2)}, u32[]{:S(2)}) collective-permute-start(bf16[128,1280]{1,0:T(8,128)(2,1)S(1)} %copy-done.36), channel_id=1, source_target_pairs={{0,8},{8,0},{16,24},{24,16},{1,9},{9,1},{17,25},{25,17},{2,10},{10... | collective-permute-start | bytes 983048 | tf_op jit(solution)/shard_map/ppermute | solution.py:278
  209.1 15.1 %collective-permute-start.47 = (bf16[128,1280]{1,0:T(8,128)(2,1)}, bf16[128,1280]{1,0:T(8,128)(2,1)S(1)}, u32[]{:S(2)}, u32[]{:S(2)}) collective-permute-start(bf16[128,1280]{1,0:T(8,128)(2,1)} %copy-done.1), channel_id=1, source_target_pairs={{0,8},{8,0},{16,24},{24,16},{1,9},{9,1},{17,25},{25,17},{2,10},{10... | collective-permute-start | bytes 983048 | tf_op jit(solution)/shard_map/ppermute | solution.py:278
  209.9 9.6 %collective-permute-start.50 = (bf16[192,256]{1,0:T(8,128)(2,1)}, bf16[192,256]{1,0:T(8,128)(2,1)S(1)}, u32[]{:S(2)}, u32[]{:S(2)}) collective-permute-start(bf16[192,256]{1,0:T(8,128)(2,1)} %get-tuple-element.188.refs_4_), channel_id=1, source_target_pairs={{0,16},{8,24},{16,0},{24,8},{1,17},{9,25},{17,1},{25,9},{2,18},{10... | collective-permute-start | bytes 294920 | tf_op jit(solution)/shard_map/ppermute | solution.py:278
  216.5 11.3 %collective-permute-start.54 = (bf16[16,256]{1,0:T(8,128)(2,1)}, bf16[16,256]{1,0:T(8,128)(2,1)S(1)}, u32[]{:S(2)}, u32[]{:S(2)}) collective-permute-start(bf16[16,256]{1,0:T(8,128)(2,1)} %nsum.1.refs_0_), channel_id=1, source_target_pairs={{0,6},{1,7},{2,4},{3,5},{4,2},{5,3},{6,0},{7,1},{8,14},{9,15},{10,... | collective-permute-start | bytes 24584 | tf_op jit(solution)/shard_map/ppermute | solution.py:270
  218.0 9.8 %collective-permute-start.53 = (bf16[16,256]{1,0:T(8,128)(2,1)}, bf16[16,256]{1,0:T(8,128)(2,1)S(1)}, u32[]{:S(2)}, u32[]{:S(2)}) collective-permute-start(bf16[16,256]{1,0:T(8,128)(2,1)} %nsum.1.refs_0_), channel_id=1, source_target_pairs={{0,4},{1,5},{2,6},{3,7},{4,0},{5,1},{6,2},{7,3},{8,12},{9,13},{10,... | collective-permute-start | bytes 24584 | tf_op jit(solution)/shard_map/ppermute | solution.py:270
  220.3 10.7 %collective-permute-start.49 = (bf16[192,256]{1,0:T(8,128)(2,1)}, bf16[192,256]{1,0:T(8,128)(2,1)S(1)}, u32[]{:S(2)}, u32[]{:S(2)}) collective-permute-start(bf16[192,256]{1,0:T(8,128)(2,1)} %get-tuple-element.188.refs_4_), channel_id=1, source_target_pairs={{0,8},{8,0},{16,24},{24,16},{1,9},{9,1},{17,25},{25,17},{2,10},{10... | collective-permute-start | bytes 294920 | tf_op jit(solution)/shard_map/ppermute | solution.py:278
  (72 other events, 285.3 us)

commit v4 on v3

--- a/solution.py
+++ b/solution.py
@@ -581,7 +581,7 @@
 
 
 def sum_slots_kernel(a, b, c, d, wk, wv, wq, bg, qg, mix, *rest):
-    near_o, far_o, send_o, acc = rest
+    near_o, far_o, send_o, norm_o, acc = rest
     me, zi = me_z()
     total = (a[...].astype(F32) + b[...].astype(F32)) + (c[...].astype(F32) + d[...].astype(F32))
     acc[...] = total.astype(BF)
@@ -600,7 +600,7 @@
     padded = [v if size == 160 else jnp.concatenate([v, jnp.zeros((8, 160 - size), F32)], axis=1) for v, size in parts]
     joined = jnp.concatenate(padded + [jnp.zeros((8, 32), F32)], axis=1)
     placed = jnp.where(lax.broadcasted_iota(jnp.int32, (8, 512), 0) == me, joined, 0.0)
-    send_o[384:400, :] = jnp.concatenate([placed[:, 0:256], placed[:, 256:512]], axis=0).astype(BF)
+    norm_o[...] = jnp.concatenate([placed[:, 0:256], placed[:, 256:512]], axis=0).astype(BF)
 
 
 def bytes_kernel(x, bg, wk, wv, dkvt, *rest):
@@ -648,22 +648,7 @@
     init_o[...] = acc[480:512, :].astype(F32)
 
 
-def finish_kernel(wq_full, lat, qg, init, *rest):
-    pieces, (key_o, value_o, query_o, init_o, acc) = rest[:NZ], rest[NZ:]
-    _, zi = me_z()
-    for r in range(NZ):
-        acc[rows_of(zi ^ r, 192), :] = pieces[r][...]
-    key_o[...] = acc[0:96, :].astype(F32)
-    for c in range(5):
-        value_o[:, 256 * c : 256 * (c + 1)] = acc[96 * (c + 1) : 96 * (c + 2), :].astype(F32)
-    query_o[...] = acc[576:736, :].astype(F32)
-    dzn = dot(acc[736:768, :], wq_full[...], 1, 1)
-    hat, inverse = ln_parts(lat[...].astype(F32))
-    init_o[...] = init[...] + ln_back(dzn, hat, inverse, qg[...][None, :])
-
-
-def norms_kernel(a, b, c, d, *outs):
-    both = (a[...].astype(F32) + b[...].astype(F32)) + (c[...].astype(F32) + d[...].astype(F32))
+def finish_norms(both, outs):
     total = jnp.concatenate([both[0:8], both[8:16]], axis=1)
     for n, (out, size) in enumerate(zip(outs, (96, 160, 160))):
         width = out.shape[0]
@@ -684,19 +669,34 @@
     return (a.astype(F32) + b.astype(F32)).astype(BF)
 
 
+def finish_kernel(wq_full, lat, qg, init, *rest):
+    pieces, (key_o, value_o, query_o, init_o), outs, acc = rest[:NZ], rest[NZ : NZ + 4], rest[NZ + 4 : NZ + 7], rest[-1]
+    _, zi = me_z()
+    for r in range(NZ):
+        acc[rows_of(zi ^ r, 192), :] = pieces[r][0:192, :]
+    a, b, c, d = [p[192:208, :].astype(F32) for p in pieces]
+    finish_norms((a + b) + (c + d), outs)
+    key_o[...] = acc[0:96, :].astype(F32)
+    for c in range(5):
+        value_o[:, 256 * c : 256 * (c + 1)] = acc[96 * (c + 1) : 96 * (c + 2), :].astype(F32)
+    query_o[...] = acc[576:736, :].astype(F32)
+    dzn = dot(acc[736:768, :], wq_full[...], 1, 1)
+    hat, inverse = ln_parts(lat[...].astype(F32))
+    init_o[...] = init[...] + ln_back(dzn, hat, inverse, qg[...][None, :])
+
+
 def sum_of_three_kernel(a, b, c, out):
     out[...] = (a[...].astype(F32) + b[...].astype(F32) + c[...].astype(F32)).astype(BF)
 
 
-def first_zq_kernel(near, far, mine, got, near_o, far_o):
+def first_zq_kernel(near, far, got, near_o, far_o):
     near_o[...] = plus(near[...], got[0:192, :])
-    far_o[0:192, :] = plus(far[...], got[192:384, :])
-    far_o[192:208, :] = plus(mine[384:400, :], got[384:400, :])
-
-
-def second_zq_kernel(near, mine, got, near_o, norm_o):
-    near_o[...] = plus(near[...], got[0:192, :])
-    norm_o[...] = plus(mine[192:208, :], got[192:208, :])
+    far_o[...] = plus(far[...], got[192:384, :])
+
+
+def second_zq_kernel(near, got, a, b, out):
+    out[0:192, :] = plus(near[...], got[...])
+    out[192:208, :] = plus(a[...], b[...])
 
 
 def sums_of_pairs_kernel(*refs):
@@ -919,9 +919,9 @@
         deps=(ofar,),
         cost=1024,
     )
-    qnear, qfar, qsend = call(
+    qnear, qfar, qsend, norm = call(
         sum_slots_kernel,
-        (sds((192, 256), BF), sds((192, 256), BF), sds((400, 256), BF)),
+        (sds((192, 256), BF), sds((192, 256), BF), sds((384, 256), BF), sds((16, 256), BF)),
         (gm[0], g1, g2, g3, key_weight, value_weight, query_weight, byte_gain, query_gain, mix),
         [VMEM] * 10,
         [pltpu.VMEM((768, 256), BF)],
@@ -935,31 +935,28 @@
     o2 = send_z(ototal, 2)
     qnear, qfar = call(
         first_zq_kernel,
-        (sds((192, 256), BF), sds((208, 256), BF)),
-        (qnear, qfar, qsend, qgot),
-        [VMEM] * 4,
+        (sds((192, 256), BF), sds((192, 256), BF)),
+        (qnear, qfar, qgot),
+        [VMEM] * 3,
         name="qsum",
         deps=(ototal,),
     )
-    qfar, oshare = tie(qfar, ototal)
-    qgot, o1 = send_z(qfar, 2), send_z(oshare, 1)
-    qtotal, norm = call(
+    qfar, norm, oshare = tie(qfar, norm, ototal)
+    qgot, n3, o1 = send_z(qfar, 2), send(norm, 1), send_z(oshare, 1)
+    (norm,) = sums_of_pairs(((norm, n3),), "nsum", cost=1024)
+    n4 = send(norm, 2)
+    (norm,) = sums_of_pairs(((norm, n4),), "nsum", cost=1024)
+    norm, o2 = tie(norm, o2)
+    n5, ofar2 = send(norm, 4), send_z(o2, 1)
+    qtotal = call(
         second_zq_kernel,
-        (sds((192, 256), BF), sds((16, 256), BF)),
-        (qnear, qfar, qgot),
-        [VMEM] * 3,
+        sds((208, 256), BF),
+        (qnear, qgot, norm, n5),
+        [VMEM] * 4,
         name="qtotal",
-        deps=(o2,),
-        cost=1024,
-    )
-    qtotal, o2 = tie(qtotal, o2)
-    q2, n3 = send_z(qtotal, 2), send(norm, 1)
-    ofar2 = send_z(o2, 1)
-    (norm,) = sums_of_pairs(((norm, n3),), "nsum", cost=1024)
-    norm, qshare = tie(norm, qtotal)
-    q1 = send_z(qshare, 1)
-    n4, n5, n6 = send(norm, 2), send(norm, 4), send(norm, 6)
-    q3 = send_z(q2, 1)
+        deps=(o2, o1),
+    )
+    q2, q1 = send_z(qtotal, 2), send_z(qtotal, 1)
     out_g, up_g, down_g, init_sum = call(
         finish_latent_kernel,
         (sds((160, 1280), F32),) * 3 + (sds((32, 1280), F32),),
@@ -967,24 +964,20 @@
         [VMEM] * NZ,
         [pltpu.VMEM((512, 1280), BF)],
         name="finish_latent",
-    )
-    byte_n, mixer_n, query_n = call(
-        norms_kernel,
-        (sds((768,), F32), sds((1280,), F32), sds((1280,), F32)),
-        (norm, n4, n5, n6),
-        [VMEM] * 4,
-        name="norms",
-        deps=(init_sum,),
         cost=1024,
     )
-    key_g, value_g, query_g, init_g = call(
+    q2, init_sum = tie(q2, init_sum)
+    q3 = send_z(q2, 1)
+    key_g, value_g, query_g, init_g, byte_n, mixer_n, query_n = call(
         finish_kernel,
-        (sds((96, 256), F32), sds((96, 1280), F32), sds((160, 256), F32), sds((32, 1280), F32)),
+        (
+            sds((96, 256), F32), sds((96, 1280), F32), sds((160, 256), F32), sds((32, 1280), F32),
+            sds((768,), F32), sds((1280,), F32), sds((1280,), F32),
+        ),
         (wq_full, latent_init, query_gain, init_sum, qtotal, q1, q2, q3),
         [VMEM] * (4 + NZ),
         [pltpu.VMEM((768, 256), BF)],
         name="finish",
-        deps=(byte_n,),
         cost=1024,
     )
     return (

time: 235 us -> 230 us (0.979)
  starting transfers between devices: 54.1 us -> 51.3 us
    ppermute x11, waiting for transfers between devices: 15.4 us -> 9.5 us  [send_z(): return lax.ppermute(x, 'rep', [(i, i ^ k) for i in range(NZ)])]
    ppermute x35 -> x34, waiting for transfers between devices: 21.7 us -> 25.5 us  [send(): return lax.ppermute(x, 'fsdp', [(i, i ^ k) for i in range(N)])]
    ppermute x35 -> x34, starting transfers between devices: 20.9 us -> 19.5 us  [send(): return lax.ppermute(x, 'fsdp', [(i, i ^ k) for i in range(N)])]
  transfers between devices with their start and end apart: 55 -> 54, of which waited for: 20 -> 22; matrix products, arithmetic and copies ran while one was open for 0% -> 0% of each run, Pallas kernels for 40% -> 40%
where the time goes in v4:
time: 230 us; the launch traced here: 229 us
  Pallas kernels  109 us (47%)
  waiting for transfers between devices  53.4 us (23%)
  starting transfers between devices  51.3 us (22%)
  local copies, waits for them, and re-layouts  13.7 us (6%)
    pallas_call x25, Pallas kernels, call(): pl.pallas_call(run, grid=grid, out_shape=out, in_specs=[ANY] * ahead + li...  109 us
    ppermute x34, waiting for transfers between devices, send(): return lax.ppermute(x, 'fsdp', [(i, i ^ k) for i in range(N)])  25.5 us
    ppermute x34, starting transfers between devices, send(): return lax.ppermute(x, 'fsdp', [(i, i ^ k) for i in range(N)])  19.5 us
    ppermute x9, waiting for transfers between devices, send_split(): lax.ppermute(x, 'fsdp', [(i, i ^ (odd if i & 1 else even)) for i in range...  18.4 us
    ppermute x11, starting transfers between devices, send_z(): return lax.ppermute(x, 'rep', [(i, i ^ k) for i in range(NZ)])  17.8 us
    ppermute x9, starting transfers between devices, send_split(): lax.ppermute(x, 'fsdp', [(i, i ^ (odd if i & 1 else even)) for i in range...  14 us
    unnamed x98, local copies, waits for them, and re-layouts  13.7 us
    ppermute x11, waiting for transfers between devices, send_z(): return lax.ppermute(x, 'rep', [(i, i ^ k) for i in range(NZ)])  9.5 us
  transfers between devices with their start and end apart: 54, of which 22 were waited for; matrix products, arithmetic and copies ran while one was open for 0% of the time, Pallas kernels for 40%

profile of v4, /device:TPU:0, one launch (start us, length us, event | category | flops | bytes accessed | tf_op | source)
XLA Modules:
  0.0 228.9 jit_solution(12144643629245794994)
XLA Ops:
  2.5 3.0 %collective-permute-start.1 = (bf16[896,256]{1,0:T(8,128)(2,1)}, bf16[896,256]{1,0:T(8,128)(2,1)}, u32[]{:S(2)}, u32[]{:S(2)}) collective-permute-start(bf16[896,256]{1,0:T(8,128)(2,1)} %pack.1.refs_3_.refs_2_.refs_1_), channel_id=1, source_target_pairs={{0,4},{1,3},{2,6},{3,1},{4,0},{5,7},{6,2},{7,5},{8,12},{9,11},{10,... | collective-permute-start | bytes 1376264 | tf_op jit(solution)/shard_map/ppermute | solution.py:274
  7.0 2.4 %pack_rows.1.refs_2_.refs_7_ = bf16[480,1280]{1,0:T(8,128)(2,1)} custom-call(bf16[160,1280]{1,0:T(8,128)(2,1)} %refs_0_.4, bf16[160,1280]{1,0:T(8,128)(2,1)} %refs_1_.11, bf16[160,1280]{1,0:T(8,128)(2,1)} %refs_2_.5, bf16[896,256]{1,0:T(8,128)(2,1)} %pack.1.refs_3_.refs_2_.refs_1_), custom_call_target="tpu_custom_call" | custom-call | flops 99999997952 | bytes 1024 | tf_op jit(solution)/shard_map/pack_rows/pallas_call | solution.py:302
  9.4 3.7 %norm.1.refs_0_ = bf16[1024,768]{1,0:T(8,128)(2,1)} custom-call(bf16[1024,768]{1,0:T(8,128)(2,1)} %bitcast.3, f32[768]{0:T(1024)} %refs_7_.1, bf16[480,1280]{1,0:T(8,128)(2,1)} %pack_rows.1.refs_2_.refs_7_), custom_call_target="tpu_custom_call" | custom-call | flops 99999997952 | bytes 1024 | tf_op jit(solution)/shard_map/norm/pallas_call | solution.py:302
  13.0 3.6 %collective-permute-done.1.refs_5_.refs_4_ = bf16[896,256]{1,0:T(8,128)(2,1)} collective-permute-done((bf16[896,256]{1,0:T(8,128)(2,1)}, bf16[896,256]{1,0:T(8,128)(2,1)}, u32[]{:S(2)}, u32[]{:S(2)}) %collective-permute-start.1) | collective-permute-done | bytes 458784 | tf_op jit(solution)/shard_map/ppermute | solution.py:274
  19.8 6.1 %collective-permute-done.2.refs_6_.refs_5_ = bf16[896,256]{1,0:T(8,128)(2,1)S(1)} collective-permute-done((bf16[896,256]{1,0:T(8,128)(2,1)}, bf16[896,256]{1,0:T(8,128)(2,1)S(1)}, u32[]{:S(2)}, u32[]{:S(2)}) %collective-permute-start.2) | collective-permute-done | bytes 458784 | tf_op jit(solution)/shard_map/ppermute | solution.py:274
  30.3 5.2 %query.1 = (bf16[1024,256]{1,0:T(8,128)(2,1)}, bf16[768,256]{1,0:T(8,128)(2,1)}, bf16[1280,256]{1,0:T(8,128)(2,1)}, bf16[256,256]{1,0:T(8,128)(2,1)}, bf16[256,1280]{1,0:T(8,128)(2,1)}) custom-call(bf16[1024,768]{1,0:T(8,128)(2,1)} %norm.1.refs_0_, f32[1280]{0:T(1024)} %refs_2_.7, bf16[896,256]{1,0:T(8,128)(2,1)} %pack.1.refs_3_.refs_2_.refs_1_, ...), custom_call_target="tpu_custom_call" | custom-call | flops 99999997952 | bytes 1024 | tf_op jit(solution)/shard_map/query/pallas_call | solution.py:302
  35.6 6.8 %scores.1 = (bf16[2,8,256,512]{3,2,1,0:T(8,128)(2,1)}, f32[2,256,128]{2,1,0:T(8,128)}) custom-call(s32[2]{0:T(128)} %refs_0_.5, bf16[1024,256]{1,0:T(8,128)(2,1)} %get-tuple-element.113.refs_1_.refs_0_, bf16[256,256]{1,0:T(8,128)(2,1)} %get-tuple-element.116.refs_2_), custom_call_target="tpu_custom_call" | custom-call | flops 99999997952 | bytes 1024 | tf_op jit(solution)/shard_map/scores/pallas_call | solution.py:302
  43.4 7.0 %values.1 = (bf16[1280,1024]{1,0:T(8,128)(2,1)}, bf16[768,1280]{1,0:T(8,128)(2,1)}) custom-call(bf16[1024,768]{1,0:T(8,128)(2,1)} %norm.1.refs_0_, bf16[896,256]{1,0:T(8,128)(2,1)} %pack.1.refs_3_.refs_2_.refs_1_, bf16[896,256]{1,0:T(8,128)(2,1)} %copy-done.28, bf16[896,256]{1,0:T(8,128)(2,1)} %collective-permute-done.refs_4_.refs_3_, ...), custom_call_target="tpu_custom_call" | custom-call | flops 99999997952 | bytes 1024 | tf_op jit(solution)/shard_map/values/pallas_call | solution.py:302
  50.4 4.4 %collective-permute-done.8.refs_9_ = bf16[480,1280]{1,0:T(8,128)(2,1)} collective-permute-done((bf16[480,1280]{1,0:T(8,128)(2,1)}, bf16[480,1280]{1,0:T(8,128)(2,1)}, u32[]{:S(2)}, u32[]{:S(2)}) %collective-permute-start.8) | collective-permute-done | bytes 1228832 | tf_op jit(solution)/shard_map/ppermute | solution.py:274
  58.2 4.4 %sums.2 = (bf16[4,64,1408]{2,1,0:T(8,128)(2,1)}, bf16[4,64,1408]{2,1,0:T(8,128)(2,1)}) custom-call(bf16[1280,1024]{1,0:T(8,128)(2,1)} %get-tuple-element.120.refs_0_.refs_1_, bf16[2,8,256,512]{3,2,1,0:T(8,128)(2,1)} %get-tuple-element.117.refs_9_.refs_1_.refs_3_, f32[2,256,128]{2,1,0:T(8,128)} %get-tuple-element.121.refs_2_), custom_call_target="tpu_custom_call" | custom-call | flops 99999997952 | bytes 1024 | tf_op jit(solution)/shard_map/sums/pallas_call | solution.py:302
  62.6 4.4 %sums.3 = (bf16[4,64,1408]{2,1,0:T(8,128)(2,1)}, bf16[4,64,1408]{2,1,0:T(8,128)(2,1)}) custom-call(bf16[1280,1024]{1,0:T(8,128)(2,1)} %get-tuple-element.120.refs_0_.refs_1_, bf16[2,8,256,512]{3,2,1,0:T(8,128)(2,1)} %get-tuple-element.117.refs_9_.refs_1_.refs_3_, ...), custom_call_target="tpu_custom_call", output_to_operand_aliasing={{0}: (3, {}), {1}: (4, {})} | custom-call | flops 99999997952 | bytes 1024 | tf_op jit(solution)/shard_map/sums/pallas_call | solution.py:302
  67.0 2.4 %collective-permute-done.10.refs_1_ = bf16[4,64,1408]{2,1,0:T(8,128)(2,1)S(1)} collective-permute-done((bf16[4,64,1408]{2,1,0:T(8,128)(2,1)}, bf16[4,64,1408]{2,1,0:T(8,128)(2,1)S(1)}, u32[]{:S(2)}, u32[]{:S(2)}) %collective-permute-start.10) | collective-permute-done | bytes 720928 | tf_op jit(solution)/shard_map/ppermute | solution.py:270
  76.5 4.1 %collective-permute-done.14.refs_1_ = bf16[64,1408]{1,0:T(8,128)(2,1)S(1)} collective-permute-done((bf16[64,1408]{1,0:T(8,128)(2,1)}, bf16[64,1408]{1,0:T(8,128)(2,1)S(1)}, u32[]{:S(2)}, u32[]{:S(2)}) %collective-permute-start.14) | collective-permute-done | bytes 180256 | tf_op jit(solution)/shard_map/ppermute | solution.py:270
  80.6 3.2 %collective-permute-done.15.refs_2_ = bf16[64,1408]{1,0:T(8,128)(2,1)S(1)} collective-permute-done((bf16[64,1408]{1,0:T(8,128)(2,1)}, bf16[64,1408]{1,0:T(8,128)(2,1)S(1)}, u32[]{:S(2)}, u32[]{:S(2)}) %collective-permute-start.15) | collective-permute-done | bytes 180256 | tf_op jit(solution)/shard_map/ppermute | solution.py:270
  86.3 11.4 %latent.1 = (bf16[64,1280]{1,0:T(8,128)(2,1)}, bf16[3,64,1280]{2,1,0:T(8,128)(2,1)}, bf16[4,3,64,160]{3,2,1,0:T(8,128)(2,1)}, bf16[4,3,64,160]{3,2,1,0:T(8,128)(...) custom-call(bf16[64,1408]{1,0:T(8,128)(2,1)} %get-tuple-element.129.refs_0_, bf16[64,1408]{1,0:T(8,128)(2,1)} %copy-done.44, ...), custom_call_target="tpu_custom_call" | custom-call | flops 99999997952 | bytes 1024 | tf_op jit(solution)/shard_map/latent/pallas_call | solution.py:302
  101.8 4.6 %collective-permute-done.21.refs_10_ = bf16[64,1408]{1,0:T(8,128)(2,1)S(1)} collective-permute-done((bf16[64,1408]{1,0:T(8,128)(2,1)}, bf16[64,1408]{1,0:T(8,128)(2,1)S(1)}, u32[]{:S(2)}, u32[]{:S(2)}) %collective-permute-start.21) | collective-permute-done | bytes 180256 | tf_op jit(solution)/shard_map/ppermute | solution.py:270
  106.4 2.5 %collective-permute-done.20.refs_8_ = bf16[64,1408]{1,0:T(8,128)(2,1)S(1)} collective-permute-done((bf16[64,1408]{1,0:T(8,128)(2,1)}, bf16[64,1408]{1,0:T(8,128)(2,1)S(1)}, u32[]{:S(2)}, u32[]{:S(2)}) %collective-permute-start.20) | collective-permute-done | bytes 180256 | tf_op jit(solution)/shard_map/ppermute | solution.py:270
  112.9 8.5 %backward.2 = (bf16[1536,1024]{1,0:T(8,128)(2,1)}, f32[256,256]{1,0:T(8,128)}, bf16[2,3,64,160]{3,2,1,0:T(8,128)(2,1)}, bf16[2,3,64,160]{3,2,1,0:T(8,128)(2,1)}, bf16[2,3,64,160]{3,2,1,0:T(8,128)(2,1)}) custom-call(bf16[1024,256]{1,0:T(8,128)(2,1)} %get-tuple-element.113.refs_1_.refs_0_, bf16[1280,1024]{1,0:T(8,128)(2,1)} %get-tuple-element.120.refs_0_.refs_1_, ...), custom_call_target="tpu_custom_call" | custom-call | flops 99999997952 | bytes 1024 | tf_op jit(solution)/shard_map/backward/pallas_call | solution.py:302
  121.4 2.5 %collective-permute-done.27.refs_6_ = bf16[3,64,1280]{2,1,0:T(8,128)(2,1)S(1)} collective-permute-done((bf16[3,64,1280]{2,1,0:T(8,128)(2,1)}, bf16[3,64,1280]{2,1,0:T(8,128)(2,1)S(1)}, u32[]{:S(2)}, u32[]{:S(2)}) %collective-permute-start.27) | collective-permute-done | bytes 491552 | tf_op jit(solution)/shard_map/ppermute | solution.py:274
  128.2 8.3 %backward.3 = (bf16[1536,1024]{1,0:T(8,128)(2,1)}, f32[256,256]{1,0:T(8,128)}) custom-call(bf16[1024,256]{1,0:T(8,128)(2,1)} %get-tuple-element.113.refs_1_.refs_0_, bf16[1280,1024]{1,0:T(8,128)(2,1)} %get-tuple-element.120.refs_0_.refs_1_, bf16[256,256]{1,0:T(8,128)(2,1)} %get-tuple-element.116.refs_2_, ...), custom_call_target="tpu_custom_call", output_to_operand_aliasing={{0}: (12, {})} | custom-call | flops 1024 | bytes 1024 | tf_op jit(solution)/shard_map/backward/pallas_call | solution.py:302
  137.1 7.2 %weights.1 = (bf16[4,768,256]{2,1,0:T(8,128)(2,1)}, bf16[4,768,256]{2,1,0:T(8,128)(2,1)}) custom-call(bf16[1024,768]{1,0:T(8,128)(2,1)} %norm.1.refs_0_, bf16[256,1280]{1,0:T(8,128)(2,1)} %get-tuple-element.160.refs_1_, bf16[1536,1024]{1,0:T(8,128)(2,1)} %get-tuple-element.148.refs_2_.refs_4_, f32[256,256]{1,0:T(8,128)} %get-tuple-element.147.refs_13_.refs_3_, ...), custom_call_target="tpu_custom_call" | custom-call | flops 99999997952 | bytes 1024 | tf_op jit(solution)/shard_map/weights/pallas_call | solution.py:302
  145.5 6.2 %latent_grads.1 = (bf16[128,1280]{1,0:T(8,128)(2,1)}, bf16[128,1280]{1,0:T(8,128)(2,1)}, bf16[128,1280]{1,0:T(8,128)(2,1)}, bf16[128,1280]{1,0:T(8,128)(2,1)}, f32[8,160]{1,0:T(8,128)}) custom-call(f32[32,1280]{1,0:T(8,128)} %get-tuple-element.149.refs_0_, bf16[160,1280]{1,0:T(8,128)(2,1)} %refs_1_.11, f32[1280]{0:T(1024)} %refs_2_.6, ...), custom_call_target="tpu_custom_call" | custom-call | flops 99999997952 | bytes 1024 | tf_op jit(solution)/shard_map/latent_grads/pallas_call | solution.py:302
  154.7 3.1 %add4g.1 = (bf16[768,256]{1,0:T(8,128)(2,1)}, bf16[768,256]{1,0:T(8,128)(2,1)}, bf16[768,256]{1,0:T(8,128)(2,1)}, bf16[768,256]{1,0:T(8,128)(2,1)}) custom-call(bf16[4,768,256]{2,1,0:T(8,128)(2,1)} %get-tuple-element.165.refs_0_, bf16[4,768,256]{2,1,0:T(8,128)(2,1)} %copy-done.18, bf16[128,1280]{1,0:T(8,128)(2,1)} %get-tuple-element.166.refs_2_.refs_1_), custom_call_target="tpu_custom_call" | custom-call | flops 99999997952 | bytes 1024 | tf_op jit(solution)/shard_map/add4g/pallas_call | solution.py:302
  166.5 2.6 %collective-permute-start.43 = (bf16[128,1280]{1,0:T(8,128)(2,1)}, bf16[128,1280]{1,0:T(8,128)(2,1)S(1)}, u32[]{:S(2)}, u32[]{:S(2)}) collective-permute-start(bf16[128,1280]{1,0:T(8,128)(2,1)} %osum.1.refs_5_), channel_id=1, source_target_pairs={{0,16},{8,24},{16,0},{24,8},{1,17},{9,25},{17,1},{25,9},{2,18},{10... | collective-permute-start | bytes 983048 | tf_op jit(solution)/shard_map/ppermute | solution.py:278
  169.1 7.6 %bytes.1.refs_10_ = f32[2,512,768]{2,1,0:T(8,128)} custom-call(bf16[1024,768]{1,0:T(8,128)(2,1)} %bitcast.4, f32[768]{0:T(1024)} %refs_7_.1, bf16[768,256]{1,0:T(8,128)(2,1)} %get-tuple-element.135.refs_2_, bf16[768,1280]{1,0:T(8,128)(2,1)} %get-tuple-element.136.refs_3_, bf16[1536,1024]{1,0:T(8,128)(2,1)} %get-tuple-element.148.refs_2_.refs_4_, ...), custom_call_target="tpu_custom_call" | custom-call | flops 1024 | bytes 1024 | tf_op jit(solution)/shard_map/bytes/pallas_call | solution.py:302
  179.6 2.8 %gsum.1 = (bf16[192,256]{1,0:T(8,128)(2,1)}, bf16[192,256]{1,0:T(8,128)(2,1)}, bf16[384,256]{1,0:T(8,128)(2,1)}, bf16[16,256]{1,0:T(8,128)(2,1)}) custom-call(bf16[768,256]{1,0:T(8,128)(2,1)} %get-tuple-element.167.refs_2_.refs_0_, bf16[768,256]{1,0:T(8,128)(2,1)} %copy-done.34, bf16[768,256]{1,0:T(8,128)(2,1)} %copy-done.35, bf16[768,256]{1,0:T(8,128)(2,1)} %copy-done.36, ...), custom_call_target="tpu_custom_call" | custom-call | flops 99999997952 | bytes 1024 | tf_op jit(solution)/shard_map/gsum/pallas_call | solution.py:302
  198.7 3.0 %collective-permute-done.46.refs_1_ = bf16[16,256]{1,0:T(8,128)(2,1)S(1)} collective-permute-done((bf16[16,256]{1,0:T(8,128)(2,1)}, bf16[16,256]{1,0:T(8,128)(2,1)S(1)}, u32[]{:S(2)}, u32[]{:S(2)}) %collective-permute-start.46) | collective-permute-done | bytes 8224 | tf_op jit(solution)/shard_map/ppermute | solution.py:270
  210.4 3.2 %collective-permute-start.52 = (bf16[208,256]{1,0:T(8,128)(2,1)}, bf16[208,256]{1,0:T(8,128)(2,1)S(1)}, u32[]{:S(2)}, u32[]{:S(2)}) collective-permute-start(bf16[208,256]{1,0:T(8,128)(2,1)} %qtotal.1.refs_4_), channel_id=1, source_target_pairs={{0,8},{8,0},{16,24},{24,16},{1,9},{9,1},{17,25},{25,17},{2,10},{10... | collective-permute-start | bytes 319496 | tf_op jit(solution)/shard_map/ppermute | solution.py:278
  213.6 2.7 %collective-permute-done.51.refs_3_ = bf16[128,1280]{1,0:T(8,128)(2,1)S(1)} collective-permute-done((bf16[128,1280]{1,0:T(8,128)(2,1)S(1)}, bf16[128,1280]{1,0:T(8,128)(2,1)S(1)}, u32[]{:S(2)}, u32[]{:S(2)}) %collective-permute-start.51) | collective-permute-done | bytes 327712 | tf_op jit(solution)/shard_map/ppermute | solution.py:278
  217.0 2.9 %finish_latent.1 = (f32[160,1280]{1,0:T(8,128)}, f32[160,1280]{1,0:T(8,128)}, f32[160,1280]{1,0:T(8,128)}, f32[32,1280]{1,0:T(8,128)}) custom-call(bf16[128,1280]{1,0:T(8,128)(2,1)} %ototal.1.refs_3_.refs_0_, bf16[128,1280]{1,0:T(8,128)(2,1)} %copy-done.3, bf16[128,1280]{1,0:T(8,128)(2,1)} %copy-done.2, bf16[128,1280]{1,0:T(8,128)(2,1)} %copy-done.4), custom_call_target="tpu_custom_call" | custom-call | flops 1024 | bytes 1024 | tf_op jit(solution)/shard_map/finish_latent/pallas_call | solution.py:302
  220.8 3.9 %collective-permute-done.53.refs_7_ = bf16[208,256]{1,0:T(8,128)(2,1)S(1)} collective-permute-done((bf16[208,256]{1,0:T(8,128)(2,1)S(1)}, bf16[208,256]{1,0:T(8,128)(2,1)S(1)}, u32[]{:S(2)}, u32[]{:S(2)}) %collective-permute-start.53) | collective-permute-done | bytes 106528 | tf_op jit(solution)/shard_map/ppermute | solution.py:278
  225.3 3.5 %finish.1 = (f32[96,256]{1,0:T(8,128)}, f32[96,1280]{1,0:T(8,128)}, f32[160,256]{1,0:T(8,128)}, f32[32,1280]{1,0:T(8,128)}, f32[768]{0:T(1024)}, /*index=5*/f32[1280]{0:T(1024)}, f32[1280]{0:T(1024)}) custom-call(bf16[1280,256]{1,0:T(8,128)(2,1)} %get-tuple-element.170.refs_0_, bf16[32,1280]{1,0:T(8,128)(2,1)} %refs_1_.13, f32[1280]{0:T(1024)} %refs_2_.7, ...), custom_call_target="tpu_custom_call" | custom-call | flops 1024 | bytes 1024 | tf_op jit(solution)/shard_map/finish/pallas_call | solution.py:302
  (199 shorter events, 80.5 us)
Async XLA Ops:
  2.5 14.1 %collective-permute-start.1 = (bf16[896,256]{1,0:T(8,128)(2,1)}, bf16[896,256]{1,0:T(8,128)(2,1)}, u32[]{:S(2)}, u32[]{:S(2)}) collective-permute-start(bf16[896,256]{1,0:T(8,128)(2,1)} %pack.1.refs_3_.refs_2_.refs_1_), channel_id=1, source_target_pairs={{0,4},{1,3},{2,6},{3,1},{4,0},{5,7},{6,2},{7,5},{8,12},{9,11},{10,... | collective-permute-start | bytes 1376264 | tf_op jit(solution)/shard_map/ppermute | solution.py:274
  5.5 11.2 %collective-permute-start = (bf16[896,256]{1,0:T(8,128)(2,1)}, bf16[896,256]{1,0:T(8,128)(2,1)}, u32[]{:S(2)}, u32[]{:S(2)}) collective-permute-start(bf16[896,256]{1,0:T(8,128)(2,1)} %pack.1.refs_3_.refs_2_.refs_1_), channel_id=1, source_target_pairs={{0,2},{1,5},{2,0},{3,7},{4,6},{5,1},{6,4},{7,3},{8,10},{9,13},{10,... | collective-permute-start | bytes 1376264 | tf_op jit(solution)/shard_map/ppermute | solution.py:274
  19.2 9.4 %collective-permute-start.4 = (bf16[896,256]{1,0:T(8,128)(2,1)}, bf16[896,256]{1,0:T(8,128)(2,1)S(1)}, u32[]{:S(2)}, u32[]{:S(2)}) collective-permute-start(bf16[896,256]{1,0:T(8,128)(2,1)} %collective-permute-done.refs_4_.refs_3_), channel_id=1, source_target_pairs={{0,1},{1,0},{2,3},{3,2},{4,5},{5,4},{6,7},{7,6},{8,9},{9,8},{10,11... | collective-permute-start | bytes 1376264 | tf_op jit(solution)/shard_map/ppermute | solution.py:270
  19.2 9.3 %collective-permute-start.5 = (bf16[896,256]{1,0:T(8,128)(2,1)}, bf16[896,256]{1,0:T(8,128)(2,1)S(1)}, u32[]{:S(2)}, u32[]{:S(2)}) collective-permute-start(bf16[896,256]{1,0:T(8,128)(2,1)} %collective-permute-done.1.refs_5_.refs_4_), channel_id=1, source_target_pairs={{0,1},{1,0},{2,3},{3,2},{4,5},{5,4},{6,7},{7,6},{8,9},{9,8},{10,11... | collective-permute-start | bytes 1376264 | tf_op jit(solution)/shard_map/ppermute | solution.py:270
  25.9 28.9 %collective-permute-start.8 = (bf16[480,1280]{1,0:T(8,128)(2,1)}, bf16[480,1280]{1,0:T(8,128)(2,1)}, u32[]{:S(2)}, u32[]{:S(2)}) collective-permute-start(bf16[480,1280]{1,0:T(8,128)(2,1)} %pack_rows.1.refs_2_.refs_7_), channel_id=1, source_target_pairs={{0,2},{1,5},{2,0},{3,7},{4,6},{5,1},{6,4},{7,3},{8,10},{9,13},{10,... | collective-permute-start | bytes 3686408 | tf_op jit(solution)/shard_map/ppermute | solution.py:274
  26.9 29.1 %collective-permute-start.9 = (bf16[480,1280]{1,0:T(8,128)(2,1)}, bf16[480,1280]{1,0:T(8,128)(2,1)}, u32[]{:S(2)}, u32[]{:S(2)}) collective-permute-start(bf16[480,1280]{1,0:T(8,128)(2,1)} %pack_rows.1.refs_2_.refs_7_), channel_id=1, source_target_pairs={{0,4},{1,3},{2,6},{3,1},{4,0},{5,7},{6,2},{7,5},{8,12},{9,11},{10,... | collective-permute-start | bytes 3686408 | tf_op jit(solution)/shard_map/ppermute | solution.py:274
  55.9 17.0 %collective-permute-start.13 = (bf16[480,1280]{1,0:T(8,128)(2,1)}, bf16[480,1280]{1,0:T(8,128)(2,1)}, u32[]{:S(2)}, u32[]{:S(2)}) collective-permute-start(bf16[480,1280]{1,0:T(8,128)(2,1)} %collective-permute-done.8.refs_9_), channel_id=1, source_target_pairs={{0,4},{1,3},{2,6},{3,1},{4,0},{5,7},{6,2},{7,5},{8,12},{9,11},{10,... | collective-permute-start | bytes 3686408 | tf_op jit(solution)/shard_map/ppermute | solution.py:274
  57.7 11.7 %collective-permute-start.11 = (bf16[480,1280]{1,0:T(8,128)(2,1)}, bf16[480,1280]{1,0:T(8,128)(2,1)}, u32[]{:S(2)}, u32[]{:S(2)}) collective-permute-start(bf16[480,1280]{1,0:T(8,128)(2,1)} %collective-permute-done.8.refs_9_), channel_id=1, source_target_pairs={{0,1},{1,0},{2,3},{3,2},{4,5},{5,4},{6,7},{7,6},{8,9},{9,8},{10,11... | collective-permute-start | bytes 3686408 | tf_op jit(solution)/shard_map/ppermute | solution.py:270
  57.7 11.7 %collective-permute-start.12 = (bf16[480,1280]{1,0:T(8,128)(2,1)}, bf16[480,1280]{1,0:T(8,128)(2,1)}, u32[]{:S(2)}, u32[]{:S(2)}) collective-permute-start(bf16[480,1280]{1,0:T(8,128)(2,1)} %collective-permute-done.9.refs_10_), channel_id=1, source_target_pairs={{0,1},{1,0},{2,3},{3,2},{4,5},{5,4},{6,7},{7,6},{8,9},{9,8},{10,11... | collective-permute-start | bytes 3686408 | tf_op jit(solution)/shard_map/ppermute | solution.py:270
  73.0 12.2 %collective-permute-start.17 = (bf16[480,1280]{1,0:T(8,128)(2,1)}, bf16[480,1280]{1,0:T(8,128)(2,1)S(1)}, u32[]{:S(2)}, u32[]{:S(2)}) collective-permute-start(bf16[480,1280]{1,0:T(8,128)(2,1)} %collective-permute-done.13.refs_11_), channel_id=1, source_target_pairs={{0,1},{1,0},{2,3},{3,2},{4,5},{5,4},{6,7},{7,6},{8,9},{9,8},{10,11... | collective-permute-start | bytes 3686408 | tf_op jit(solution)/shard_map/ppermute | solution.py:270
  73.7 10.2 %collective-permute-start.15 = (bf16[64,1408]{1,0:T(8,128)(2,1)}, bf16[64,1408]{1,0:T(8,128)(2,1)S(1)}, u32[]{:S(2)}, u32[]{:S(2)}) collective-permute-start(bf16[64,1408]{1,0:T(8,128)(2,1)} %get-tuple-element.131), channel_id=1, source_target_pairs={{0,4},{1,5},{2,6},{3,7},{4,0},{5,1},{6,2},{7,3},{8,12},{9,13},{10,... | collective-permute-start | bytes 540680 | tf_op jit(solution)/shard_map/ppermute | solution.py:270
  75.4 9.8 %collective-permute-start.16 = (bf16[64,1408]{1,0:T(8,128)(2,1)}, bf16[64,1408]{1,0:T(8,128)(2,1)S(1)}, u32[]{:S(2)}, u32[]{:S(2)}) collective-permute-start(bf16[64,1408]{1,0:T(8,128)(2,1)} %get-tuple-element.132), channel_id=1, source_target_pairs={{0,6},{1,7},{2,4},{3,5},{4,2},{5,3},{6,0},{7,1},{8,14},{9,15},{10,... | collective-permute-start | bytes 540680 | tf_op jit(solution)/shard_map/ppermute | solution.py:270
  109.6 11.8 %collective-permute-start.28 = (bf16[3,64,1280]{2,1,0:T(8,128)(2,1)}, bf16[3,64,1280]{2,1,0:T(8,128)(2,1)S(1)}, u32[]{:S(2)}, u32[]{:S(2)}) collective-permute-start(bf16[3,64,1280]{2,1,0:T(8,128)(2,1)} %get-tuple-element.146.refs_3_), channel_id=1, source_target_pairs={{0,1},{1,0},{2,3},{3,2},{4,5},{5,4},{6,7},{7,6},{8,9},{9,8},{10,11... | collective-permute-start | bytes 1474568 | tf_op jit(solution)/shard_map/ppermute | solution.py:270
  110.0 13.9 %collective-permute-start.27 = (bf16[3,64,1280]{2,1,0:T(8,128)(2,1)}, bf16[3,64,1280]{2,1,0:T(8,128)(2,1)S(1)}, u32[]{:S(2)}, u32[]{:S(2)}) collective-permute-start(bf16[3,64,1280]{2,1,0:T(8,128)(2,1)} %get-tuple-element.146.refs_3_), channel_id=1, source_target_pairs={{0,4},{1,3},{2,6},{3,1},{4,0},{5,7},{6,2},{7,5},{8,12},{9,11},{10,... | collective-permute-start | bytes 1474568 | tf_op jit(solution)/shard_map/ppermute | solution.py:274
  110.6 13.3 %collective-permute-start.26 = (bf16[3,64,1280]{2,1,0:T(8,128)(2,1)}, bf16[3,64,1280]{2,1,0:T(8,128)(2,1)S(1)}, u32[]{:S(2)}, u32[]{:S(2)}) collective-permute-start(bf16[3,64,1280]{2,1,0:T(8,128)(2,1)} %get-tuple-element.146.refs_3_), channel_id=1, source_target_pairs={{0,2},{1,5},{2,0},{3,7},{4,6},{5,1},{6,4},{7,3},{8,10},{9,13},{10,... | collective-permute-start | bytes 1474568 | tf_op jit(solution)/shard_map/ppermute | solution.py:274
  123.9 12.6 %collective-permute-start.30 = (bf16[3,64,1280]{2,1,0:T(8,128)(2,1)S(1)}, bf16[3,64,1280]{2,1,0:T(8,128)(2,1)S(1)}, u32[]{:S(2)}, u32[]{:S(2)}) collective-permute-start(bf16[3,64,1280]{2,1,0:T(8,128)(2,1)S(1)} %collective-permute-done.26.refs_5_), channel_id=1, source_target_pairs={{0,1},{1,0},{2,3},{3,2},{4,5},{5,4},{6,7},{7,6},{8,9},{9,8},{10,11... | collective-permute-start | bytes 1474568 | tf_op jit(solution)/shard_map/ppermute | solution.py:270
  124.0 12.6 %collective-permute-start.29 = (bf16[3,64,1280]{2,1,0:T(8,128)(2,1)S(1)}, bf16[3,64,1280]{2,1,0:T(8,128)(2,1)}, u32[]{:S(2)}, u32[]{:S(2)}) collective-permute-start(bf16[3,64,1280]{2,1,0:T(8,128)(2,1)S(1)} %collective-permute-done.26.refs_5_), channel_id=1, source_target_pairs={{0,4},{1,3},{2,6},{3,1},{4,0},{5,7},{6,2},{7,5},{8,12},{9,11},{10,... | collective-permute-start | bytes 1474568 | tf_op jit(solution)/shard_map/ppermute | solution.py:274
  124.7 19.6 %collective-permute-start.33 = (bf16[2,3,64,160]{3,2,1,0:T(8,128)(2,1)}, bf16[2,3,64,160]{3,2,1,0:T(8,128)(2,1)S(1)}, u32[]{:S(2)}, u32[]{:S(2)}) collective-permute-start(bf16[2,3,64,160]{3,2,1,0:T(8,128)(2,1)} %get-tuple-element.157), channel_id=1, source_target_pairs={{0,2},{1,3},{2,0},{3,1},{4,6},{5,7},{6,4},{7,5},{8,10},{9,11},{10,... | collective-permute-start | bytes 368648 | tf_op jit(solution)/shard_map/ppermute | solution.py:270
  126.1 18.3 %collective-permute-start.34 = (bf16[2,3,64,160]{3,2,1,0:T(8,128)(2,1)}, bf16[2,3,64,160]{3,2,1,0:T(8,128)(2,1)S(1)}, u32[]{:S(2)}, u32[]{:S(2)}) collective-permute-start(bf16[2,3,64,160]{3,2,1,0:T(8,128)(2,1)} %get-tuple-element.158), channel_id=1, source_target_pairs={{0,4},{1,5},{2,6},{3,7},{4,0},{5,1},{6,2},{7,3},{8,12},{9,13},{10,... | collective-permute-start | bytes 368648 | tf_op jit(solution)/shard_map/ppermute | solution.py:270
  126.9 17.6 %collective-permute-start.35 = (bf16[2,3,64,160]{3,2,1,0:T(8,128)(2,1)}, bf16[2,3,64,160]{3,2,1,0:T(8,128)(2,1)}, u32[]{:S(2)}, u32[]{:S(2)}) collective-permute-start(bf16[2,3,64,160]{3,2,1,0:T(8,128)(2,1)} %get-tuple-element.159), channel_id=1, source_target_pairs={{0,6},{1,7},{2,4},{3,5},{4,2},{5,3},{6,0},{7,1},{8,14},{9,15},{10,... | collective-permute-start | bytes 368648 | tf_op jit(solution)/shard_map/ppermute | solution.py:270
  151.7 10.4 %collective-permute-start.36 = (bf16[128,1280]{1,0:T(8,128)(2,1)}, bf16[128,1280]{1,0:T(8,128)(2,1)S(1)}, u32[]{:S(2)}, u32[]{:S(2)}) collective-permute-start(bf16[128,1280]{1,0:T(8,128)(2,1)} %get-tuple-element.164), channel_id=1, source_target_pairs={{0,8},{8,0},{16,24},{24,16},{1,9},{9,1},{17,25},{25,17},{2,10},{10... | collective-permute-start | bytes 983048 | tf_op jit(solution)/shard_map/ppermute | solution.py:278
  157.8 18.9 %collective-permute-start.38 = (bf16[768,256]{1,0:T(8,128)(2,1)}, bf16[768,256]{1,0:T(8,128)(2,1)S(1)}, u32[]{:S(2)}, u32[]{:S(2)}) collective-permute-start(bf16[768,256]{1,0:T(8,128)(2,1)} %get-tuple-element.171), channel_id=1, source_target_pairs={{0,2},{1,3},{2,0},{3,1},{4,6},{5,7},{6,4},{7,5},{8,10},{9,11},{10,... | collective-permute-start | bytes 1179656 | tf_op jit(solution)/shard_map/ppermute | solution.py:270
  159.2 19.5 %collective-permute-start.39 = (bf16[768,256]{1,0:T(8,128)(2,1)}, bf16[768,256]{1,0:T(8,128)(2,1)S(1)}, u32[]{:S(2)}, u32[]{:S(2)}) collective-permute-start(bf16[768,256]{1,0:T(8,128)(2,1)} %get-tuple-element.172), channel_id=1, source_target_pairs={{0,4},{1,5},{2,6},{3,7},{4,0},{5,1},{6,2},{7,3},{8,12},{9,13},{10,... | collective-permute-start | bytes 1179656 | tf_op jit(solution)/shard_map/ppermute | solution.py:270
  160.0 18.7 %collective-permute-start.40 = (bf16[768,256]{1,0:T(8,128)(2,1)}, bf16[768,256]{1,0:T(8,128)(2,1)S(1)}, u32[]{:S(2)}, u32[]{:S(2)}) collective-permute-start(bf16[768,256]{1,0:T(8,128)(2,1)} %get-tuple-element.173), channel_id=1, source_target_pairs={{0,6},{1,7},{2,4},{3,5},{4,2},{5,3},{6,0},{7,1},{8,14},{9,15},{10,... | collective-permute-start | bytes 1179656 | tf_op jit(solution)/shard_map/ppermute | solution.py:270
  164.7 18.0 %collective-permute-start.42 = (bf16[128,1280]{1,0:T(8,128)(2,1)S(1)}, bf16[128,1280]{1,0:T(8,128)(2,1)S(1)}, u32[]{:S(2)}, u32[]{:S(2)}) collective-permute-start(bf16[128,1280]{1,0:T(8,128)(2,1)S(1)} %copy-done.37), channel_id=1, source_target_pairs={{0,8},{8,0},{16,24},{24,16},{1,9},{9,1},{17,25},{25,17},{2,10},{10... | collective-permute-start | bytes 983048 | tf_op jit(solution)/shard_map/ppermute | solution.py:278
  166.5 17.1 %collective-permute-start.43 = (bf16[128,1280]{1,0:T(8,128)(2,1)}, bf16[128,1280]{1,0:T(8,128)(2,1)S(1)}, u32[]{:S(2)}, u32[]{:S(2)}) collective-permute-start(bf16[128,1280]{1,0:T(8,128)(2,1)} %osum.1.refs_5_), channel_id=1, source_target_pairs={{0,16},{8,24},{16,0},{24,8},{1,17},{9,25},{17,1},{25,9},{2,18},{10... | collective-permute-start | bytes 983048 | tf_op jit(solution)/shard_map/ppermute | solution.py:278
  186.3 17.3 %collective-permute-start.47 = (bf16[128,1280]{1,0:T(8,128)(2,1)}, bf16[128,1280]{1,0:T(8,128)(2,1)S(1)}, u32[]{:S(2)}, u32[]{:S(2)}) collective-permute-start(bf16[128,1280]{1,0:T(8,128)(2,1)} %ototal.1.refs_3_.refs_0_), channel_id=1, source_target_pairs={{0,16},{8,24},{16,0},{24,8},{1,17},{9,25},{17,1},{25,9},{2,18},{10... | collective-permute-start | bytes 983048 | tf_op jit(solution)/shard_map/ppermute | solution.py:278
  192.1 15.4 %collective-permute-start.49 = (bf16[128,1280]{1,0:T(8,128)(2,1)S(1)}, bf16[128,1280]{1,0:T(8,128)(2,1)S(1)}, u32[]{:S(2)}, u32[]{:S(2)}) collective-permute-start(bf16[128,1280]{1,0:T(8,128)(2,1)S(1)} %copy-done.1), channel_id=1, source_target_pairs={{0,8},{8,0},{16,24},{24,16},{1,9},{9,1},{17,25},{25,17},{2,10},{10... | collective-permute-start | bytes 983048 | tf_op jit(solution)/shard_map/ppermute | solution.py:278
  192.4 14.1 %collective-permute-start.44 = (bf16[192,256]{1,0:T(8,128)(2,1)}, bf16[192,256]{1,0:T(8,128)(2,1)S(1)}, u32[]{:S(2)}, u32[]{:S(2)}) collective-permute-start(bf16[192,256]{1,0:T(8,128)(2,1)} %get-tuple-element.182), channel_id=1, source_target_pairs={{0,16},{8,24},{16,0},{24,8},{1,17},{9,25},{17,1},{25,9},{2,18},{10... | collective-permute-start | bytes 294920 | tf_op jit(solution)/shard_map/ppermute | solution.py:278
  204.5 11.8 %collective-permute-start.51 = (bf16[128,1280]{1,0:T(8,128)(2,1)S(1)}, bf16[128,1280]{1,0:T(8,128)(2,1)S(1)}, u32[]{:S(2)}, u32[]{:S(2)}) collective-permute-start(bf16[128,1280]{1,0:T(8,128)(2,1)S(1)} %collective-permute-done.47.refs_4_.refs_2_), channel_id=1, source_target_pairs={{0,8},{8,0},{16,24},{24,16},{1,9},{9,1},{17,25},{25,17},{2,10},{10... | collective-permute-start | bytes 983048 | tf_op jit(solution)/shard_map/ppermute | solution.py:278
  209.8 10.1 %collective-permute-start.50 = (bf16[208,256]{1,0:T(8,128)(2,1)}, bf16[208,256]{1,0:T(8,128)(2,1)S(1)}, u32[]{:S(2)}, u32[]{:S(2)}) collective-permute-start(bf16[208,256]{1,0:T(8,128)(2,1)} %qtotal.1.refs_4_), channel_id=1, source_target_pairs={{0,16},{8,24},{16,0},{24,8},{1,17},{9,25},{17,1},{25,9},{2,18},{10... | collective-permute-start | bytes 319496 | tf_op jit(solution)/shard_map/ppermute | solution.py:278
  210.4 10.4 %collective-permute-start.52 = (bf16[208,256]{1,0:T(8,128)(2,1)}, bf16[208,256]{1,0:T(8,128)(2,1)S(1)}, u32[]{:S(2)}, u32[]{:S(2)}) collective-permute-start(bf16[208,256]{1,0:T(8,128)(2,1)} %qtotal.1.refs_4_), channel_id=1, source_target_pairs={{0,8},{8,0},{16,24},{24,16},{1,9},{9,1},{17,25},{25,17},{2,10},{10... | collective-permute-start | bytes 319496 | tf_op jit(solution)/shard_map/ppermute | solution.py:278
  (71 other events, 264.5 us)

commit v5 on v4

--- a/solution.py
+++ b/solution.py
@@ -966,7 +966,6 @@
         name="finish_latent",
         cost=1024,
     )
-    q2, init_sum = tie(q2, init_sum)
     q3 = send_z(q2, 1)
     key_g, value_g, query_g, init_g, byte_n, mixer_n, query_n = call(
         finish_kernel,

time: 230 us -> 228 us (level)
  waiting for transfers between devices: 53.4 us -> 50.1 us
    ppermute x11, waiting for transfers between devices: 9.5 us -> 6.23 us  [send_z(): return lax.ppermute(x, 'rep', [(i, i ^ k) for i in range(NZ)])]
  transfers between devices with their start and end apart: 54 -> 54, of which waited for: 22 -> 21; matrix products, arithmetic and copies ran while one was open for 0% -> 0% of each run, Pallas kernels for 40% -> 41%
where the time goes in v5:
time: 228 us; the launch traced here: 227 us
  Pallas kernels  109 us (48%)
  starting transfers between devices  52.3 us (23%)
  waiting for transfers between devices  50.1 us (22%)
  local copies, waits for them, and re-layouts  13.8 us (6%)
    pallas_call x25, Pallas kernels, call(): pl.pallas_call(run, grid=grid, out_shape=out, in_specs=[ANY] * ahead + li...  109 us
    ppermute x34, waiting for transfers between devices, send(): return lax.ppermute(x, 'fsdp', [(i, i ^ k) for i in range(N)])  25.5 us
    ppermute x34, starting transfers between devices, send(): return lax.ppermute(x, 'fsdp', [(i, i ^ k) for i in range(N)])  19.5 us
    ppermute x11, starting transfers between devices, send_z(): return lax.ppermute(x, 'rep', [(i, i ^ k) for i in range(NZ)])  18.8 us
    ppermute x9, waiting for transfers between devices, send_split(): lax.ppermute(x, 'fsdp', [(i, i ^ (odd if i & 1 else even)) for i in range...  18.4 us
    ppermute x9, starting transfers between devices, send_split(): lax.ppermute(x, 'fsdp', [(i, i ^ (odd if i & 1 else even)) for i in range...  14 us
    unnamed x98, local copies, waits for them, and re-layouts  13.8 us
    ppermute x11, waiting for transfers between devices, send_z(): return lax.ppermute(x, 'rep', [(i, i ^ k) for i in range(NZ)])  6.23 us
  transfers between devices with their start and end apart: 54, of which 21 were waited for; matrix products, arithmetic and copies ran while one was open for 0% of the time, Pallas kernels for 41%

profile of v5, /device:TPU:0, one launch (start us, length us, event | category | flops | bytes accessed | tf_op | source)
XLA Modules:
  0.0 226.7 jit_solution(3599005430063996782)
XLA Ops:
  2.5 3.0 %collective-permute-start.1 = (bf16[896,256]{1,0:T(8,128)(2,1)}, bf16[896,256]{1,0:T(8,128)(2,1)}, u32[]{:S(2)}, u32[]{:S(2)}) collective-permute-start(bf16[896,256]{1,0:T(8,128)(2,1)} %pack.1.refs_3_.refs_2_.refs_1_), channel_id=1, source_target_pairs={{0,4},{1,3},{2,6},{3,1},{4,0},{5,7},{6,2},{7,5},{8,12},{9,11},{10,... | collective-permute-start | bytes 1376264 | tf_op jit(solution)/shard_map/ppermute | solution.py:274
  7.0 2.4 %pack_rows.1.refs_2_.refs_7_ = bf16[480,1280]{1,0:T(8,128)(2,1)} custom-call(bf16[160,1280]{1,0:T(8,128)(2,1)} %refs_0_.4, bf16[160,1280]{1,0:T(8,128)(2,1)} %refs_1_.11, bf16[160,1280]{1,0:T(8,128)(2,1)} %refs_2_.5, bf16[896,256]{1,0:T(8,128)(2,1)} %pack.1.refs_3_.refs_2_.refs_1_), custom_call_target="tpu_custom_call" | custom-call | flops 99999997952 | bytes 1024 | tf_op jit(solution)/shard_map/pack_rows/pallas_call | solution.py:302
  9.4 3.7 %norm.1.refs_0_ = bf16[1024,768]{1,0:T(8,128)(2,1)} custom-call(bf16[1024,768]{1,0:T(8,128)(2,1)} %bitcast.3, f32[768]{0:T(1024)} %refs_7_.1, bf16[480,1280]{1,0:T(8,128)(2,1)} %pack_rows.1.refs_2_.refs_7_), custom_call_target="tpu_custom_call" | custom-call | flops 99999997952 | bytes 1024 | tf_op jit(solution)/shard_map/norm/pallas_call | solution.py:302
  13.0 3.6 %collective-permute-done.1.refs_5_.refs_4_ = bf16[896,256]{1,0:T(8,128)(2,1)} collective-permute-done((bf16[896,256]{1,0:T(8,128)(2,1)}, bf16[896,256]{1,0:T(8,128)(2,1)}, u32[]{:S(2)}, u32[]{:S(2)}) %collective-permute-start.1) | collective-permute-done | bytes 458784 | tf_op jit(solution)/shard_map/ppermute | solution.py:274
  19.8 6.1 %collective-permute-done.2.refs_6_.refs_5_ = bf16[896,256]{1,0:T(8,128)(2,1)S(1)} collective-permute-done((bf16[896,256]{1,0:T(8,128)(2,1)}, bf16[896,256]{1,0:T(8,128)(2,1)S(1)}, u32[]{:S(2)}, u32[]{:S(2)}) %collective-permute-start.2) | collective-permute-done | bytes 458784 | tf_op jit(solution)/shard_map/ppermute | solution.py:274
  30.3 5.2 %query.1 = (bf16[1024,256]{1,0:T(8,128)(2,1)}, bf16[768,256]{1,0:T(8,128)(2,1)}, bf16[1280,256]{1,0:T(8,128)(2,1)}, bf16[256,256]{1,0:T(8,128)(2,1)}, bf16[256,1280]{1,0:T(8,128)(2,1)}) custom-call(bf16[1024,768]{1,0:T(8,128)(2,1)} %norm.1.refs_0_, f32[1280]{0:T(1024)} %refs_2_.7, bf16[896,256]{1,0:T(8,128)(2,1)} %pack.1.refs_3_.refs_2_.refs_1_, ...), custom_call_target="tpu_custom_call" | custom-call | flops 99999997952 | bytes 1024 | tf_op jit(solution)/shard_map/query/pallas_call | solution.py:302
  35.6 6.8 %scores.1 = (bf16[2,8,256,512]{3,2,1,0:T(8,128)(2,1)}, f32[2,256,128]{2,1,0:T(8,128)}) custom-call(s32[2]{0:T(128)} %refs_0_.5, bf16[1024,256]{1,0:T(8,128)(2,1)} %get-tuple-element.111.refs_1_.refs_0_, bf16[256,256]{1,0:T(8,128)(2,1)} %get-tuple-element.114.refs_2_), custom_call_target="tpu_custom_call" | custom-call | flops 99999997952 | bytes 1024 | tf_op jit(solution)/shard_map/scores/pallas_call | solution.py:302
  43.4 7.0 %values.1 = (bf16[1280,1024]{1,0:T(8,128)(2,1)}, bf16[768,1280]{1,0:T(8,128)(2,1)}) custom-call(bf16[1024,768]{1,0:T(8,128)(2,1)} %norm.1.refs_0_, bf16[896,256]{1,0:T(8,128)(2,1)} %pack.1.refs_3_.refs_2_.refs_1_, bf16[896,256]{1,0:T(8,128)(2,1)} %copy-done.28, bf16[896,256]{1,0:T(8,128)(2,1)} %collective-permute-done.refs_4_.refs_3_, ...), custom_call_target="tpu_custom_call" | custom-call | flops 99999997952 | bytes 1024 | tf_op jit(solution)/shard_map/values/pallas_call | solution.py:302
  50.4 4.4 %collective-permute-done.8.refs_9_ = bf16[480,1280]{1,0:T(8,128)(2,1)} collective-permute-done((bf16[480,1280]{1,0:T(8,128)(2,1)}, bf16[480,1280]{1,0:T(8,128)(2,1)}, u32[]{:S(2)}, u32[]{:S(2)}) %collective-permute-start.8) | collective-permute-done | bytes 1228832 | tf_op jit(solution)/shard_map/ppermute | solution.py:274
  58.2 4.4 %sums.2 = (bf16[4,64,1408]{2,1,0:T(8,128)(2,1)}, bf16[4,64,1408]{2,1,0:T(8,128)(2,1)}) custom-call(bf16[1280,1024]{1,0:T(8,128)(2,1)} %get-tuple-element.118.refs_0_.refs_1_, bf16[2,8,256,512]{3,2,1,0:T(8,128)(2,1)} %get-tuple-element.115.refs_9_.refs_1_.refs_3_, f32[2,256,128]{2,1,0:T(8,128)} %get-tuple-element.119.refs_2_), custom_call_target="tpu_custom_call" | custom-call | flops 99999997952 | bytes 1024 | tf_op jit(solution)/shard_map/sums/pallas_call | solution.py:302
  62.6 4.4 %sums.3 = (bf16[4,64,1408]{2,1,0:T(8,128)(2,1)}, bf16[4,64,1408]{2,1,0:T(8,128)(2,1)}) custom-call(bf16[1280,1024]{1,0:T(8,128)(2,1)} %get-tuple-element.118.refs_0_.refs_1_, bf16[2,8,256,512]{3,2,1,0:T(8,128)(2,1)} %get-tuple-element.115.refs_9_.refs_1_.refs_3_, ...), custom_call_target="tpu_custom_call", output_to_operand_aliasing={{0}: (3, {}), {1}: (4, {})} | custom-call | flops 99999997952 | bytes 1024 | tf_op jit(solution)/shard_map/sums/pallas_call | solution.py:302
  67.0 2.4 %collective-permute-done.10.refs_1_ = bf16[4,64,1408]{2,1,0:T(8,128)(2,1)S(1)} collective-permute-done((bf16[4,64,1408]{2,1,0:T(8,128)(2,1)}, bf16[4,64,1408]{2,1,0:T(8,128)(2,1)S(1)}, u32[]{:S(2)}, u32[]{:S(2)}) %collective-permute-start.10) | collective-permute-done | bytes 720928 | tf_op jit(solution)/shard_map/ppermute | solution.py:270
  76.5 4.1 %collective-permute-done.14.refs_1_ = bf16[64,1408]{1,0:T(8,128)(2,1)S(1)} collective-permute-done((bf16[64,1408]{1,0:T(8,128)(2,1)}, bf16[64,1408]{1,0:T(8,128)(2,1)S(1)}, u32[]{:S(2)}, u32[]{:S(2)}) %collective-permute-start.14) | collective-permute-done | bytes 180256 | tf_op jit(solution)/shard_map/ppermute | solution.py:270
  80.6 3.2 %collective-permute-done.15.refs_2_ = bf16[64,1408]{1,0:T(8,128)(2,1)S(1)} collective-permute-done((bf16[64,1408]{1,0:T(8,128)(2,1)}, bf16[64,1408]{1,0:T(8,128)(2,1)S(1)}, u32[]{:S(2)}, u32[]{:S(2)}) %collective-permute-start.15) | collective-permute-done | bytes 180256 | tf_op jit(solution)/shard_map/ppermute | solution.py:270
  86.3 11.4 %latent.1 = (bf16[64,1280]{1,0:T(8,128)(2,1)}, bf16[3,64,1280]{2,1,0:T(8,128)(2,1)}, bf16[4,3,64,160]{3,2,1,0:T(8,128)(2,1)}, bf16[4,3,64,160]{3,2,1,0:T(8,128)(...) custom-call(bf16[64,1408]{1,0:T(8,128)(2,1)} %get-tuple-element.127.refs_0_, bf16[64,1408]{1,0:T(8,128)(2,1)} %copy-done.44, ...), custom_call_target="tpu_custom_call" | custom-call | flops 99999997952 | bytes 1024 | tf_op jit(solution)/shard_map/latent/pallas_call | solution.py:302
  101.8 4.6 %collective-permute-done.21.refs_10_ = bf16[64,1408]{1,0:T(8,128)(2,1)S(1)} collective-permute-done((bf16[64,1408]{1,0:T(8,128)(2,1)}, bf16[64,1408]{1,0:T(8,128)(2,1)S(1)}, u32[]{:S(2)}, u32[]{:S(2)}) %collective-permute-start.21) | collective-permute-done | bytes 180256 | tf_op jit(solution)/shard_map/ppermute | solution.py:270
  106.4 2.5 %collective-permute-done.20.refs_8_ = bf16[64,1408]{1,0:T(8,128)(2,1)S(1)} collective-permute-done((bf16[64,1408]{1,0:T(8,128)(2,1)}, bf16[64,1408]{1,0:T(8,128)(2,1)S(1)}, u32[]{:S(2)}, u32[]{:S(2)}) %collective-permute-start.20) | collective-permute-done | bytes 180256 | tf_op jit(solution)/shard_map/ppermute | solution.py:270
  112.9 8.5 %backward.2 = (bf16[1536,1024]{1,0:T(8,128)(2,1)}, f32[256,256]{1,0:T(8,128)}, bf16[2,3,64,160]{3,2,1,0:T(8,128)(2,1)}, bf16[2,3,64,160]{3,2,1,0:T(8,128)(2,1)}, bf16[2,3,64,160]{3,2,1,0:T(8,128)(2,1)}) custom-call(bf16[1024,256]{1,0:T(8,128)(2,1)} %get-tuple-element.111.refs_1_.refs_0_, bf16[1280,1024]{1,0:T(8,128)(2,1)} %get-tuple-element.118.refs_0_.refs_1_, ...), custom_call_target="tpu_custom_call" | custom-call | flops 99999997952 | bytes 1024 | tf_op jit(solution)/shard_map/backward/pallas_call | solution.py:302
  121.4 2.5 %collective-permute-done.27.refs_6_ = bf16[3,64,1280]{2,1,0:T(8,128)(2,1)S(1)} collective-permute-done((bf16[3,64,1280]{2,1,0:T(8,128)(2,1)}, bf16[3,64,1280]{2,1,0:T(8,128)(2,1)S(1)}, u32[]{:S(2)}, u32[]{:S(2)}) %collective-permute-start.27) | collective-permute-done | bytes 491552 | tf_op jit(solution)/shard_map/ppermute | solution.py:274
  128.2 8.3 %backward.3 = (bf16[1536,1024]{1,0:T(8,128)(2,1)}, f32[256,256]{1,0:T(8,128)}) custom-call(bf16[1024,256]{1,0:T(8,128)(2,1)} %get-tuple-element.111.refs_1_.refs_0_, bf16[1280,1024]{1,0:T(8,128)(2,1)} %get-tuple-element.118.refs_0_.refs_1_, bf16[256,256]{1,0:T(8,128)(2,1)} %get-tuple-element.114.refs_2_, ...), custom_call_target="tpu_custom_call", output_to_operand_aliasing={{0}: (12, {})} | custom-call | flops 1024 | bytes 1024 | tf_op jit(solution)/shard_map/backward/pallas_call | solution.py:302
  137.1 7.2 %weights.1 = (bf16[4,768,256]{2,1,0:T(8,128)(2,1)}, bf16[4,768,256]{2,1,0:T(8,128)(2,1)}) custom-call(bf16[1024,768]{1,0:T(8,128)(2,1)} %norm.1.refs_0_, bf16[256,1280]{1,0:T(8,128)(2,1)} %get-tuple-element.158.refs_1_, bf16[1536,1024]{1,0:T(8,128)(2,1)} %get-tuple-element.146.refs_2_.refs_4_, f32[256,256]{1,0:T(8,128)} %get-tuple-element.145.refs_13_.refs_3_, ...), custom_call_target="tpu_custom_call" | custom-call | flops 99999997952 | bytes 1024 | tf_op jit(solution)/shard_map/weights/pallas_call | solution.py:302
  145.5 6.2 %latent_grads.1 = (bf16[128,1280]{1,0:T(8,128)(2,1)}, bf16[128,1280]{1,0:T(8,128)(2,1)}, bf16[128,1280]{1,0:T(8,128)(2,1)}, bf16[128,1280]{1,0:T(8,128)(2,1)}, f32[8,160]{1,0:T(8,128)}) custom-call(f32[32,1280]{1,0:T(8,128)} %get-tuple-element.147.refs_0_, bf16[160,1280]{1,0:T(8,128)(2,1)} %refs_1_.11, f32[1280]{0:T(1024)} %refs_2_.6, ...), custom_call_target="tpu_custom_call" | custom-call | flops 99999997952 | bytes 1024 | tf_op jit(solution)/shard_map/latent_grads/pallas_call | solution.py:302
  154.7 3.1 %add4g.1 = (bf16[768,256]{1,0:T(8,128)(2,1)}, bf16[768,256]{1,0:T(8,128)(2,1)}, bf16[768,256]{1,0:T(8,128)(2,1)}, bf16[768,256]{1,0:T(8,128)(2,1)}) custom-call(bf16[4,768,256]{2,1,0:T(8,128)(2,1)} %get-tuple-element.163.refs_0_, bf16[4,768,256]{2,1,0:T(8,128)(2,1)} %copy-done.18, bf16[128,1280]{1,0:T(8,128)(2,1)} %get-tuple-element.164.refs_2_.refs_1_), custom_call_target="tpu_custom_call" | custom-call | flops 99999997952 | bytes 1024 | tf_op jit(solution)/shard_map/add4g/pallas_call | solution.py:302
  166.5 2.6 %collective-permute-start.42 = (bf16[128,1280]{1,0:T(8,128)(2,1)}, bf16[128,1280]{1,0:T(8,128)(2,1)S(1)}, u32[]{:S(2)}, u32[]{:S(2)}) collective-permute-start(bf16[128,1280]{1,0:T(8,128)(2,1)} %osum.1.refs_5_), channel_id=1, source_target_pairs={{0,16},{8,24},{16,0},{24,8},{1,17},{9,25},{17,1},{25,9},{2,18},{10... | collective-permute-start | bytes 983048 | tf_op jit(solution)/shard_map/ppermute | solution.py:278
  169.1 7.6 %bytes.1.refs_10_ = f32[2,512,768]{2,1,0:T(8,128)} custom-call(bf16[1024,768]{1,0:T(8,128)(2,1)} %bitcast.4, f32[768]{0:T(1024)} %refs_7_.1, bf16[768,256]{1,0:T(8,128)(2,1)} %get-tuple-element.133.refs_2_, bf16[768,1280]{1,0:T(8,128)(2,1)} %get-tuple-element.134.refs_3_, bf16[1536,1024]{1,0:T(8,128)(2,1)} %get-tuple-element.146.refs_2_.refs_4_, ...), custom_call_target="tpu_custom_call" | custom-call | flops 1024 | bytes 1024 | tf_op jit(solution)/shard_map/bytes/pallas_call | solution.py:302
  179.6 2.8 %gsum.1 = (bf16[192,256]{1,0:T(8,128)(2,1)}, bf16[192,256]{1,0:T(8,128)(2,1)}, bf16[384,256]{1,0:T(8,128)(2,1)}, bf16[16,256]{1,0:T(8,128)(2,1)}) custom-call(bf16[768,256]{1,0:T(8,128)(2,1)} %get-tuple-element.165.refs_2_.refs_0_, bf16[768,256]{1,0:T(8,128)(2,1)} %copy-done.34, bf16[768,256]{1,0:T(8,128)(2,1)} %copy-done.35, bf16[768,256]{1,0:T(8,128)(2,1)} %copy-done.36, ...), custom_call_target="tpu_custom_call" | custom-call | flops 99999997952 | bytes 1024 | tf_op jit(solution)/shard_map/gsum/pallas_call | solution.py:302
  192.4 2.4 %collective-permute-start.49 = (bf16[192,256]{1,0:T(8,128)(2,1)}, bf16[192,256]{1,0:T(8,128)(2,1)S(1)}, u32[]{:S(2)}, u32[]{:S(2)}) collective-permute-start(bf16[192,256]{1,0:T(8,128)(2,1)} %get-tuple-element.184), channel_id=1, source_target_pairs={{0,16},{8,24},{16,0},{24,8},{1,17},{9,25},{17,1},{25,9},{2,18},{10... | collective-permute-start | bytes 294920 | tf_op jit(solution)/shard_map/ppermute | solution.py:278
  198.7 3.0 %collective-permute-done.46.refs_1_ = bf16[16,256]{1,0:T(8,128)(2,1)S(1)} collective-permute-done((bf16[16,256]{1,0:T(8,128)(2,1)}, bf16[16,256]{1,0:T(8,128)(2,1)S(1)}, u32[]{:S(2)}, u32[]{:S(2)}) %collective-permute-start.46) | collective-permute-done | bytes 8224 | tf_op jit(solution)/shard_map/ppermute | solution.py:270
  210.4 3.2 %collective-permute-start.51 = (bf16[208,256]{1,0:T(8,128)(2,1)}, bf16[208,256]{1,0:T(8,128)(2,1)S(1)}, u32[]{:S(2)}, u32[]{:S(2)}) collective-permute-start(bf16[208,256]{1,0:T(8,128)(2,1)} %qtotal.1.refs_4_), channel_id=1, source_target_pairs={{0,8},{8,0},{16,24},{24,16},{1,9},{9,1},{17,25},{25,17},{2,10},{10... | collective-permute-start | bytes 319496 | tf_op jit(solution)/shard_map/ppermute | solution.py:278
  213.6 3.4 %collective-permute-done.52.refs_6_ = bf16[208,256]{1,0:T(8,128)(2,1)S(1)} collective-permute-done((bf16[208,256]{1,0:T(8,128)(2,1)}, bf16[208,256]{1,0:T(8,128)(2,1)S(1)}, u32[]{:S(2)}, u32[]{:S(2)}) %collective-permute-start.52) | collective-permute-done | bytes 106528 | tf_op jit(solution)/shard_map/ppermute | solution.py:278
  219.6 2.9 %finish_latent.1 = (f32[160,1280]{1,0:T(8,128)}, f32[160,1280]{1,0:T(8,128)}, f32[160,1280]{1,0:T(8,128)}, f32[32,1280]{1,0:T(8,128)}) custom-call(bf16[128,1280]{1,0:T(8,128)(2,1)} %ototal.1.refs_3_.refs_0_, bf16[128,1280]{1,0:T(8,128)(2,1)} %copy-done.3, bf16[128,1280]{1,0:T(8,128)(2,1)} %copy-done.2, bf16[128,1280]{1,0:T(8,128)(2,1)} %copy-done.4), custom_call_target="tpu_custom_call" | custom-call | flops 1024 | bytes 1024 | tf_op jit(solution)/shard_map/finish_latent/pallas_call | solution.py:302
  223.2 3.5 %finish.1 = (f32[96,256]{1,0:T(8,128)}, f32[96,1280]{1,0:T(8,128)}, f32[160,256]{1,0:T(8,128)}, f32[32,1280]{1,0:T(8,128)}, f32[768]{0:T(1024)}, /*index=5*/f32[1280]{0:T(1024)}, f32[1280]{0:T(1024)}) custom-call(bf16[1280,256]{1,0:T(8,128)(2,1)} %get-tuple-element.168.refs_0_, bf16[32,1280]{1,0:T(8,128)(2,1)} %refs_1_.13, f32[1280]{0:T(1024)} %refs_2_.7, ...), custom_call_target="tpu_custom_call" | custom-call | flops 1024 | bytes 1024 | tf_op jit(solution)/shard_map/finish/pallas_call | solution.py:302
  (199 shorter events, 79.2 us)
Async XLA Ops:
  2.5 14.1 %collective-permute-start.1 = (bf16[896,256]{1,0:T(8,128)(2,1)}, bf16[896,256]{1,0:T(8,128)(2,1)}, u32[]{:S(2)}, u32[]{:S(2)}) collective-permute-start(bf16[896,256]{1,0:T(8,128)(2,1)} %pack.1.refs_3_.refs_2_.refs_1_), channel_id=1, source_target_pairs={{0,4},{1,3},{2,6},{3,1},{4,0},{5,7},{6,2},{7,5},{8,12},{9,11},{10,... | collective-permute-start | bytes 1376264 | tf_op jit(solution)/shard_map/ppermute | solution.py:274
  5.5 11.2 %collective-permute-start = (bf16[896,256]{1,0:T(8,128)(2,1)}, bf16[896,256]{1,0:T(8,128)(2,1)}, u32[]{:S(2)}, u32[]{:S(2)}) collective-permute-start(bf16[896,256]{1,0:T(8,128)(2,1)} %pack.1.refs_3_.refs_2_.refs_1_), channel_id=1, source_target_pairs={{0,2},{1,5},{2,0},{3,7},{4,6},{5,1},{6,4},{7,3},{8,10},{9,13},{10,... | collective-permute-start | bytes 1376264 | tf_op jit(solution)/shard_map/ppermute | solution.py:274
  19.2 9.4 %collective-permute-start.4 = (bf16[896,256]{1,0:T(8,128)(2,1)}, bf16[896,256]{1,0:T(8,128)(2,1)S(1)}, u32[]{:S(2)}, u32[]{:S(2)}) collective-permute-start(bf16[896,256]{1,0:T(8,128)(2,1)} %collective-permute-done.refs_4_.refs_3_), channel_id=1, source_target_pairs={{0,1},{1,0},{2,3},{3,2},{4,5},{5,4},{6,7},{7,6},{8,9},{9,8},{10,11... | collective-permute-start | bytes 1376264 | tf_op jit(solution)/shard_map/ppermute | solution.py:270
  19.2 9.3 %collective-permute-start.5 = (bf16[896,256]{1,0:T(8,128)(2,1)}, bf16[896,256]{1,0:T(8,128)(2,1)S(1)}, u32[]{:S(2)}, u32[]{:S(2)}) collective-permute-start(bf16[896,256]{1,0:T(8,128)(2,1)} %collective-permute-done.1.refs_5_.refs_4_), channel_id=1, source_target_pairs={{0,1},{1,0},{2,3},{3,2},{4,5},{5,4},{6,7},{7,6},{8,9},{9,8},{10,11... | collective-permute-start | bytes 1376264 | tf_op jit(solution)/shard_map/ppermute | solution.py:270
  25.9 28.9 %collective-permute-start.8 = (bf16[480,1280]{1,0:T(8,128)(2,1)}, bf16[480,1280]{1,0:T(8,128)(2,1)}, u32[]{:S(2)}, u32[]{:S(2)}) collective-permute-start(bf16[480,1280]{1,0:T(8,128)(2,1)} %pack_rows.1.refs_2_.refs_7_), channel_id=1, source_target_pairs={{0,2},{1,5},{2,0},{3,7},{4,6},{5,1},{6,4},{7,3},{8,10},{9,13},{10,... | collective-permute-start | bytes 3686408 | tf_op jit(solution)/shard_map/ppermute | solution.py:274
  26.9 29.1 %collective-permute-start.9 = (bf16[480,1280]{1,0:T(8,128)(2,1)}, bf16[480,1280]{1,0:T(8,128)(2,1)}, u32[]{:S(2)}, u32[]{:S(2)}) collective-permute-start(bf16[480,1280]{1,0:T(8,128)(2,1)} %pack_rows.1.refs_2_.refs_7_), channel_id=1, source_target_pairs={{0,4},{1,3},{2,6},{3,1},{4,0},{5,7},{6,2},{7,5},{8,12},{9,11},{10,... | collective-permute-start | bytes 3686408 | tf_op jit(solution)/shard_map/ppermute | solution.py:274
  55.9 17.0 %collective-permute-start.13 = (bf16[480,1280]{1,0:T(8,128)(2,1)}, bf16[480,1280]{1,0:T(8,128)(2,1)}, u32[]{:S(2)}, u32[]{:S(2)}) collective-permute-start(bf16[480,1280]{1,0:T(8,128)(2,1)} %collective-permute-done.8.refs_9_), channel_id=1, source_target_pairs={{0,4},{1,3},{2,6},{3,1},{4,0},{5,7},{6,2},{7,5},{8,12},{9,11},{10,... | collective-permute-start | bytes 3686408 | tf_op jit(solution)/shard_map/ppermute | solution.py:274
  57.7 11.7 %collective-permute-start.11 = (bf16[480,1280]{1,0:T(8,128)(2,1)}, bf16[480,1280]{1,0:T(8,128)(2,1)}, u32[]{:S(2)}, u32[]{:S(2)}) collective-permute-start(bf16[480,1280]{1,0:T(8,128)(2,1)} %collective-permute-done.8.refs_9_), channel_id=1, source_target_pairs={{0,1},{1,0},{2,3},{3,2},{4,5},{5,4},{6,7},{7,6},{8,9},{9,8},{10,11... | collective-permute-start | bytes 3686408 | tf_op jit(solution)/shard_map/ppermute | solution.py:270
  57.7 11.7 %collective-permute-start.12 = (bf16[480,1280]{1,0:T(8,128)(2,1)}, bf16[480,1280]{1,0:T(8,128)(2,1)}, u32[]{:S(2)}, u32[]{:S(2)}) collective-permute-start(bf16[480,1280]{1,0:T(8,128)(2,1)} %collective-permute-done.9.refs_10_), channel_id=1, source_target_pairs={{0,1},{1,0},{2,3},{3,2},{4,5},{5,4},{6,7},{7,6},{8,9},{9,8},{10,11... | collective-permute-start | bytes 3686408 | tf_op jit(solution)/shard_map/ppermute | solution.py:270
  73.0 12.2 %collective-permute-start.17 = (bf16[480,1280]{1,0:T(8,128)(2,1)}, bf16[480,1280]{1,0:T(8,128)(2,1)S(1)}, u32[]{:S(2)}, u32[]{:S(2)}) collective-permute-start(bf16[480,1280]{1,0:T(8,128)(2,1)} %collective-permute-done.13.refs_11_), channel_id=1, source_target_pairs={{0,1},{1,0},{2,3},{3,2},{4,5},{5,4},{6,7},{7,6},{8,9},{9,8},{10,11... | collective-permute-start | bytes 3686408 | tf_op jit(solution)/shard_map/ppermute | solution.py:270
  73.7 10.2 %collective-permute-start.15 = (bf16[64,1408]{1,0:T(8,128)(2,1)}, bf16[64,1408]{1,0:T(8,128)(2,1)S(1)}, u32[]{:S(2)}, u32[]{:S(2)}) collective-permute-start(bf16[64,1408]{1,0:T(8,128)(2,1)} %get-tuple-element.129), channel_id=1, source_target_pairs={{0,4},{1,5},{2,6},{3,7},{4,0},{5,1},{6,2},{7,3},{8,12},{9,13},{10,... | collective-permute-start | bytes 540680 | tf_op jit(solution)/shard_map/ppermute | solution.py:270
  75.4 9.8 %collective-permute-start.16 = (bf16[64,1408]{1,0:T(8,128)(2,1)}, bf16[64,1408]{1,0:T(8,128)(2,1)S(1)}, u32[]{:S(2)}, u32[]{:S(2)}) collective-permute-start(bf16[64,1408]{1,0:T(8,128)(2,1)} %get-tuple-element.130), channel_id=1, source_target_pairs={{0,6},{1,7},{2,4},{3,5},{4,2},{5,3},{6,0},{7,1},{8,14},{9,15},{10,... | collective-permute-start | bytes 540680 | tf_op jit(solution)/shard_map/ppermute | solution.py:270
  99.6 9.3 %collective-permute-start.20 = (bf16[64,1408]{1,0:T(8,128)(2,1)}, bf16[64,1408]{1,0:T(8,128)(2,1)S(1)}, u32[]{:S(2)}, u32[]{:S(2)}) collective-permute-start(bf16[64,1408]{1,0:T(8,128)(2,1)} %get-tuple-element.135.refs_4_), channel_id=1, source_target_pairs={{0,4},{1,5},{2,6},{3,7},{4,0},{5,1},{6,2},{7,3},{8,12},{9,13},{10,... | collective-permute-start | bytes 540680 | tf_op jit(solution)/shard_map/ppermute | solution.py:270
  109.6 11.8 %collective-permute-start.28 = (bf16[3,64,1280]{2,1,0:T(8,128)(2,1)}, bf16[3,64,1280]{2,1,0:T(8,128)(2,1)S(1)}, u32[]{:S(2)}, u32[]{:S(2)}) collective-permute-start(bf16[3,64,1280]{2,1,0:T(8,128)(2,1)} %get-tuple-element.144.refs_3_), channel_id=1, source_target_pairs={{0,1},{1,0},{2,3},{3,2},{4,5},{5,4},{6,7},{7,6},{8,9},{9,8},{10,11... | collective-permute-start | bytes 1474568 | tf_op jit(solution)/shard_map/ppermute | solution.py:270
  110.0 13.9 %collective-permute-start.27 = (bf16[3,64,1280]{2,1,0:T(8,128)(2,1)}, bf16[3,64,1280]{2,1,0:T(8,128)(2,1)S(1)}, u32[]{:S(2)}, u32[]{:S(2)}) collective-permute-start(bf16[3,64,1280]{2,1,0:T(8,128)(2,1)} %get-tuple-element.144.refs_3_), channel_id=1, source_target_pairs={{0,4},{1,3},{2,6},{3,1},{4,0},{5,7},{6,2},{7,5},{8,12},{9,11},{10,... | collective-permute-start | bytes 1474568 | tf_op jit(solution)/shard_map/ppermute | solution.py:274
  110.6 13.3 %collective-permute-start.26 = (bf16[3,64,1280]{2,1,0:T(8,128)(2,1)}, bf16[3,64,1280]{2,1,0:T(8,128)(2,1)S(1)}, u32[]{:S(2)}, u32[]{:S(2)}) collective-permute-start(bf16[3,64,1280]{2,1,0:T(8,128)(2,1)} %get-tuple-element.144.refs_3_), channel_id=1, source_target_pairs={{0,2},{1,5},{2,0},{3,7},{4,6},{5,1},{6,4},{7,3},{8,10},{9,13},{10,... | collective-permute-start | bytes 1474568 | tf_op jit(solution)/shard_map/ppermute | solution.py:274
  123.9 12.6 %collective-permute-start.30 = (bf16[3,64,1280]{2,1,0:T(8,128)(2,1)S(1)}, bf16[3,64,1280]{2,1,0:T(8,128)(2,1)S(1)}, u32[]{:S(2)}, u32[]{:S(2)}) collective-permute-start(bf16[3,64,1280]{2,1,0:T(8,128)(2,1)S(1)} %collective-permute-done.26.refs_5_), channel_id=1, source_target_pairs={{0,1},{1,0},{2,3},{3,2},{4,5},{5,4},{6,7},{7,6},{8,9},{9,8},{10,11... | collective-permute-start | bytes 1474568 | tf_op jit(solution)/shard_map/ppermute | solution.py:270
  124.0 12.6 %collective-permute-start.29 = (bf16[3,64,1280]{2,1,0:T(8,128)(2,1)S(1)}, bf16[3,64,1280]{2,1,0:T(8,128)(2,1)}, u32[]{:S(2)}, u32[]{:S(2)}) collective-permute-start(bf16[3,64,1280]{2,1,0:T(8,128)(2,1)S(1)} %collective-permute-done.26.refs_5_), channel_id=1, source_target_pairs={{0,4},{1,3},{2,6},{3,1},{4,0},{5,7},{6,2},{7,5},{8,12},{9,11},{10,... | collective-permute-start | bytes 1474568 | tf_op jit(solution)/shard_map/ppermute | solution.py:274
  124.7 19.6 %collective-permute-start.33 = (bf16[2,3,64,160]{3,2,1,0:T(8,128)(2,1)}, bf16[2,3,64,160]{3,2,1,0:T(8,128)(2,1)S(1)}, u32[]{:S(2)}, u32[]{:S(2)}) collective-permute-start(bf16[2,3,64,160]{3,2,1,0:T(8,128)(2,1)} %get-tuple-element.155), channel_id=1, source_target_pairs={{0,2},{1,3},{2,0},{3,1},{4,6},{5,7},{6,4},{7,5},{8,10},{9,11},{10,... | collective-permute-start | bytes 368648 | tf_op jit(solution)/shard_map/ppermute | solution.py:270
  126.1 18.3 %collective-permute-start.34 = (bf16[2,3,64,160]{3,2,1,0:T(8,128)(2,1)}, bf16[2,3,64,160]{3,2,1,0:T(8,128)(2,1)S(1)}, u32[]{:S(2)}, u32[]{:S(2)}) collective-permute-start(bf16[2,3,64,160]{3,2,1,0:T(8,128)(2,1)} %get-tuple-element.156), channel_id=1, source_target_pairs={{0,4},{1,5},{2,6},{3,7},{4,0},{5,1},{6,2},{7,3},{8,12},{9,13},{10,... | collective-permute-start | bytes 368648 | tf_op jit(solution)/shard_map/ppermute | solution.py:270
  126.9 17.6 %collective-permute-start.35 = (bf16[2,3,64,160]{3,2,1,0:T(8,128)(2,1)}, bf16[2,3,64,160]{3,2,1,0:T(8,128)(2,1)}, u32[]{:S(2)}, u32[]{:S(2)}) collective-permute-start(bf16[2,3,64,160]{3,2,1,0:T(8,128)(2,1)} %get-tuple-element.157), channel_id=1, source_target_pairs={{0,6},{1,7},{2,4},{3,5},{4,2},{5,3},{6,0},{7,1},{8,14},{9,15},{10,... | collective-permute-start | bytes 368648 | tf_op jit(solution)/shard_map/ppermute | solution.py:270
  151.7 10.4 %collective-permute-start.36 = (bf16[128,1280]{1,0:T(8,128)(2,1)}, bf16[128,1280]{1,0:T(8,128)(2,1)S(1)}, u32[]{:S(2)}, u32[]{:S(2)}) collective-permute-start(bf16[128,1280]{1,0:T(8,128)(2,1)} %get-tuple-element.162), channel_id=1, source_target_pairs={{0,8},{8,0},{16,24},{24,16},{1,9},{9,1},{17,25},{25,17},{2,10},{10... | collective-permute-start | bytes 983048 | tf_op jit(solution)/shard_map/ppermute | solution.py:278
  157.8 18.9 %collective-permute-start.38 = (bf16[768,256]{1,0:T(8,128)(2,1)}, bf16[768,256]{1,0:T(8,128)(2,1)S(1)}, u32[]{:S(2)}, u32[]{:S(2)}) collective-permute-start(bf16[768,256]{1,0:T(8,128)(2,1)} %get-tuple-element.169), channel_id=1, source_target_pairs={{0,2},{1,3},{2,0},{3,1},{4,6},{5,7},{6,4},{7,5},{8,10},{9,11},{10,... | collective-permute-start | bytes 1179656 | tf_op jit(solution)/shard_map/ppermute | solution.py:270
  159.2 19.5 %collective-permute-start.39 = (bf16[768,256]{1,0:T(8,128)(2,1)}, bf16[768,256]{1,0:T(8,128)(2,1)S(1)}, u32[]{:S(2)}, u32[]{:S(2)}) collective-permute-start(bf16[768,256]{1,0:T(8,128)(2,1)} %get-tuple-element.170), channel_id=1, source_target_pairs={{0,4},{1,5},{2,6},{3,7},{4,0},{5,1},{6,2},{7,3},{8,12},{9,13},{10,... | collective-permute-start | bytes 1179656 | tf_op jit(solution)/shard_map/ppermute | solution.py:270
  160.0 18.7 %collective-permute-start.40 = (bf16[768,256]{1,0:T(8,128)(2,1)}, bf16[768,256]{1,0:T(8,128)(2,1)S(1)}, u32[]{:S(2)}, u32[]{:S(2)}) collective-permute-start(bf16[768,256]{1,0:T(8,128)(2,1)} %get-tuple-element.171), channel_id=1, source_target_pairs={{0,6},{1,7},{2,4},{3,5},{4,2},{5,3},{6,0},{7,1},{8,14},{9,15},{10,... | collective-permute-start | bytes 1179656 | tf_op jit(solution)/shard_map/ppermute | solution.py:270
  164.7 18.0 %collective-permute-start.41 = (bf16[128,1280]{1,0:T(8,128)(2,1)S(1)}, bf16[128,1280]{1,0:T(8,128)(2,1)S(1)}, u32[]{:S(2)}, u32[]{:S(2)}) collective-permute-start(bf16[128,1280]{1,0:T(8,128)(2,1)S(1)} %copy-done.37), channel_id=1, source_target_pairs={{0,8},{8,0},{16,24},{24,16},{1,9},{9,1},{17,25},{25,17},{2,10},{10... | collective-permute-start | bytes 983048 | tf_op jit(solution)/shard_map/ppermute | solution.py:278
  166.5 17.1 %collective-permute-start.42 = (bf16[128,1280]{1,0:T(8,128)(2,1)}, bf16[128,1280]{1,0:T(8,128)(2,1)S(1)}, u32[]{:S(2)}, u32[]{:S(2)}) collective-permute-start(bf16[128,1280]{1,0:T(8,128)(2,1)} %osum.1.refs_5_), channel_id=1, source_target_pairs={{0,16},{8,24},{16,0},{24,8},{1,17},{9,25},{17,1},{25,9},{2,18},{10... | collective-permute-start | bytes 983048 | tf_op jit(solution)/shard_map/ppermute | solution.py:278
  186.3 17.3 %collective-permute-start.47 = (bf16[128,1280]{1,0:T(8,128)(2,1)}, bf16[128,1280]{1,0:T(8,128)(2,1)S(1)}, u32[]{:S(2)}, u32[]{:S(2)}) collective-permute-start(bf16[128,1280]{1,0:T(8,128)(2,1)} %ototal.1.refs_3_.refs_0_), channel_id=1, source_target_pairs={{0,16},{8,24},{16,0},{24,8},{1,17},{9,25},{17,1},{25,9},{2,18},{10... | collective-permute-start | bytes 983048 | tf_op jit(solution)/shard_map/ppermute | solution.py:278
  192.1 15.4 %collective-permute-start.44 = (bf16[128,1280]{1,0:T(8,128)(2,1)S(1)}, bf16[128,1280]{1,0:T(8,128)(2,1)S(1)}, u32[]{:S(2)}, u32[]{:S(2)}) collective-permute-start(bf16[128,1280]{1,0:T(8,128)(2,1)S(1)} %copy-done.1), channel_id=1, source_target_pairs={{0,8},{8,0},{16,24},{24,16},{1,9},{9,1},{17,25},{25,17},{2,10},{10... | collective-permute-start | bytes 983048 | tf_op jit(solution)/shard_map/ppermute | solution.py:278
  192.4 14.1 %collective-permute-start.49 = (bf16[192,256]{1,0:T(8,128)(2,1)}, bf16[192,256]{1,0:T(8,128)(2,1)S(1)}, u32[]{:S(2)}, u32[]{:S(2)}) collective-permute-start(bf16[192,256]{1,0:T(8,128)(2,1)} %get-tuple-element.184), channel_id=1, source_target_pairs={{0,16},{8,24},{16,0},{24,8},{1,17},{9,25},{17,1},{25,9},{2,18},{10... | collective-permute-start | bytes 294920 | tf_op jit(solution)/shard_map/ppermute | solution.py:278
  204.5 14.3 %collective-permute-start.48 = (bf16[128,1280]{1,0:T(8,128)(2,1)S(1)}, bf16[128,1280]{1,0:T(8,128)(2,1)S(1)}, u32[]{:S(2)}, u32[]{:S(2)}) collective-permute-start(bf16[128,1280]{1,0:T(8,128)(2,1)S(1)} %collective-permute-done.47.refs_2_.refs_4_), channel_id=1, source_target_pairs={{0,8},{8,0},{16,24},{24,16},{1,9},{9,1},{17,25},{25,17},{2,10},{10... | collective-permute-start | bytes 983048 | tf_op jit(solution)/shard_map/ppermute | solution.py:278
  210.4 12.1 %collective-permute-start.51 = (bf16[208,256]{1,0:T(8,128)(2,1)}, bf16[208,256]{1,0:T(8,128)(2,1)S(1)}, u32[]{:S(2)}, u32[]{:S(2)}) collective-permute-start(bf16[208,256]{1,0:T(8,128)(2,1)} %qtotal.1.refs_4_), channel_id=1, source_target_pairs={{0,8},{8,0},{16,24},{24,16},{1,9},{9,1},{17,25},{25,17},{2,10},{10... | collective-permute-start | bytes 319496 | tf_op jit(solution)/shard_map/ppermute | solution.py:278
  (71 other events, 260.6 us)

commit v6 on v5

--- a/solution.py
+++ b/solution.py
@@ -451,7 +451,7 @@
 
 def add4_kernel(a, b, *outs):
     for kk in range(4):
-        outs[kk][...] = (a[kk].astype(F32) + b[kk].astype(F32)).astype(BF)
+        outs[kk][...] = a[kk] + b[kk]
 
 
 def latent_kernel(m0, r1, r2, r3, lat, mg1, cot, *rest):
@@ -652,8 +652,8 @@
     total = jnp.concatenate([both[0:8], both[8:16]], axis=1)
     for n, (out, size) in enumerate(zip(outs, (96, 160, 160))):
         width = out.shape[0]
-        at = lax.broadcasted_iota(jnp.int32, (160, width), 1)
-        pick = (at % size == lax.broadcasted_iota(jnp.int32, (160, width), 0)).astype(F32)
+        at = lax.broadcasted_iota(jnp.int32, (1, width), 1) % size
+        pick = (at == lax.broadcasted_iota(jnp.int32, (160, width), 0)).astype(F32)
         wide = lax.dot_general(
             total[:, 160 * n : 160 * (n + 1)],
             pick,
@@ -661,12 +661,12 @@
             precision=lax.Precision.HIGHEST,
             preferred_element_type=F32,
         )
-        mine = lax.broadcasted_iota(jnp.int32, (8, width), 0) == lax.broadcasted_iota(jnp.int32, (8, width), 1) // size
+        mine = lax.broadcasted_iota(jnp.int32, (8, width), 0) == lax.broadcasted_iota(jnp.int32, (1, width), 1) // size
         out[...] = jnp.sum(jnp.where(mine, wide, 0.0), axis=0)
 
 
 def plus(a, b):
-    return (a.astype(F32) + b.astype(F32)).astype(BF)
+    return a + b
 
 
 def finish_kernel(wq_full, lat, qg, init, *rest):
@@ -703,7 +703,7 @@
     n = len(refs) // 3
     for k in range(n):
         a, b, out = refs[2 * k], refs[2 * k + 1], refs[2 * n + k]
-        out[...] = (a[...].astype(F32) + b[...].astype(F32)).astype(out.dtype)
+        out[...] = plus(a[...], b[...])
 
 
 def sums_of_pairs(pairs, name, deps=(), cost=COST):

time: 228 us -> 228 us (level)
  no operation moved by 1% of the time
where the time goes in v6:
time: 228 us; the launch traced here: 227 us
  Pallas kernels  109 us (48%)
  starting transfers between devices  52.4 us (23%)
  waiting for transfers between devices  50.2 us (22%)
  local copies, waits for them, and re-layouts  13.8 us (6%)
    pallas_call x25, Pallas kernels, call(): pl.pallas_call(run, grid=grid, out_shape=out, in_specs=[ANY] * ahead + li...  109 us
    ppermute x34, waiting for transfers between devices, send(): return lax.ppermute(x, 'fsdp', [(i, i ^ k) for i in range(N)])  25.5 us
    ppermute x34, starting transfers between devices, send(): return lax.ppermute(x, 'fsdp', [(i, i ^ k) for i in range(N)])  19.5 us
    ppermute x11, starting transfers between devices, send_z(): return lax.ppermute(x, 'rep', [(i, i ^ k) for i in range(NZ)])  18.9 us
    ppermute x9, waiting for transfers between devices, send_split(): lax.ppermute(x, 'fsdp', [(i, i ^ (odd if i & 1 else even)) for i in range...  18.4 us
    ppermute x9, starting transfers between devices, send_split(): lax.ppermute(x, 'fsdp', [(i, i ^ (odd if i & 1 else even)) for i in range...  14 us
    unnamed x98, local copies, waits for them, and re-layouts  13.8 us
    ppermute x11, waiting for transfers between devices, send_z(): return lax.ppermute(x, 'rep', [(i, i ^ k) for i in range(NZ)])  6.28 us
  transfers between devices with their start and end apart: 54, of which 21 were waited for; matrix products, arithmetic and copies ran while one was open for 0% of the time, Pallas kernels for 41%

profile of v6, /device:TPU:0, one launch (start us, length us, event | category | flops | bytes accessed | tf_op | source)
XLA Modules:
  0.0 226.7 jit_solution(10690773465003087632)
XLA Ops:
  2.5 3.0 %collective-permute-start.1 = (bf16[896,256]{1,0:T(8,128)(2,1)}, bf16[896,256]{1,0:T(8,128)(2,1)}, u32[]{:S(2)}, u32[]{:S(2)}) collective-permute-start(bf16[896,256]{1,0:T(8,128)(2,1)} %pack.1.refs_3_.refs_2_.refs_1_), channel_id=1, source_target_pairs={{0,4},{1,3},{2,6},{3,1},{4,0},{5,7},{6,2},{7,5},{8,12},{9,11},{10,... | collective-permute-start | bytes 1376264 | tf_op jit(solution)/shard_map/ppermute | solution.py:274
  7.0 2.4 %pack_rows.1.refs_2_.refs_7_ = bf16[480,1280]{1,0:T(8,128)(2,1)} custom-call(bf16[160,1280]{1,0:T(8,128)(2,1)} %refs_0_.4, bf16[160,1280]{1,0:T(8,128)(2,1)} %refs_1_.11, bf16[160,1280]{1,0:T(8,128)(2,1)} %refs_2_.5, bf16[896,256]{1,0:T(8,128)(2,1)} %pack.1.refs_3_.refs_2_.refs_1_), custom_call_target="tpu_custom_call" | custom-call | flops 99999997952 | bytes 1024 | tf_op jit(solution)/shard_map/pack_rows/pallas_call | solution.py:302
  9.4 3.7 %norm.1.refs_0_ = bf16[1024,768]{1,0:T(8,128)(2,1)} custom-call(bf16[1024,768]{1,0:T(8,128)(2,1)} %bitcast.3, f32[768]{0:T(1024)} %refs_7_.1, bf16[480,1280]{1,0:T(8,128)(2,1)} %pack_rows.1.refs_2_.refs_7_), custom_call_target="tpu_custom_call" | custom-call | flops 99999997952 | bytes 1024 | tf_op jit(solution)/shard_map/norm/pallas_call | solution.py:302
  13.0 3.6 %collective-permute-done.1.refs_5_.refs_4_ = bf16[896,256]{1,0:T(8,128)(2,1)} collective-permute-done((bf16[896,256]{1,0:T(8,128)(2,1)}, bf16[896,256]{1,0:T(8,128)(2,1)}, u32[]{:S(2)}, u32[]{:S(2)}) %collective-permute-start.1) | collective-permute-done | bytes 458784 | tf_op jit(solution)/shard_map/ppermute | solution.py:274
  19.8 6.1 %collective-permute-done.2.refs_6_.refs_5_ = bf16[896,256]{1,0:T(8,128)(2,1)S(1)} collective-permute-done((bf16[896,256]{1,0:T(8,128)(2,1)}, bf16[896,256]{1,0:T(8,128)(2,1)S(1)}, u32[]{:S(2)}, u32[]{:S(2)}) %collective-permute-start.2) | collective-permute-done | bytes 458784 | tf_op jit(solution)/shard_map/ppermute | solution.py:274
  30.3 5.2 %query.1 = (bf16[1024,256]{1,0:T(8,128)(2,1)}, bf16[768,256]{1,0:T(8,128)(2,1)}, bf16[1280,256]{1,0:T(8,128)(2,1)}, bf16[256,256]{1,0:T(8,128)(2,1)}, bf16[256,1280]{1,0:T(8,128)(2,1)}) custom-call(bf16[1024,768]{1,0:T(8,128)(2,1)} %norm.1.refs_0_, f32[1280]{0:T(1024)} %refs_2_.7, bf16[896,256]{1,0:T(8,128)(2,1)} %pack.1.refs_3_.refs_2_.refs_1_, ...), custom_call_target="tpu_custom_call" | custom-call | flops 99999997952 | bytes 1024 | tf_op jit(solution)/shard_map/query/pallas_call | solution.py:302
  35.6 6.8 %scores.1 = (bf16[2,8,256,512]{3,2,1,0:T(8,128)(2,1)}, f32[2,256,128]{2,1,0:T(8,128)}) custom-call(s32[2]{0:T(128)} %refs_0_.5, bf16[1024,256]{1,0:T(8,128)(2,1)} %get-tuple-element.111.refs_1_.refs_0_, bf16[256,256]{1,0:T(8,128)(2,1)} %get-tuple-element.114.refs_2_), custom_call_target="tpu_custom_call" | custom-call | flops 99999997952 | bytes 1024 | tf_op jit(solution)/shard_map/scores/pallas_call | solution.py:302
  43.4 7.0 %values.1 = (bf16[1280,1024]{1,0:T(8,128)(2,1)}, bf16[768,1280]{1,0:T(8,128)(2,1)}) custom-call(bf16[1024,768]{1,0:T(8,128)(2,1)} %norm.1.refs_0_, bf16[896,256]{1,0:T(8,128)(2,1)} %pack.1.refs_3_.refs_2_.refs_1_, bf16[896,256]{1,0:T(8,128)(2,1)} %copy-done.28, bf16[896,256]{1,0:T(8,128)(2,1)} %collective-permute-done.refs_4_.refs_3_, ...), custom_call_target="tpu_custom_call" | custom-call | flops 99999997952 | bytes 1024 | tf_op jit(solution)/shard_map/values/pallas_call | solution.py:302
  50.4 4.4 %collective-permute-done.8.refs_9_ = bf16[480,1280]{1,0:T(8,128)(2,1)} collective-permute-done((bf16[480,1280]{1,0:T(8,128)(2,1)}, bf16[480,1280]{1,0:T(8,128)(2,1)}, u32[]{:S(2)}, u32[]{:S(2)}) %collective-permute-start.8) | collective-permute-done | bytes 1228832 | tf_op jit(solution)/shard_map/ppermute | solution.py:274
  58.2 4.4 %sums.2 = (bf16[4,64,1408]{2,1,0:T(8,128)(2,1)}, bf16[4,64,1408]{2,1,0:T(8,128)(2,1)}) custom-call(bf16[1280,1024]{1,0:T(8,128)(2,1)} %get-tuple-element.118.refs_0_.refs_1_, bf16[2,8,256,512]{3,2,1,0:T(8,128)(2,1)} %get-tuple-element.115.refs_9_.refs_1_.refs_3_, f32[2,256,128]{2,1,0:T(8,128)} %get-tuple-element.119.refs_2_), custom_call_target="tpu_custom_call" | custom-call | flops 99999997952 | bytes 1024 | tf_op jit(solution)/shard_map/sums/pallas_call | solution.py:302
  62.6 4.4 %sums.3 = (bf16[4,64,1408]{2,1,0:T(8,128)(2,1)}, bf16[4,64,1408]{2,1,0:T(8,128)(2,1)}) custom-call(bf16[1280,1024]{1,0:T(8,128)(2,1)} %get-tuple-element.118.refs_0_.refs_1_, bf16[2,8,256,512]{3,2,1,0:T(8,128)(2,1)} %get-tuple-element.115.refs_9_.refs_1_.refs_3_, ...), custom_call_target="tpu_custom_call", output_to_operand_aliasing={{0}: (3, {}), {1}: (4, {})} | custom-call | flops 99999997952 | bytes 1024 | tf_op jit(solution)/shard_map/sums/pallas_call | solution.py:302
  67.0 2.4 %collective-permute-done.10.refs_1_ = bf16[4,64,1408]{2,1,0:T(8,128)(2,1)S(1)} collective-permute-done((bf16[4,64,1408]{2,1,0:T(8,128)(2,1)}, bf16[4,64,1408]{2,1,0:T(8,128)(2,1)S(1)}, u32[]{:S(2)}, u32[]{:S(2)}) %collective-permute-start.10) | collective-permute-done | bytes 720928 | tf_op jit(solution)/shard_map/ppermute | solution.py:270
  76.5 4.1 %collective-permute-done.14.refs_1_ = bf16[64,1408]{1,0:T(8,128)(2,1)S(1)} collective-permute-done((bf16[64,1408]{1,0:T(8,128)(2,1)}, bf16[64,1408]{1,0:T(8,128)(2,1)S(1)}, u32[]{:S(2)}, u32[]{:S(2)}) %collective-permute-start.14) | collective-permute-done | bytes 180256 | tf_op jit(solution)/shard_map/ppermute | solution.py:270
  80.6 3.2 %collective-permute-done.15.refs_2_ = bf16[64,1408]{1,0:T(8,128)(2,1)S(1)} collective-permute-done((bf16[64,1408]{1,0:T(8,128)(2,1)}, bf16[64,1408]{1,0:T(8,128)(2,1)S(1)}, u32[]{:S(2)}, u32[]{:S(2)}) %collective-permute-start.15) | collective-permute-done | bytes 180256 | tf_op jit(solution)/shard_map/ppermute | solution.py:270
  86.3 11.4 %latent.1 = (bf16[64,1280]{1,0:T(8,128)(2,1)}, bf16[3,64,1280]{2,1,0:T(8,128)(2,1)}, bf16[4,3,64,160]{3,2,1,0:T(8,128)(2,1)}, bf16[4,3,64,160]{3,2,1,0:T(8,128)(...) custom-call(bf16[64,1408]{1,0:T(8,128)(2,1)} %get-tuple-element.127.refs_0_, bf16[64,1408]{1,0:T(8,128)(2,1)} %copy-done.44, ...), custom_call_target="tpu_custom_call" | custom-call | flops 99999997952 | bytes 1024 | tf_op jit(solution)/shard_map/latent/pallas_call | solution.py:302
  101.8 4.6 %collective-permute-done.21.refs_10_ = bf16[64,1408]{1,0:T(8,128)(2,1)S(1)} collective-permute-done((bf16[64,1408]{1,0:T(8,128)(2,1)}, bf16[64,1408]{1,0:T(8,128)(2,1)S(1)}, u32[]{:S(2)}, u32[]{:S(2)}) %collective-permute-start.21) | collective-permute-done | bytes 180256 | tf_op jit(solution)/shard_map/ppermute | solution.py:270
  106.4 2.5 %collective-permute-done.20.refs_8_ = bf16[64,1408]{1,0:T(8,128)(2,1)S(1)} collective-permute-done((bf16[64,1408]{1,0:T(8,128)(2,1)}, bf16[64,1408]{1,0:T(8,128)(2,1)S(1)}, u32[]{:S(2)}, u32[]{:S(2)}) %collective-permute-start.20) | collective-permute-done | bytes 180256 | tf_op jit(solution)/shard_map/ppermute | solution.py:270
  112.9 8.5 %backward.2 = (bf16[1536,1024]{1,0:T(8,128)(2,1)}, f32[256,256]{1,0:T(8,128)}, bf16[2,3,64,160]{3,2,1,0:T(8,128)(2,1)}, bf16[2,3,64,160]{3,2,1,0:T(8,128)(2,1)}, bf16[2,3,64,160]{3,2,1,0:T(8,128)(2,1)}) custom-call(bf16[1024,256]{1,0:T(8,128)(2,1)} %get-tuple-element.111.refs_1_.refs_0_, bf16[1280,1024]{1,0:T(8,128)(2,1)} %get-tuple-element.118.refs_0_.refs_1_, ...), custom_call_target="tpu_custom_call" | custom-call | flops 99999997952 | bytes 1024 | tf_op jit(solution)/shard_map/backward/pallas_call | solution.py:302
  121.4 2.5 %collective-permute-done.27.refs_6_ = bf16[3,64,1280]{2,1,0:T(8,128)(2,1)S(1)} collective-permute-done((bf16[3,64,1280]{2,1,0:T(8,128)(2,1)}, bf16[3,64,1280]{2,1,0:T(8,128)(2,1)S(1)}, u32[]{:S(2)}, u32[]{:S(2)}) %collective-permute-start.27) | collective-permute-done | bytes 491552 | tf_op jit(solution)/shard_map/ppermute | solution.py:274
  128.2 8.3 %backward.3 = (bf16[1536,1024]{1,0:T(8,128)(2,1)}, f32[256,256]{1,0:T(8,128)}) custom-call(bf16[1024,256]{1,0:T(8,128)(2,1)} %get-tuple-element.111.refs_1_.refs_0_, bf16[1280,1024]{1,0:T(8,128)(2,1)} %get-tuple-element.118.refs_0_.refs_1_, bf16[256,256]{1,0:T(8,128)(2,1)} %get-tuple-element.114.refs_2_, ...), custom_call_target="tpu_custom_call", output_to_operand_aliasing={{0}: (12, {})} | custom-call | flops 1024 | bytes 1024 | tf_op jit(solution)/shard_map/backward/pallas_call | solution.py:302
  137.1 7.2 %weights.1 = (bf16[4,768,256]{2,1,0:T(8,128)(2,1)}, bf16[4,768,256]{2,1,0:T(8,128)(2,1)}) custom-call(bf16[1024,768]{1,0:T(8,128)(2,1)} %norm.1.refs_0_, bf16[256,1280]{1,0:T(8,128)(2,1)} %get-tuple-element.158.refs_1_, bf16[1536,1024]{1,0:T(8,128)(2,1)} %get-tuple-element.146.refs_2_.refs_4_, f32[256,256]{1,0:T(8,128)} %get-tuple-element.145.refs_13_.refs_3_, ...), custom_call_target="tpu_custom_call" | custom-call | flops 99999997952 | bytes 1024 | tf_op jit(solution)/shard_map/weights/pallas_call | solution.py:302
  145.5 6.2 %latent_grads.1 = (bf16[128,1280]{1,0:T(8,128)(2,1)}, bf16[128,1280]{1,0:T(8,128)(2,1)}, bf16[128,1280]{1,0:T(8,128)(2,1)}, bf16[128,1280]{1,0:T(8,128)(2,1)}, f32[8,160]{1,0:T(8,128)}) custom-call(f32[32,1280]{1,0:T(8,128)} %get-tuple-element.147.refs_0_, bf16[160,1280]{1,0:T(8,128)(2,1)} %refs_1_.11, f32[1280]{0:T(1024)} %refs_2_.6, ...), custom_call_target="tpu_custom_call" | custom-call | flops 99999997952 | bytes 1024 | tf_op jit(solution)/shard_map/latent_grads/pallas_call | solution.py:302
  154.7 3.1 %add4g.1 = (bf16[768,256]{1,0:T(8,128)(2,1)}, bf16[768,256]{1,0:T(8,128)(2,1)}, bf16[768,256]{1,0:T(8,128)(2,1)}, bf16[768,256]{1,0:T(8,128)(2,1)}) custom-call(bf16[4,768,256]{2,1,0:T(8,128)(2,1)} %get-tuple-element.163.refs_0_, bf16[4,768,256]{2,1,0:T(8,128)(2,1)} %copy-done.18, bf16[128,1280]{1,0:T(8,128)(2,1)} %get-tuple-element.164.refs_2_.refs_1_), custom_call_target="tpu_custom_call" | custom-call | flops 99999997952 | bytes 1024 | tf_op jit(solution)/shard_map/add4g/pallas_call | solution.py:302
  166.4 2.6 %collective-permute-start.42 = (bf16[128,1280]{1,0:T(8,128)(2,1)}, bf16[128,1280]{1,0:T(8,128)(2,1)S(1)}, u32[]{:S(2)}, u32[]{:S(2)}) collective-permute-start(bf16[128,1280]{1,0:T(8,128)(2,1)} %osum.1.refs_5_), channel_id=1, source_target_pairs={{0,16},{8,24},{16,0},{24,8},{1,17},{9,25},{17,1},{25,9},{2,18},{10... | collective-permute-start | bytes 983048 | tf_op jit(solution)/shard_map/ppermute | solution.py:278
  169.0 7.6 %bytes.1.refs_10_ = f32[2,512,768]{2,1,0:T(8,128)} custom-call(bf16[1024,768]{1,0:T(8,128)(2,1)} %bitcast.4, f32[768]{0:T(1024)} %refs_7_.1, bf16[768,256]{1,0:T(8,128)(2,1)} %get-tuple-element.133.refs_2_, bf16[768,1280]{1,0:T(8,128)(2,1)} %get-tuple-element.134.refs_3_, bf16[1536,1024]{1,0:T(8,128)(2,1)} %get-tuple-element.146.refs_2_.refs_4_, ...), custom_call_target="tpu_custom_call" | custom-call | flops 1024 | bytes 1024 | tf_op jit(solution)/shard_map/bytes/pallas_call | solution.py:302
  179.6 2.8 %gsum.1 = (bf16[192,256]{1,0:T(8,128)(2,1)}, bf16[192,256]{1,0:T(8,128)(2,1)}, bf16[384,256]{1,0:T(8,128)(2,1)}, bf16[16,256]{1,0:T(8,128)(2,1)}) custom-call(bf16[768,256]{1,0:T(8,128)(2,1)} %get-tuple-element.165.refs_2_.refs_0_, bf16[768,256]{1,0:T(8,128)(2,1)} %copy-done.34, bf16[768,256]{1,0:T(8,128)(2,1)} %copy-done.35, bf16[768,256]{1,0:T(8,128)(2,1)} %copy-done.36, ...), custom_call_target="tpu_custom_call" | custom-call | flops 99999997952 | bytes 1024 | tf_op jit(solution)/shard_map/gsum/pallas_call | solution.py:302
  192.3 2.4 %collective-permute-start.49 = (bf16[192,256]{1,0:T(8,128)(2,1)}, bf16[192,256]{1,0:T(8,128)(2,1)S(1)}, u32[]{:S(2)}, u32[]{:S(2)}) collective-permute-start(bf16[192,256]{1,0:T(8,128)(2,1)} %get-tuple-element.184), channel_id=1, source_target_pairs={{0,16},{8,24},{16,0},{24,8},{1,17},{9,25},{17,1},{25,9},{2,18},{10... | collective-permute-start | bytes 294920 | tf_op jit(solution)/shard_map/ppermute | solution.py:278
  198.6 3.0 %collective-permute-done.46.refs_1_ = bf16[16,256]{1,0:T(8,128)(2,1)S(1)} collective-permute-done((bf16[16,256]{1,0:T(8,128)(2,1)}, bf16[16,256]{1,0:T(8,128)(2,1)S(1)}, u32[]{:S(2)}, u32[]{:S(2)}) %collective-permute-start.46) | collective-permute-done | bytes 8224 | tf_op jit(solution)/shard_map/ppermute | solution.py:270
  210.3 3.2 %collective-permute-start.51 = (bf16[208,256]{1,0:T(8,128)(2,1)}, bf16[208,256]{1,0:T(8,128)(2,1)S(1)}, u32[]{:S(2)}, u32[]{:S(2)}) collective-permute-start(bf16[208,256]{1,0:T(8,128)(2,1)} %qtotal.1.refs_4_), channel_id=1, source_target_pairs={{0,8},{8,0},{16,24},{24,16},{1,9},{9,1},{17,25},{25,17},{2,10},{10... | collective-permute-start | bytes 319496 | tf_op jit(solution)/shard_map/ppermute | solution.py:278
  213.5 3.4 %collective-permute-done.52.refs_6_ = bf16[208,256]{1,0:T(8,128)(2,1)S(1)} collective-permute-done((bf16[208,256]{1,0:T(8,128)(2,1)}, bf16[208,256]{1,0:T(8,128)(2,1)S(1)}, u32[]{:S(2)}, u32[]{:S(2)}) %collective-permute-start.52) | collective-permute-done | bytes 106528 | tf_op jit(solution)/shard_map/ppermute | solution.py:278
  219.5 2.9 %finish_latent.1 = (f32[160,1280]{1,0:T(8,128)}, f32[160,1280]{1,0:T(8,128)}, f32[160,1280]{1,0:T(8,128)}, f32[32,1280]{1,0:T(8,128)}) custom-call(bf16[128,1280]{1,0:T(8,128)(2,1)} %ototal.1.refs_3_.refs_0_, bf16[128,1280]{1,0:T(8,128)(2,1)} %copy-done.3, bf16[128,1280]{1,0:T(8,128)(2,1)} %copy-done.2, bf16[128,1280]{1,0:T(8,128)(2,1)} %copy-done.4), custom_call_target="tpu_custom_call" | custom-call | flops 1024 | bytes 1024 | tf_op jit(solution)/shard_map/finish_latent/pallas_call | solution.py:302
  223.1 3.5 %finish.1 = (f32[96,256]{1,0:T(8,128)}, f32[96,1280]{1,0:T(8,128)}, f32[160,256]{1,0:T(8,128)}, f32[32,1280]{1,0:T(8,128)}, f32[768]{0:T(1024)}, /*index=5*/f32[1280]{0:T(1024)}, f32[1280]{0:T(1024)}) custom-call(bf16[1280,256]{1,0:T(8,128)(2,1)} %get-tuple-element.168.refs_0_, bf16[32,1280]{1,0:T(8,128)(2,1)} %refs_1_.13, f32[1280]{0:T(1024)} %refs_2_.7, ...), custom_call_target="tpu_custom_call" | custom-call | flops 1024 | bytes 1024 | tf_op jit(solution)/shard_map/finish/pallas_call | solution.py:302
  (199 shorter events, 79.2 us)
Async XLA Ops:
  2.5 14.1 %collective-permute-start.1 = (bf16[896,256]{1,0:T(8,128)(2,1)}, bf16[896,256]{1,0:T(8,128)(2,1)}, u32[]{:S(2)}, u32[]{:S(2)}) collective-permute-start(bf16[896,256]{1,0:T(8,128)(2,1)} %pack.1.refs_3_.refs_2_.refs_1_), channel_id=1, source_target_pairs={{0,4},{1,3},{2,6},{3,1},{4,0},{5,7},{6,2},{7,5},{8,12},{9,11},{10,... | collective-permute-start | bytes 1376264 | tf_op jit(solution)/shard_map/ppermute | solution.py:274
  5.5 11.2 %collective-permute-start = (bf16[896,256]{1,0:T(8,128)(2,1)}, bf16[896,256]{1,0:T(8,128)(2,1)}, u32[]{:S(2)}, u32[]{:S(2)}) collective-permute-start(bf16[896,256]{1,0:T(8,128)(2,1)} %pack.1.refs_3_.refs_2_.refs_1_), channel_id=1, source_target_pairs={{0,2},{1,5},{2,0},{3,7},{4,6},{5,1},{6,4},{7,3},{8,10},{9,13},{10,... | collective-permute-start | bytes 1376264 | tf_op jit(solution)/shard_map/ppermute | solution.py:274
  19.2 9.4 %collective-permute-start.4 = (bf16[896,256]{1,0:T(8,128)(2,1)}, bf16[896,256]{1,0:T(8,128)(2,1)S(1)}, u32[]{:S(2)}, u32[]{:S(2)}) collective-permute-start(bf16[896,256]{1,0:T(8,128)(2,1)} %collective-permute-done.refs_4_.refs_3_), channel_id=1, source_target_pairs={{0,1},{1,0},{2,3},{3,2},{4,5},{5,4},{6,7},{7,6},{8,9},{9,8},{10,11... | collective-permute-start | bytes 1376264 | tf_op jit(solution)/shard_map/ppermute | solution.py:270
  19.2 9.3 %collective-permute-start.5 = (bf16[896,256]{1,0:T(8,128)(2,1)}, bf16[896,256]{1,0:T(8,128)(2,1)S(1)}, u32[]{:S(2)}, u32[]{:S(2)}) collective-permute-start(bf16[896,256]{1,0:T(8,128)(2,1)} %collective-permute-done.1.refs_5_.refs_4_), channel_id=1, source_target_pairs={{0,1},{1,0},{2,3},{3,2},{4,5},{5,4},{6,7},{7,6},{8,9},{9,8},{10,11... | collective-permute-start | bytes 1376264 | tf_op jit(solution)/shard_map/ppermute | solution.py:270
  25.9 28.9 %collective-permute-start.8 = (bf16[480,1280]{1,0:T(8,128)(2,1)}, bf16[480,1280]{1,0:T(8,128)(2,1)}, u32[]{:S(2)}, u32[]{:S(2)}) collective-permute-start(bf16[480,1280]{1,0:T(8,128)(2,1)} %pack_rows.1.refs_2_.refs_7_), channel_id=1, source_target_pairs={{0,2},{1,5},{2,0},{3,7},{4,6},{5,1},{6,4},{7,3},{8,10},{9,13},{10,... | collective-permute-start | bytes 3686408 | tf_op jit(solution)/shard_map/ppermute | solution.py:274
  26.9 29.1 %collective-permute-start.9 = (bf16[480,1280]{1,0:T(8,128)(2,1)}, bf16[480,1280]{1,0:T(8,128)(2,1)}, u32[]{:S(2)}, u32[]{:S(2)}) collective-permute-start(bf16[480,1280]{1,0:T(8,128)(2,1)} %pack_rows.1.refs_2_.refs_7_), channel_id=1, source_target_pairs={{0,4},{1,3},{2,6},{3,1},{4,0},{5,7},{6,2},{7,5},{8,12},{9,11},{10,... | collective-permute-start | bytes 3686408 | tf_op jit(solution)/shard_map/ppermute | solution.py:274
  55.9 17.0 %collective-permute-start.13 = (bf16[480,1280]{1,0:T(8,128)(2,1)}, bf16[480,1280]{1,0:T(8,128)(2,1)}, u32[]{:S(2)}, u32[]{:S(2)}) collective-permute-start(bf16[480,1280]{1,0:T(8,128)(2,1)} %collective-permute-done.8.refs_9_), channel_id=1, source_target_pairs={{0,4},{1,3},{2,6},{3,1},{4,0},{5,7},{6,2},{7,5},{8,12},{9,11},{10,... | collective-permute-start | bytes 3686408 | tf_op jit(solution)/shard_map/ppermute | solution.py:274
  57.7 11.7 %collective-permute-start.11 = (bf16[480,1280]{1,0:T(8,128)(2,1)}, bf16[480,1280]{1,0:T(8,128)(2,1)}, u32[]{:S(2)}, u32[]{:S(2)}) collective-permute-start(bf16[480,1280]{1,0:T(8,128)(2,1)} %collective-permute-done.8.refs_9_), channel_id=1, source_target_pairs={{0,1},{1,0},{2,3},{3,2},{4,5},{5,4},{6,7},{7,6},{8,9},{9,8},{10,11... | collective-permute-start | bytes 3686408 | tf_op jit(solution)/shard_map/ppermute | solution.py:270
  57.7 11.7 %collective-permute-start.12 = (bf16[480,1280]{1,0:T(8,128)(2,1)}, bf16[480,1280]{1,0:T(8,128)(2,1)}, u32[]{:S(2)}, u32[]{:S(2)}) collective-permute-start(bf16[480,1280]{1,0:T(8,128)(2,1)} %collective-permute-done.9.refs_10_), channel_id=1, source_target_pairs={{0,1},{1,0},{2,3},{3,2},{4,5},{5,4},{6,7},{7,6},{8,9},{9,8},{10,11... | collective-permute-start | bytes 3686408 | tf_op jit(solution)/shard_map/ppermute | solution.py:270
  73.0 12.2 %collective-permute-start.17 = (bf16[480,1280]{1,0:T(8,128)(2,1)}, bf16[480,1280]{1,0:T(8,128)(2,1)S(1)}, u32[]{:S(2)}, u32[]{:S(2)}) collective-permute-start(bf16[480,1280]{1,0:T(8,128)(2,1)} %collective-permute-done.13.refs_11_), channel_id=1, source_target_pairs={{0,1},{1,0},{2,3},{3,2},{4,5},{5,4},{6,7},{7,6},{8,9},{9,8},{10,11... | collective-permute-start | bytes 3686408 | tf_op jit(solution)/shard_map/ppermute | solution.py:270
  73.7 10.2 %collective-permute-start.15 = (bf16[64,1408]{1,0:T(8,128)(2,1)}, bf16[64,1408]{1,0:T(8,128)(2,1)S(1)}, u32[]{:S(2)}, u32[]{:S(2)}) collective-permute-start(bf16[64,1408]{1,0:T(8,128)(2,1)} %get-tuple-element.129), channel_id=1, source_target_pairs={{0,4},{1,5},{2,6},{3,7},{4,0},{5,1},{6,2},{7,3},{8,12},{9,13},{10,... | collective-permute-start | bytes 540680 | tf_op jit(solution)/shard_map/ppermute | solution.py:270
  75.4 9.8 %collective-permute-start.16 = (bf16[64,1408]{1,0:T(8,128)(2,1)}, bf16[64,1408]{1,0:T(8,128)(2,1)S(1)}, u32[]{:S(2)}, u32[]{:S(2)}) collective-permute-start(bf16[64,1408]{1,0:T(8,128)(2,1)} %get-tuple-element.130), channel_id=1, source_target_pairs={{0,6},{1,7},{2,4},{3,5},{4,2},{5,3},{6,0},{7,1},{8,14},{9,15},{10,... | collective-permute-start | bytes 540680 | tf_op jit(solution)/shard_map/ppermute | solution.py:270
  99.6 9.3 %collective-permute-start.20 = (bf16[64,1408]{1,0:T(8,128)(2,1)}, bf16[64,1408]{1,0:T(8,128)(2,1)S(1)}, u32[]{:S(2)}, u32[]{:S(2)}) collective-permute-start(bf16[64,1408]{1,0:T(8,128)(2,1)} %get-tuple-element.135.refs_4_), channel_id=1, source_target_pairs={{0,4},{1,5},{2,6},{3,7},{4,0},{5,1},{6,2},{7,3},{8,12},{9,13},{10,... | collective-permute-start | bytes 540680 | tf_op jit(solution)/shard_map/ppermute | solution.py:270
  109.6 11.8 %collective-permute-start.28 = (bf16[3,64,1280]{2,1,0:T(8,128)(2,1)}, bf16[3,64,1280]{2,1,0:T(8,128)(2,1)S(1)}, u32[]{:S(2)}, u32[]{:S(2)}) collective-permute-start(bf16[3,64,1280]{2,1,0:T(8,128)(2,1)} %get-tuple-element.144.refs_3_), channel_id=1, source_target_pairs={{0,1},{1,0},{2,3},{3,2},{4,5},{5,4},{6,7},{7,6},{8,9},{9,8},{10,11... | collective-permute-start | bytes 1474568 | tf_op jit(solution)/shard_map/ppermute | solution.py:270
  110.0 13.9 %collective-permute-start.27 = (bf16[3,64,1280]{2,1,0:T(8,128)(2,1)}, bf16[3,64,1280]{2,1,0:T(8,128)(2,1)S(1)}, u32[]{:S(2)}, u32[]{:S(2)}) collective-permute-start(bf16[3,64,1280]{2,1,0:T(8,128)(2,1)} %get-tuple-element.144.refs_3_), channel_id=1, source_target_pairs={{0,4},{1,3},{2,6},{3,1},{4,0},{5,7},{6,2},{7,5},{8,12},{9,11},{10,... | collective-permute-start | bytes 1474568 | tf_op jit(solution)/shard_map/ppermute | solution.py:274
  110.6 13.3 %collective-permute-start.26 = (bf16[3,64,1280]{2,1,0:T(8,128)(2,1)}, bf16[3,64,1280]{2,1,0:T(8,128)(2,1)S(1)}, u32[]{:S(2)}, u32[]{:S(2)}) collective-permute-start(bf16[3,64,1280]{2,1,0:T(8,128)(2,1)} %get-tuple-element.144.refs_3_), channel_id=1, source_target_pairs={{0,2},{1,5},{2,0},{3,7},{4,6},{5,1},{6,4},{7,3},{8,10},{9,13},{10,... | collective-permute-start | bytes 1474568 | tf_op jit(solution)/shard_map/ppermute | solution.py:274
  123.9 12.6 %collective-permute-start.30 = (bf16[3,64,1280]{2,1,0:T(8,128)(2,1)S(1)}, bf16[3,64,1280]{2,1,0:T(8,128)(2,1)S(1)}, u32[]{:S(2)}, u32[]{:S(2)}) collective-permute-start(bf16[3,64,1280]{2,1,0:T(8,128)(2,1)S(1)} %collective-permute-done.26.refs_5_), channel_id=1, source_target_pairs={{0,1},{1,0},{2,3},{3,2},{4,5},{5,4},{6,7},{7,6},{8,9},{9,8},{10,11... | collective-permute-start | bytes 1474568 | tf_op jit(solution)/shard_map/ppermute | solution.py:270
  124.0 12.6 %collective-permute-start.29 = (bf16[3,64,1280]{2,1,0:T(8,128)(2,1)S(1)}, bf16[3,64,1280]{2,1,0:T(8,128)(2,1)}, u32[]{:S(2)}, u32[]{:S(2)}) collective-permute-start(bf16[3,64,1280]{2,1,0:T(8,128)(2,1)S(1)} %collective-permute-done.26.refs_5_), channel_id=1, source_target_pairs={{0,4},{1,3},{2,6},{3,1},{4,0},{5,7},{6,2},{7,5},{8,12},{9,11},{10,... | collective-permute-start | bytes 1474568 | tf_op jit(solution)/shard_map/ppermute | solution.py:274
  124.7 19.6 %collective-permute-start.33 = (bf16[2,3,64,160]{3,2,1,0:T(8,128)(2,1)}, bf16[2,3,64,160]{3,2,1,0:T(8,128)(2,1)S(1)}, u32[]{:S(2)}, u32[]{:S(2)}) collective-permute-start(bf16[2,3,64,160]{3,2,1,0:T(8,128)(2,1)} %get-tuple-element.155), channel_id=1, source_target_pairs={{0,2},{1,3},{2,0},{3,1},{4,6},{5,7},{6,4},{7,5},{8,10},{9,11},{10,... | collective-permute-start | bytes 368648 | tf_op jit(solution)/shard_map/ppermute | solution.py:270
  126.1 18.3 %collective-permute-start.34 = (bf16[2,3,64,160]{3,2,1,0:T(8,128)(2,1)}, bf16[2,3,64,160]{3,2,1,0:T(8,128)(2,1)S(1)}, u32[]{:S(2)}, u32[]{:S(2)}) collective-permute-start(bf16[2,3,64,160]{3,2,1,0:T(8,128)(2,1)} %get-tuple-element.156), channel_id=1, source_target_pairs={{0,4},{1,5},{2,6},{3,7},{4,0},{5,1},{6,2},{7,3},{8,12},{9,13},{10,... | collective-permute-start | bytes 368648 | tf_op jit(solution)/shard_map/ppermute | solution.py:270
  126.9 17.6 %collective-permute-start.35 = (bf16[2,3,64,160]{3,2,1,0:T(8,128)(2,1)}, bf16[2,3,64,160]{3,2,1,0:T(8,128)(2,1)}, u32[]{:S(2)}, u32[]{:S(2)}) collective-permute-start(bf16[2,3,64,160]{3,2,1,0:T(8,128)(2,1)} %get-tuple-element.157), channel_id=1, source_target_pairs={{0,6},{1,7},{2,4},{3,5},{4,2},{5,3},{6,0},{7,1},{8,14},{9,15},{10,... | collective-permute-start | bytes 368648 | tf_op jit(solution)/shard_map/ppermute | solution.py:270
  151.7 10.4 %collective-permute-start.36 = (bf16[128,1280]{1,0:T(8,128)(2,1)}, bf16[128,1280]{1,0:T(8,128)(2,1)S(1)}, u32[]{:S(2)}, u32[]{:S(2)}) collective-permute-start(bf16[128,1280]{1,0:T(8,128)(2,1)} %get-tuple-element.162), channel_id=1, source_target_pairs={{0,8},{8,0},{16,24},{24,16},{1,9},{9,1},{17,25},{25,17},{2,10},{10... | collective-permute-start | bytes 983048 | tf_op jit(solution)/shard_map/ppermute | solution.py:278
  157.8 18.9 %collective-permute-start.38 = (bf16[768,256]{1,0:T(8,128)(2,1)}, bf16[768,256]{1,0:T(8,128)(2,1)S(1)}, u32[]{:S(2)}, u32[]{:S(2)}) collective-permute-start(bf16[768,256]{1,0:T(8,128)(2,1)} %get-tuple-element.169), channel_id=1, source_target_pairs={{0,2},{1,3},{2,0},{3,1},{4,6},{5,7},{6,4},{7,5},{8,10},{9,11},{10,... | collective-permute-start | bytes 1179656 | tf_op jit(solution)/shard_map/ppermute | solution.py:270
  159.2 19.5 %collective-permute-start.39 = (bf16[768,256]{1,0:T(8,128)(2,1)}, bf16[768,256]{1,0:T(8,128)(2,1)S(1)}, u32[]{:S(2)}, u32[]{:S(2)}) collective-permute-start(bf16[768,256]{1,0:T(8,128)(2,1)} %get-tuple-element.170), channel_id=1, source_target_pairs={{0,4},{1,5},{2,6},{3,7},{4,0},{5,1},{6,2},{7,3},{8,12},{9,13},{10,... | collective-permute-start | bytes 1179656 | tf_op jit(solution)/shard_map/ppermute | solution.py:270
  160.0 18.7 %collective-permute-start.40 = (bf16[768,256]{1,0:T(8,128)(2,1)}, bf16[768,256]{1,0:T(8,128)(2,1)S(1)}, u32[]{:S(2)}, u32[]{:S(2)}) collective-permute-start(bf16[768,256]{1,0:T(8,128)(2,1)} %get-tuple-element.171), channel_id=1, source_target_pairs={{0,6},{1,7},{2,4},{3,5},{4,2},{5,3},{6,0},{7,1},{8,14},{9,15},{10,... | collective-permute-start | bytes 1179656 | tf_op jit(solution)/shard_map/ppermute | solution.py:270
  164.7 18.0 %collective-permute-start.41 = (bf16[128,1280]{1,0:T(8,128)(2,1)S(1)}, bf16[128,1280]{1,0:T(8,128)(2,1)S(1)}, u32[]{:S(2)}, u32[]{:S(2)}) collective-permute-start(bf16[128,1280]{1,0:T(8,128)(2,1)S(1)} %copy-done.37), channel_id=1, source_target_pairs={{0,8},{8,0},{16,24},{24,16},{1,9},{9,1},{17,25},{25,17},{2,10},{10... | collective-permute-start | bytes 983048 | tf_op jit(solution)/shard_map/ppermute | solution.py:278
  166.4 17.1 %collective-permute-start.42 = (bf16[128,1280]{1,0:T(8,128)(2,1)}, bf16[128,1280]{1,0:T(8,128)(2,1)S(1)}, u32[]{:S(2)}, u32[]{:S(2)}) collective-permute-start(bf16[128,1280]{1,0:T(8,128)(2,1)} %osum.1.refs_5_), channel_id=1, source_target_pairs={{0,16},{8,24},{16,0},{24,8},{1,17},{9,25},{17,1},{25,9},{2,18},{10... | collective-permute-start | bytes 983048 | tf_op jit(solution)/shard_map/ppermute | solution.py:278
  186.3 17.3 %collective-permute-start.47 = (bf16[128,1280]{1,0:T(8,128)(2,1)}, bf16[128,1280]{1,0:T(8,128)(2,1)S(1)}, u32[]{:S(2)}, u32[]{:S(2)}) collective-permute-start(bf16[128,1280]{1,0:T(8,128)(2,1)} %ototal.1.refs_3_.refs_0_), channel_id=1, source_target_pairs={{0,16},{8,24},{16,0},{24,8},{1,17},{9,25},{17,1},{25,9},{2,18},{10... | collective-permute-start | bytes 983048 | tf_op jit(solution)/shard_map/ppermute | solution.py:278
  192.0 15.4 %collective-permute-start.44 = (bf16[128,1280]{1,0:T(8,128)(2,1)S(1)}, bf16[128,1280]{1,0:T(8,128)(2,1)S(1)}, u32[]{:S(2)}, u32[]{:S(2)}) collective-permute-start(bf16[128,1280]{1,0:T(8,128)(2,1)S(1)} %copy-done.1), channel_id=1, source_target_pairs={{0,8},{8,0},{16,24},{24,16},{1,9},{9,1},{17,25},{25,17},{2,10},{10... | collective-permute-start | bytes 983048 | tf_op jit(solution)/shard_map/ppermute | solution.py:278
  192.3 14.1 %collective-permute-start.49 = (bf16[192,256]{1,0:T(8,128)(2,1)}, bf16[192,256]{1,0:T(8,128)(2,1)S(1)}, u32[]{:S(2)}, u32[]{:S(2)}) collective-permute-start(bf16[192,256]{1,0:T(8,128)(2,1)} %get-tuple-element.184), channel_id=1, source_target_pairs={{0,16},{8,24},{16,0},{24,8},{1,17},{9,25},{17,1},{25,9},{2,18},{10... | collective-permute-start | bytes 294920 | tf_op jit(solution)/shard_map/ppermute | solution.py:278
  204.5 14.4 %collective-permute-start.48 = (bf16[128,1280]{1,0:T(8,128)(2,1)S(1)}, bf16[128,1280]{1,0:T(8,128)(2,1)S(1)}, u32[]{:S(2)}, u32[]{:S(2)}) collective-permute-start(bf16[128,1280]{1,0:T(8,128)(2,1)S(1)} %collective-permute-done.47.refs_2_.refs_4_), channel_id=1, source_target_pairs={{0,8},{8,0},{16,24},{24,16},{1,9},{9,1},{17,25},{25,17},{2,10},{10... | collective-permute-start | bytes 983048 | tf_op jit(solution)/shard_map/ppermute | solution.py:278
  210.3 12.1 %collective-permute-start.51 = (bf16[208,256]{1,0:T(8,128)(2,1)}, bf16[208,256]{1,0:T(8,128)(2,1)S(1)}, u32[]{:S(2)}, u32[]{:S(2)}) collective-permute-start(bf16[208,256]{1,0:T(8,128)(2,1)} %qtotal.1.refs_4_), channel_id=1, source_target_pairs={{0,8},{8,0},{16,24},{24,16},{1,9},{9,1},{17,25},{25,17},{2,10},{10... | collective-permute-start | bytes 319496 | tf_op jit(solution)/shard_map/ppermute | solution.py:278
  (71 other events, 260.6 us)
